TPU v7x, 128 devices: a whole 4x4x4 slice. The times are simulated.
128 devices in a mesh: blk: 8 (over y, core), grp: 16 (over x, z).
Axes of the slice: x: 4, y: 4, z: 4, core: 2. Of those that a mesh axis runs over, the one named last changes fastest.
Arguments:
- gas_state: bfloat16 [16, 32, 131072], P(None, None, ('grp', 'blk')), may hold values from -6 to 6
- cos_zenith: bfloat16 [131072], P(('grp', 'blk')), may hold values from 0.049804688 to 1
- daylit: int32 [131072], P(('grp', 'blk')), may hold values from 0 to 1
- fine_area: float32 [524288], P(('grp', 'blk')), may hold values from 0.25 to 4
- fine_albedo: float32 [2, 524288], P(None, ('grp', 'blk')), may hold values from 0.05 to 0.85
- parent_of: int32 [524288], P(('grp', 'blk')), may hold values from 0 to 8191, as said below
- optics_weight: bfloat16 [64, 16], replicated, may hold values from -1.5 to 1.5
- solar_weight: float32 [32], replicated, may hold values from 0.01 to 0.1
- neighbours: int32 [3, 131072], P(None, ('grp', 'blk')), may hold values from 0 to 131071, as said below
- side_weight: float32 [3, 131072], P(None, ('grp', 'blk')), may hold values from 0.05 to 0.3
Outputs:
- fluxes: float32 [2, 33, 131072], P(None, None, ('grp', 'blk'))
Inputs may be any that keep to these rules, and one draw needn't show every extreme that they name: `parent_of`: the fine cells of one index of grp have their parents among that index's columns, numbered from 0 within it; each column has exactly 4 fine cells, and the 128 fine cells of an aligned block share 128 // 4 consecutive columns. `neighbours`: every neighbour lies within 128 columns of its column and among the columns of the same index of grp; a neighbour may be the column itself.
All inputs are finite; a program needn't handle non-finite values.
Results may differ from a plain program's by a relative error of at most 0.0003.
Values may be sent and summed in bfloat16 or wider, within the bound.
No kernel may reach another device: no remote copies, remote signals or barrier semaphores. Data moves between devices by JAX's collectives and lax.ppermute only.
A program may use at most 64 MiB of HBM per device.

v0:
```python
import jax
import jax.numpy as jnp
from jax import lax
from jax.experimental import pallas as pl
from jax.experimental.pallas import tpu as pltpu
from jax.sharding import PartitionSpec as P

F = 16
LEV = 32
CB = 128
G = 32
KIDS = 4
NB = 8
NBLK = 8
ROWS = 72
STEP = 8
FINE_BLOCKS = NB * KIDS
COLS = NB * CB

ASYM = 0.8
TAU_SCALE = 0.08
SSA_MAX = 0.98
LOG2E = 1.4426950408889634

SLOPE = 0.5 * (1.25 + 0.75 * ASYM)
UNIT = 0.5 * SLOPE * SSA_MAX
SHIFT = 1.0 / UNIT - 1.0
BETA = 0.375 * (1.0 - ASYM) / SLOPE
RATE = -2.0 * TAU_SCALE * UNIT
SCATTER = UNIT / (0.375 * (1.0 - ASYM))

F32 = jnp.float32
BF16 = jnp.bfloat16
IN_VMEM = pl.BlockSpec(memory_space=pltpu.VMEM)
IN_HBM = pl.BlockSpec(memory_space=pltpu.HBM)
UNREAD = pl.BlockSpec(memory_space=pl.ANY)


def params(mebibytes):
    return pltpu.CompilerParams(vmem_limit_bytes=mebibytes << 20)


def shape(dims, kind=F32):
    return jax.ShapeDtypeStruct(dims, kind)


def sum_tiles(x):
    return (x[0:8] + x[8:16]) + (x[16:24] + x[24:32])


def block_lanes(block):
    return pl.ds(pl.multiple_of(block * CB, CB), CB)


def place_albedo(parent_ref, area_ref, albedo_ref, part_ref, mine):
    sub = lax.broadcasted_iota(jnp.int32, (CB, CB), 0)
    for j in range(FINE_BLOCKS):
        parent = parent_ref[j : j + 1, :]
        hot = jnp.where((parent & (CB - 1)) == sub, 1.0, 0.0).astype(BF16)
        area = area_ref[j : j + 1, :]
        terms = jnp.concatenate(
            [area, area * albedo_ref[j, 0:1, :], area * albedo_ref[j, 1:2, :]], axis=0
        )
        first = terms.astype(BF16)
        rest = terms - first.astype(F32)
        second = rest.astype(BF16)
        third = (rest - second.astype(F32)).astype(BF16)
        dims = (((1,), (1,)), ((), ()))
        total = lax.dot_general(first, hot, dims, preferred_element_type=F32)
        total = total + (
            lax.dot_general(second, hot, dims, preferred_element_type=F32)
            + lax.dot_general(third, hot, dims, preferred_element_type=F32)
        )
        for row in range(3):
            part_ref[row, j : j + 1, :] = total[row : row + 1, :]
    area = part_ref[0]
    here = area > 0.0
    safe = jnp.where(here, area, 1.0)
    owner = (parent_ref[:, 0:1] >> 7) ^ (mine * NB)
    slot = lax.broadcasted_iota(jnp.int32, (FINE_BLOCKS, NBLK * NB), 1)
    where_to = jnp.where(owner == slot, 1.0, 0.0).astype(BF16)
    placed = []
    for s in range(2):
        albedo = jnp.where(here, part_ref[1 + s] / safe, 0.0).astype(BF16)
        placed.append(
            lax.dot_general(
                where_to, albedo, (((0,), (0,)), ((), ())), preferred_element_type=F32
            ).astype(BF16)
        )
    return placed


def spread_weights(weight_ref, wide_ref):
    row = lax.broadcasted_iota(jnp.int32, (F, F * STEP), 0)
    col = lax.broadcasted_iota(jnp.int32, (F, F * STEP), 1)
    spread = jnp.where(col // STEP == row, 1.0, 0.0).astype(BF16)
    depth = lax.broadcasted_iota(jnp.int32, (F, 2 * G), 1) < G
    scaled = weight_ref[...].astype(F32) * jnp.where(depth, LOG2E, 0.5)
    high = scaled.astype(BF16)
    low = (scaled - high.astype(F32)).astype(BF16)
    wide = jnp.concatenate(
        [
            lax.dot_general(x, spread, (((0,), (0,)), ((), ())), preferred_element_type=F32)
            for x in (high, low)
        ],
        axis=1,
    )
    level = lax.broadcasted_iota(jnp.int32, (2 * G, 2 * F * STEP), 1) % STEP
    for l in range(STEP):
        wide_ref[l * 2 * G : (l + 1) * 2 * G, :] = jnp.where(level == l, wide, 0.0).astype(BF16)


def column_constants(cosine, lit, column_ref):
    back = 0.5 * (1.0 - ASYM * cosine)
    column_ref[0] = -TAU_SCALE / cosine
    column_ref[1] = back * SCATTER
    column_ref[2] = (1.0 - back) * SCATTER
    column_ref[3] = cosine
    column_ref[4] = lit


def surface_kernel(
    parent_hbm,
    area_hbm,
    albedo_hbm,
    weight_hbm,
    cosine_hbm,
    lit_hbm,
    solar_hbm,
    neighbour_hbm,
    side_hbm,
    gas_hbm,
    send_ref,
    keep_ref,
    gas_ref,
    wide_ref,
    column_ref,
    solar_ref,
    neighbour_ref,
    side_ref,
    parent_ref,
    area_ref,
    albedo_ref,
    weight_ref,
    cosine_ref,
    lit_ref,
    sun_ref,
    part_ref,
    sems,
):
    pairs = (
        (parent_hbm, parent_ref),
        (area_hbm, area_ref),
        (albedo_hbm, albedo_ref),
        (weight_hbm, weight_ref),
        (cosine_hbm, cosine_ref),
        (lit_hbm, lit_ref),
        (solar_hbm, sun_ref),
        (neighbour_hbm, neighbour_ref),
        (side_hbm, side_ref),
        (gas_hbm, gas_ref),
    )
    copies = [
        pltpu.make_async_copy(source, target, sems.at[i])
        for i, (source, target) in enumerate(pairs)
    ]
    for copy in copies:
        copy.start()
    for copy in copies[:7]:
        copy.wait()
    mine = lax.axis_index("blk")
    placed = place_albedo(parent_ref, area_ref, albedo_ref, part_ref, mine)
    for s in range(2):
        for i in range(NBLK // 2):
            keep_ref[i, s] = placed[s][2 * i * NB : (2 * i + 1) * NB]
            send_ref[i, s] = placed[s][(2 * i + 1) * NB : (2 * i + 2) * NB]
    spread_weights(weight_ref, wide_ref)
    column_constants(cosine_ref[...].astype(F32), lit_ref[...].astype(F32), column_ref)
    row = lax.broadcasted_iota(jnp.int32, (G, G), 0)
    col = lax.broadcasted_iota(jnp.int32, (G, G), 1)
    sun = jnp.sum(jnp.where(row == col, sun_ref[...], 0.0), axis=1, keepdims=True)
    solar_ref[...] = jnp.broadcast_to(sun, (G, CB))
    for copy in copies[7:]:
        copy.wait()


def surface(
    parent_of,
    fine_area,
    fine_albedo,
    optics_weight,
    cos_zenith,
    daylit,
    solar_weight,
    neighbours,
    side_weight,
    gas_state,
):
    return pl.pallas_call(
        surface_kernel,
        in_specs=[IN_HBM] * 10,
        out_specs=[IN_VMEM] * 8,
        out_shape=[
            shape((NBLK // 2, 2, NB, CB), BF16),
            shape((NBLK // 2, 2, NB, CB), BF16),
            shape((F, LEV, COLS), BF16),
            shape((2 * G * STEP, 2 * F * STEP), BF16),
            shape((5, NB, CB)),
            shape((G, CB)),
            shape((3, COLS), jnp.int32),
            shape((3, COLS)),
        ],
        scratch_shapes=[
            pltpu.VMEM((FINE_BLOCKS, CB), jnp.int32),
            pltpu.VMEM((FINE_BLOCKS, CB), F32),
            pltpu.VMEM((FINE_BLOCKS, 2, CB), F32),
            pltpu.VMEM((F, 2 * G), BF16),
            pltpu.VMEM((NB, CB), BF16),
            pltpu.VMEM((NB, CB), jnp.int32),
            pltpu.VMEM((1, G), F32),
            pltpu.VMEM((3, FINE_BLOCKS, CB), F32),
            pltpu.SemaphoreType.DMA((10,)),
        ],
        compiler_params=params(4),
        name="surface",
    )(
        *[
            pltpu.with_memory_space_constraint(x, pltpu.HBM)
            for x in (
                parent_of.reshape(FINE_BLOCKS, CB),
                fine_area.reshape(FINE_BLOCKS, CB),
                fine_albedo.reshape(2, FINE_BLOCKS, CB).transpose(1, 0, 2),
                optics_weight.T,
                cos_zenith.reshape(NB, CB),
                daylit.reshape(NB, CB),
                solar_weight.reshape(1, G),
                neighbours,
                side_weight,
                gas_state,
            )
        ]
    )


def merge_kernel(keep_ref, got_ref, after_ref, send_ref, next_ref):
    del after_ref
    for i in range(keep_ref.shape[0]):
        total = (keep_ref[i].astype(F32) + got_ref[i].astype(F32)).astype(BF16)
        target = send_ref if i % 2 else next_ref
        target[i // 2] = total


def merge(keep, got, after):
    half = shape((keep.shape[0] // 2,) + keep.shape[1:], BF16)
    return pl.pallas_call(
        merge_kernel,
        in_specs=[IN_VMEM, IN_VMEM, UNREAD],
        out_specs=[IN_VMEM] * 2,
        out_shape=[half, half],
        compiler_params=params(2),
        name="merge",
    )(keep, got, after)


def layer_terms(depth_mix, albedo_mix, slant_rate):
    soft = jnp.maximum(depth_mix, jnp.log2(1.0 + jnp.exp2(jnp.minimum(depth_mix, 60.0))))
    e_dir = jnp.exp2(soft * slant_rate)
    bend = jnp.tanh(albedo_mix)
    gamma_one = SHIFT - bend
    gamma_two = BETA * bend + BETA
    product = (gamma_one - gamma_two) * (gamma_one + gamma_two)
    root = product * lax.rsqrt(product)
    damping = jnp.exp2(RATE * (root * soft))
    plus = gamma_one + root
    minus = gamma_one - root
    damped_sq = damping * damping
    divisor = plus - minus * damped_sq
    mirrored = plus * damped_sq - minus
    reflect = gamma_two - gamma_two * damped_sq
    transmit = (root + root) * damping
    return e_dir, gamma_two, divisor, mirrored, reflect, transmit


def mix_all(gas_ref, lanes, wide_ref):
    products = []
    for step in range(LEV // STEP):
        gas = gas_ref[:, step * STEP : (step + 1) * STEP, lanes].reshape(F * STEP, CB)
        products.append(
            jnp.dot(
                wide_ref[...],
                jnp.concatenate([gas, gas], axis=0),
                preferred_element_type=F32,
            )
        )
    return products


def eliminate(block, gas_ref, wide_ref, column_ref, solar_ref, coef_ref, esum_ref, state_ref):
    products = mix_all(gas_ref, block_lanes(block), wide_ref)
    slant_rate, rising, falling, cosine = [
        column_ref[i, pl.ds(block, 1), :] for i in range(4)
    ]
    direct = solar_ref[...] * cosine
    above = jnp.zeros((G, CB), F32)
    source = jnp.zeros((G, CB), F32)
    for l in range(LEV):
        at = (l % STEP) * 2 * G
        mix = products[l // STEP]
        e_dir, gamma_two, divisor, mirrored, reflect, transmit = layer_terms(
            mix[at : at + G], mix[at + G : at + 2 * G], slant_rate
        )
        esum_ref[l] = sum_tiles(direct + source)
        below = direct * e_dir
        scattered = gamma_two * (direct - below)
        up_source = scattered * rising
        inverse = pl.reciprocal(divisor - above * reflect, approx=False)
        incident = (source + above * up_source) * inverse
        coef_ref[l, 0] = above
        coef_ref[l, 1] = transmit * inverse
        coef_ref[l, 2] = up_source + reflect * incident
        source = scattered * falling + transmit * incident
        above = (reflect + above * mirrored) * inverse
        direct = below
    esum_ref[LEV] = sum_tiles(direct + source)
    state_ref[0] = above
    state_ref[1] = source
    state_ref[2] = direct


def add_sublanes(rows):
    sub = lax.broadcasted_iota(jnp.int32, (8, CB), 0)
    four, two, one = sub < 4, (sub & 2) == 0, (sub & 1) == 0
    rows = [
        jnp.where(four, rows[r], rows[r + 4])
        + pltpu.roll(jnp.where(four, rows[r + 4], rows[r]), 4, 0)
        for r in range(4)
    ]
    rows = [
        jnp.where(
            two,
            rows[r] + pltpu.roll(rows[r], 6, 0),
            rows[r + 2] + pltpu.roll(rows[r + 2], 2, 0),
        )
        for r in range(2)
    ]
    return jnp.where(
        one, rows[0] + pltpu.roll(rows[0], 7, 0), rows[1] + pltpu.roll(rows[1], 1, 0)
    )


def substitute(coef_ref, esum_ref, state_ref, albedo_direct, albedo_diffuse, lit, flux_ref):
    above, source, direct = state_ref[0], state_ref[1], state_ref[2]
    upward = (albedo_diffuse * source + albedo_direct * direct) * pl.reciprocal(
        1.0 - albedo_diffuse * above, approx=False
    )
    none = jnp.zeros((8, CB), F32)
    pending = [esum_ref[LEV] + sum_tiles(above * upward), sum_tiles(upward)] + [none] * 6
    flux_ref[2 * LEV : 2 * LEV + 8, :] = add_sublanes(pending) * lit
    pending = []
    for l in range(LEV - 1, -1, -1):
        upward = coef_ref[l, 1] * upward + coef_ref[l, 2]
        pending = [
            esum_ref[l] + sum_tiles(coef_ref[l, 0] * upward),
            sum_tiles(upward),
        ] + pending
        if l % 4 == 0:
            flux_ref[2 * l : 2 * l + 8, :] = add_sublanes(pending) * lit
            pending = []


COEF = (LEV, 3, G, CB)
ESUM = (LEV + 1, 8, CB)
STATE = (3, G, CB)


def down_kernel(block):
    def kernel(gas_ref, wide_ref, column_ref, solar_ref, after_ref, coef_ref, esum_ref, state_ref):
        del after_ref
        eliminate(block, gas_ref, wide_ref, column_ref, solar_ref, coef_ref, esum_ref, state_ref)

    return kernel


def down(block, gas, wide, column, solar, after):
    return pl.pallas_call(
        down_kernel(block),
        in_specs=[IN_VMEM] * 4 + [UNREAD],
        out_specs=[IN_VMEM] * 3,
        out_shape=[shape(COEF), shape(ESUM), shape(STATE)],
        compiler_params=params(6),
        cost_estimate=pl.CostEstimate(
            flops=200000000, transcendentals=0, bytes_accessed=4000000
        ),
        name="down",
    )(gas, wide, column, solar, after)


EARLY = (0, NB - 1, 1)


def up_kernel(*refs):
    parts, (keep_ref, got_ref, column_ref), flux_refs, (albedo_ref,) = (
        [refs[3 * i : 3 * i + 3] for i in range(3)],
        refs[9:12],
        refs[12:15],
        refs[15:16],
    )
    for s in range(2):
        albedo_ref[s] = keep_ref[0, s].astype(F32) + got_ref[0, s].astype(F32)
    for block, part, flux_ref in zip(EARLY, parts, flux_refs):
        at = slice(block, block + 1)
        substitute(
            *part, albedo_ref[0, at, :], albedo_ref[1, at, :], column_ref[4, at, :], flux_ref
        )


def up(parts, keep, got, column):
    return pl.pallas_call(
        up_kernel,
        in_specs=[IN_VMEM] * 12,
        out_specs=[IN_VMEM] * 4,
        out_shape=[shape((ROWS, CB))] * 3 + [shape((2, NB, CB))],
        compiler_params=params(2),
        cost_estimate=pl.CostEstimate(flops=4000000, transcendentals=0, bytes_accessed=4000000),
        name="up",
    )(*[x for part in parts for x in part], keep, got, column)


def correct(block, before, own, after, neighbour_ref, side_ref, out_ref):
    lanes = block_lanes(block)
    at_lane, firsts, lasts, weights = [], [], [], []
    for k in range(3):
        at = jnp.broadcast_to(neighbour_ref[k : k + 1, lanes], (8, CB))
        place = ((at >> 7) - block + 1) & (NB - 1)
        at_lane.append(at & (CB - 1))
        firsts.append(place == 0)
        lasts.append(place == 2)
        weights.append(jnp.broadcast_to(side_ref[k : k + 1, lanes], (8, CB)))
    for row in range(0, ROWS, 8):
        rows = [part[row : row + 8, :] for part in (before, own, after)]
        total = rows[1]
        for k in range(3):
            low, mid, high = [
                jnp.take_along_axis(x, at_lane[k], axis=1, mode="promise_in_bounds")
                for x in rows
            ]
            beside = jnp.where(firsts[k], low, jnp.where(lasts[k], high, mid))
            total = total + weights[k] * (beside - rows[1])
        for l in range(row // 2, min(row // 2 + 4, LEV + 1)):
            out_ref[l, :, lanes] = total[2 * l - row : 2 * l - row + 2]


def inner_kernel(
    gas_ref,
    wide_ref,
    column_ref,
    solar_ref,
    albedo_ref,
    first_ref,
    final_ref,
    second_ref,
    neighbour_ref,
    side_ref,
    out_ref,
    near_ref,
    coef_ref,
    esum_ref,
    state_ref,
    flux_ref,
):
    flux_ref[0] = first_ref[...]
    flux_ref[1] = second_ref[...]
    flux_ref[NB - 1] = final_ref[...]

    def start(n):
        at = n % 2
        eliminate(
            n,
            gas_ref,
            wide_ref,
            column_ref,
            solar_ref,
            coef_ref.at[at],
            esum_ref.at[at],
            state_ref.at[at],
        )

    def finish(n):
        at = n % 2
        row = pl.ds(n, 1)
        substitute(
            coef_ref.at[at],
            esum_ref.at[at],
            state_ref.at[at],
            albedo_ref[0, row, :],
            albedo_ref[1, row, :],
            column_ref[4, row, :],
            flux_ref.at[n],
        )

    def side(n):
        correct(
            n,
            flux_ref.at[(n + NB - 1) % NB],
            flux_ref.at[n],
            flux_ref.at[n + 1],
            neighbour_ref,
            side_ref,
            out_ref,
        )

    start(2)

    def turn(n, carry):
        start(n)
        finish(n - 1)
        side(n - 3)
        return carry

    lax.fori_loop(3, NB - 1, turn, 0)
    finish(NB - 2)
    for n in range(NB - 4, NB - 1):
        side(n)
    near_ref[0] = flux_ref[1]
    near_ref[1] = flux_ref[NB - 2]


def inner(gas, wide, column, solar, albedo, first, final, second, neighbours, side_weight):
    return pl.pallas_call(
        inner_kernel,
        in_specs=[IN_VMEM] * 10,
        out_specs=[IN_VMEM] * 2,
        out_shape=[shape((LEV + 1, 2, COLS)), shape((2, ROWS, CB))],
        scratch_shapes=[
            pltpu.VMEM((2,) + COEF, F32),
            pltpu.VMEM((2,) + ESUM, F32),
            pltpu.VMEM((2,) + STATE, F32),
            pltpu.VMEM((NB, ROWS, CB), F32),
        ],
        compiler_params=params(10),
        cost_estimate=pl.CostEstimate(
            flops=2000000000, transcendentals=0, bytes_accessed=4000000
        ),
        name="inner",
    )(gas, wide, column, solar, albedo, first, final, second, neighbours, side_weight)


def edge_side_kernel(
    low_ref,
    high_ref,
    first_ref,
    final_ref,
    near_ref,
    neighbour_ref,
    side_ref,
    full_ref,
    out_hbm,
    edge_ref,
    sems,
):
    middle = pl.ds(CB, COLS - 2 * CB)
    copies = [
        pltpu.make_async_copy(full_ref.at[:, :, middle], out_hbm.at[:, :, middle], sems.at[0])
    ]
    copies[0].start()
    edges = (
        (0, low_ref, first_ref, near_ref.at[0]),
        (NB - 1, near_ref.at[1], final_ref, high_ref),
    )
    for i, (block, before, own, after) in enumerate(edges):
        correct(block, before, own, after, neighbour_ref, side_ref, edge_ref)
        lanes = pl.ds(block * CB, CB)
        copies.append(
            pltpu.make_async_copy(
                edge_ref.at[:, :, lanes], out_hbm.at[:, :, lanes], sems.at[1 + i]
            )
        )
        copies[-1].start()
    for copy in copies:
        copy.wait()


def edge_side(low, high, first, final, near, neighbours, side_weight, full):
    return pl.pallas_call(
        edge_side_kernel,
        in_specs=[IN_VMEM] * 8,
        out_specs=IN_HBM,
        out_shape=shape((LEV + 1, 2, COLS)),
        scratch_shapes=[
            pltpu.VMEM((LEV + 1, 2, COLS), F32),
            pltpu.SemaphoreType.DMA((3,)),
        ],
        compiler_params=params(4),
        name="edge_side",
    )(low, high, first, final, near, neighbours, side_weight, full)


def exchange(x, bit):
    count = lax.axis_size("blk")
    return lax.ppermute(x, "blk", [(i, i ^ bit) for i in range(count)])


def local(
    gas_state,
    cos_zenith,
    daylit,
    fine_area,
    fine_albedo,
    parent_of,
    optics_weight,
    solar_weight,
    neighbours,
    side_weight,
):
    send, keep, gas, wide, column, solar, beside, weights = surface(
        parent_of,
        fine_area,
        fine_albedo,
        optics_weight,
        cos_zenith,
        daylit,
        solar_weight,
        neighbours,
        side_weight,
        gas_state,
    )
    parts = []
    for i, block in enumerate(EARLY):
        got = exchange(send, 1 << i)
        parts.append(down(block, gas, wide, column, solar, keep))
        if i < 2:
            send, keep = merge(keep, got, parts[-1][2])
    first, final, second, albedo = up(parts, keep, got, column)
    count = lax.axis_size("blk")
    low = lax.ppermute(final, "blk", [(i, (i + 1) % count) for i in range(count)])
    high = lax.ppermute(first, "blk", [((i + 1) % count, i) for i in range(count)])
    full, near = inner(
        gas, wide, column, solar, albedo, first, final, second, beside, weights
    )
    done = edge_side(low, high, first, final, near, beside, weights, full)
    return done.transpose(1, 0, 2)


def solution(mesh):
    both = ("grp", "blk")
    in_specs = (
        P(None, None, both),
        P(both),
        P(both),
        P(both),
        P(None, both),
        P(both),
        P(),
        P(),
        P(None, both),
        P(None, both),
    )
    return jax.shard_map(
        local, mesh=mesh, in_specs=in_specs, out_specs=P(None, None, both), check_vma=False
    )
```

profile of v0, /device:TPU:1, one launch (start us, length us, event | category | flops | bytes accessed | tf_op | source)
XLA Modules:
  0.0 24.8 jit_solution(13223152239441457318)
XLA Ops:
  0.0 2.8 %surface.1 = (bf16[4,2,8,128]{3,2,1,0:T(8,128)(2,1)S(1)}, bf16[4,2,8,128]{3,2,1,0:T(8,128)(2,1)S(1)}, bf16[16,32,1024]{2,1,0:T(8,128)(2,1)S(1)}, bf16[512,256]{1...) custom-call(s32[32,128]{1,0:T(8,128)} %bitcast.11, ...), custom_call_target="tpu_custom_call" | custom-call | tf_op jit(solution)/shard_map/surface/pallas_call | solution.py:199
  2.8 1.5 %collective-permute-start = (bf16[4,2,8,128]{3,2,1,0:T(8,128)(2,1)S(1)}, bf16[4,2,8,128]{3,2,1,0:T(8,128)(2,1)S(1)}, u32[]{:S(2)}, u32[]{:S(2)}) collective-permute-start(bf16[4,2,8,128]{3,2,1,0:T(8,128)(2,1)S(1)} %get-tuple-element.40), channel_id=1, source_target_pairs={{0,16},{16,0},{32,48},{48,32},{64,80},{80,64},{96,112},{112,96},{1... | collective-permute-start | bytes 49160 | tf_op jit(solution)/shard_map/ppermute | solution.py:600
  4.3 1.1 %down.3 = (f32[32,3,32,128]{3,2,1,0:T(8,128)S(1)}, f32[33,8,128]{2,1,0:T(8,128)S(1)}, f32[3,32,128]{2,1,0:T(8,128)S(1)}) custom-call(bf16[16,32,1024]{2,1,0:T(8,128)(2,1)S(1)} %get-tuple-element.32.gas_ref, bf16[512,256]{1,0:T(8,128)(2,1)S(1)} %get-tuple-element.33.wide_ref, f32[5,8,128]{2,1,0:T(8,128)S(1)} %get-tuple-element.34.column_ref.refs_11_, ...), custom_call_target="tpu_custom_call" | custom-call | flops 200000000 | bytes 4000000 | tf_op jit(solution)/shard_map/down/pallas_call | solution.py:385
  5.5 0.0 collective-permute-done.got_ref
  5.5 1.5 %collective-permute-start.1 = (bf16[2,2,8,128]{3,2,1,0:T(8,128)(2,1)S(1)}, bf16[2,2,8,128]{3,2,1,0:T(8,128)(2,1)S(1)}, u32[]{:S(2)}, u32[]{:S(2)}) collective-permute-start(bf16[2,2,8,128]{3,2,1,0:T(8,128)(2,1)S(1)} %get-tuple-element.45), channel_id=1, source_target_pairs={{0,32},{16,48},{32,0},{48,16},{64,96},{80,112},{96,64},{112,80},{1... | collective-permute-start | bytes 24584 | tf_op jit(solution)/shard_map/ppermute | solution.py:600
  6.9 1.1 %down.4 = (f32[32,3,32,128]{3,2,1,0:T(8,128)S(1)}, f32[33,8,128]{2,1,0:T(8,128)S(1)}, f32[3,32,128]{2,1,0:T(8,128)S(1)}) custom-call(bf16[16,32,1024]{2,1,0:T(8,128)(2,1)S(1)} %get-tuple-element.32.gas_ref, bf16[512,256]{1,0:T(8,128)(2,1)S(1)} %get-tuple-element.33.wide_ref, f32[5,8,128]{2,1,0:T(8,128)S(1)} %get-tuple-element.34.column_ref.refs_11_, ...), custom_call_target="tpu_custom_call" | custom-call | flops 200000000 | bytes 4000000 | tf_op jit(solution)/shard_map/down/pallas_call | solution.py:385
  8.1 0.0 collective-permute-done.1.got_ref
  8.1 3.0 %collective-permute-start.2 = (bf16[1,2,8,128]{3,2,1,0:T(8,128)(2,1)S(1)}, bf16[1,2,8,128]{3,2,1,0:T(8,128)(2,1)S(1)}, u32[]{:S(2)}, u32[]{:S(2)}) collective-permute-start(bf16[1,2,8,128]{3,2,1,0:T(8,128)(2,1)S(1)} %get-tuple-element.50), channel_id=1, source_target_pairs={{0,64},{16,80},{32,96},{48,112},{64,0},{80,16},{96,32},{112,48},{1... | collective-permute-start | bytes 12296 | tf_op jit(solution)/shard_map/ppermute | solution.py:600
  11.1 1.1 %down.5 = (f32[32,3,32,128]{3,2,1,0:T(8,128)S(1)}, f32[33,8,128]{2,1,0:T(8,128)S(1)}, f32[3,32,128]{2,1,0:T(8,128)S(1)}) custom-call(bf16[16,32,1024]{2,1,0:T(8,128)(2,1)S(1)} %get-tuple-element.32.gas_ref, bf16[512,256]{1,0:T(8,128)(2,1)S(1)} %get-tuple-element.33.wide_ref, f32[5,8,128]{2,1,0:T(8,128)S(1)} %get-tuple-element.34.column_ref.refs_11_, ...), custom_call_target="tpu_custom_call" | custom-call | flops 200000000 | bytes 4000000 | tf_op jit(solution)/shard_map/down/pallas_call | solution.py:385
  12.2 0.0 collective-permute-done.2.refs_10_
  12.2 0.4 %up.1 = (f32[72,128]{1,0:T(8,128)S(1)}, f32[72,128]{1,0:T(8,128)S(1)}, f32[72,128]{1,0:T(8,128)S(1)}, f32[2,8,128]{2,1,0:T(8,128)S(1)}) custom-call(f32[32,3,32,128]{3,2,1,0:T(8,128)S(1)} %get-tuple-element.37.refs_0_, f32[33,8,128]{2,1,0:T(8,128)S(1)} %get-tuple-element.38.refs_1_, f32[3,32,128]{2,1,0:T(8,128)S(1)} %get-tuple-element.39.after_ref.refs_2_, ...), custom_call_target="tpu_custom_call" | custom-call | flops 4000000 | bytes 4000000 | tf_op jit(solution)/shard_map/up/pallas_call | solution.py:418
  12.6 3.4 %collective-permute-start.3 = (f32[72,128]{1,0:T(8,128)S(1)}, f32[72,128]{1,0:T(8,128)S(1)}, u32[]{:S(2)}, u32[]{:S(2)}) collective-permute-start(f32[72,128]{1,0:T(8,128)S(1)} %get-tuple-element.51.final_ref), channel_id=1, source_target_pairs={{0,16},{16,32},{32,48},{48,64},{64,80},{80,96},{96,112},{112,0},{1... | collective-permute-start | bytes 110600 | tf_op jit(solution)/shard_map/ppermute | solution.py:635
  16.0 0.0 collective-permute-start.4
  16.0 7.7 %inner.1 = (f32[33,2,1024]{2,1,0:T(2,128)S(1)}, f32[2,72,128]{2,1,0:T(8,128)S(1)}) custom-call(bf16[16,32,1024]{2,1,0:T(8,128)(2,1)S(1)} %get-tuple-element.32.gas_ref, bf16[512,256]{1,0:T(8,128)(2,1)S(1)} %get-tuple-element.33.wide_ref, f32[5,8,128]{2,1,0:T(8,128)S(1)} %get-tuple-element.34.column_ref.refs_11_, f32[32,128]{1,0:T(8,128)S(1)} %get-tuple-element.35.solar_ref, ...), custom_call_target="tpu_custom_call" | custom-call | flops 2000000000 | bytes 4000000 | tf_op jit(solution)/shard_map/inner/pallas_call | solution.py:529
  23.8 0.0 collective-permute-done.3.low_ref
  23.8 0.0 collective-permute-done.4.high_ref
  23.8 1.1 %edge_side.1 = f32[33,2,1024]{2,1,0:T(2,128)} custom-call(f32[72,128]{1,0:T(8,128)S(1)} %collective-permute-done.3.low_ref, f32[72,128]{1,0:T(8,128)S(1)} %collective-permute-done.4.high_ref, f32[72,128]{1,0:T(8,128)S(1)} %get-tuple-element.52.first_ref, f32[72,128]{1,0:T(8,128)S(1)} %get-tuple-element.51.final_ref, ...), custom_call_target="tpu_custom_call" | custom-call | tf_op jit(solution)/shard_map/edge_side/pallas_call | solution.py:584
  (2 shorter events, 0.0 us)
Async XLA Ops:
  2.8 2.6 %collective-permute-start = (bf16[4,2,8,128]{3,2,1,0:T(8,128)(2,1)S(1)}, bf16[4,2,8,128]{3,2,1,0:T(8,128)(2,1)S(1)}, u32[]{:S(2)}, u32[]{:S(2)}) collective-permute-start(bf16[4,2,8,128]{3,2,1,0:T(8,128)(2,1)S(1)} %get-tuple-element.40), channel_id=1, source_target_pairs={{0,16},{16,0},{32,48},{48,32},{64,80},{80,64},{96,112},{112,96},{1... | collective-permute-start | bytes 49160 | tf_op jit(solution)/shard_map/ppermute | solution.py:600
  5.5 2.6 %collective-permute-start.1 = (bf16[2,2,8,128]{3,2,1,0:T(8,128)(2,1)S(1)}, bf16[2,2,8,128]{3,2,1,0:T(8,128)(2,1)S(1)}, u32[]{:S(2)}, u32[]{:S(2)}) collective-permute-start(bf16[2,2,8,128]{3,2,1,0:T(8,128)(2,1)S(1)} %get-tuple-element.45), channel_id=1, source_target_pairs={{0,32},{16,48},{32,0},{48,16},{64,96},{80,112},{96,64},{112,80},{1... | collective-permute-start | bytes 24584 | tf_op jit(solution)/shard_map/ppermute | solution.py:600
  8.1 4.1 %collective-permute-start.2 = (bf16[1,2,8,128]{3,2,1,0:T(8,128)(2,1)S(1)}, bf16[1,2,8,128]{3,2,1,0:T(8,128)(2,1)S(1)}, u32[]{:S(2)}, u32[]{:S(2)}) collective-permute-start(bf16[1,2,8,128]{3,2,1,0:T(8,128)(2,1)S(1)} %get-tuple-element.50), channel_id=1, source_target_pairs={{0,64},{16,80},{32,96},{48,112},{64,0},{80,16},{96,32},{112,48},{1... | collective-permute-start | bytes 12296 | tf_op jit(solution)/shard_map/ppermute | solution.py:600
  12.6 11.1 %collective-permute-start.3 = (f32[72,128]{1,0:T(8,128)S(1)}, f32[72,128]{1,0:T(8,128)S(1)}, u32[]{:S(2)}, u32[]{:S(2)}) collective-permute-start(f32[72,128]{1,0:T(8,128)S(1)} %get-tuple-element.51.final_ref), channel_id=1, source_target_pairs={{0,16},{16,32},{32,48},{48,64},{64,80},{80,96},{96,112},{112,0},{1... | collective-permute-start | bytes 110600 | tf_op jit(solution)/shard_map/ppermute | solution.py:635
  16.0 7.7 %collective-permute-start.4 = (f32[72,128]{1,0:T(8,128)S(1)}, f32[72,128]{1,0:T(8,128)S(1)}, u32[]{:S(2)}, u32[]{:S(2)}) collective-permute-start(f32[72,128]{1,0:T(8,128)S(1)} %get-tuple-element.52.first_ref), channel_id=1, source_target_pairs={{16,0},{32,16},{48,32},{64,48},{80,64},{96,80},{112,96},{0,112},{1... | collective-permute-start | bytes 110600 | tf_op jit(solution)/shard_map/ppermute | solution.py:636
where the time goes:
time: 25.3 us; the launch traced here: 24.8 us
  Pallas kernels  15.4 us (61%)
  starting transfers between devices  9.3 us (37%)
    pallas_call x1, Pallas kernels, inner(): pl.pallas_call(inner_kernel, in_specs=[IN_VMEM] * 10, out_specs=[IN_VMEM]...  7.73 us
    ppermute x3, starting transfers between devices, exchange(): return lax.ppermute(x, 'blk', [(i, i ^ bit) for i in range(count)])  5.91 us
    pallas_call x3, Pallas kernels, down(): pl.pallas_call(down_kernel(block), in_specs=[IN_VMEM] * 4 + [UNREAD], out...  3.42 us
    ppermute x1, starting transfers between devices, local(): lax.ppermute(final, 'blk', [(i, (i + 1) % count) for i in range(count)])  3.39 us
    pallas_call x1, Pallas kernels, surface(): pl.pallas_call(surface_kernel, in_specs=[IN_HBM] * 10, out_specs=[IN_VMEM...  2.81 us
    pallas_call x1, Pallas kernels, edge_side(): pl.pallas_call(edge_side_kernel, in_specs=[IN_VMEM] * 8, out_specs=IN_HBM...  1.06 us
  transfers between devices with their start and end apart: 5, of which 0 were waited for; matrix products, arithmetic and copies ran while one was open for 0% of the time, Pallas kernels for 45%

commit v1 on v0

--- a/solution.py
+++ b/solution.py
@@ -52,28 +52,44 @@
     return pl.ds(pl.multiple_of(block * CB, CB), CB)
 
 
-def place_albedo(parent_ref, area_ref, albedo_ref, part_ref, mine):
-    sub = lax.broadcasted_iota(jnp.int32, (CB, CB), 0)
-    for j in range(FINE_BLOCKS):
-        parent = parent_ref[j : j + 1, :]
-        hot = jnp.where((parent & (CB - 1)) == sub, 1.0, 0.0).astype(BF16)
-        area = area_ref[j : j + 1, :]
-        terms = jnp.concatenate(
-            [area, area * albedo_ref[j, 0:1, :], area * albedo_ref[j, 1:2, :]], axis=0
+def place_albedo(parent_ref, area_ref, albedo_ref, mine):
+    sub = lax.broadcasted_iota(jnp.int32, (CB, CB), 0).astype(F32).astype(BF16)
+    line = lax.broadcasted_iota(jnp.int32, (8, CB), 0)
+    one, zero = jnp.ones((), BF16), jnp.zeros((), BF16)
+    totals = [[], [], []]
+    for group in range(0, FINE_BLOCKS, 8):
+        rows = slice(group, group + 8)
+        area = area_ref[rows, :]
+        terms = [area, area * albedo_ref[0, rows, :], area * albedo_ref[1, rows, :]]
+        pieces = []
+        for term in terms:
+            for _ in range(3):
+                piece = term.astype(BF16).astype(F32)
+                pieces.append(piece)
+                term = term - piece
+        column = (parent_ref[rows, :] & (CB - 1)).astype(F32).astype(BF16)
+        hots, values = [], []
+        for j in range(8):
+            hots.append(
+                jnp.where(jnp.broadcast_to(column[j : j + 1, :], (CB, CB)) == sub, one, zero)
+            )
+            values.append(
+                jnp.concatenate([jnp.where(line == j, x, 0.0) for x in pieces], axis=0).astype(
+                    BF16
+                )
+            )
+        total = lax.dot_general(
+            jnp.concatenate(values, axis=1),
+            jnp.concatenate(hots, axis=1),
+            (((1,), (1,)), ((), ())),
+            preferred_element_type=F32,
         )
-        first = terms.astype(BF16)
-        rest = terms - first.astype(F32)
-        second = rest.astype(BF16)
-        third = (rest - second.astype(F32)).astype(BF16)
-        dims = (((1,), (1,)), ((), ()))
-        total = lax.dot_general(first, hot, dims, preferred_element_type=F32)
-        total = total + (
-            lax.dot_general(second, hot, dims, preferred_element_type=F32)
-            + lax.dot_general(third, hot, dims, preferred_element_type=F32)
-        )
-        for row in range(3):
-            part_ref[row, j : j + 1, :] = total[row : row + 1, :]
-    area = part_ref[0]
+        for i in range(3):
+            at = 24 * i
+            totals[i].append(
+                total[at : at + 8] + (total[at + 8 : at + 16] + total[at + 16 : at + 24])
+            )
+    area = jnp.concatenate(totals[0], axis=0)
     here = area > 0.0
     safe = jnp.where(here, area, 1.0)
     owner = (parent_ref[:, 0:1] >> 7) ^ (mine * NB)
@@ -81,7 +97,8 @@
     where_to = jnp.where(owner == slot, 1.0, 0.0).astype(BF16)
     placed = []
     for s in range(2):
-        albedo = jnp.where(here, part_ref[1 + s] / safe, 0.0).astype(BF16)
+        total = jnp.concatenate(totals[1 + s], axis=0)
+        albedo = jnp.where(here, total / safe, 0.0).astype(BF16)
         placed.append(
             lax.dot_general(
                 where_to, albedo, (((0,), (0,)), ((), ())), preferred_element_type=F32
@@ -145,13 +162,13 @@
     cosine_ref,
     lit_ref,
     sun_ref,
-    part_ref,
     sems,
 ):
     pairs = (
         (parent_hbm, parent_ref),
         (area_hbm, area_ref),
-        (albedo_hbm, albedo_ref),
+        (albedo_hbm.at[:, 0, :], albedo_ref.at[0]),
+        (albedo_hbm.at[:, 1, :], albedo_ref.at[1]),
         (weight_hbm, weight_ref),
         (cosine_hbm, cosine_ref),
         (lit_hbm, lit_ref),
@@ -166,10 +183,10 @@
     ]
     for copy in copies:
         copy.start()
-    for copy in copies[:7]:
+    for copy in copies[:8]:
         copy.wait()
     mine = lax.axis_index("blk")
-    placed = place_albedo(parent_ref, area_ref, albedo_ref, part_ref, mine)
+    placed = place_albedo(parent_ref, area_ref, albedo_ref, mine)
     for s in range(2):
         for i in range(NBLK // 2):
             keep_ref[i, s] = placed[s][2 * i * NB : (2 * i + 1) * NB]
@@ -180,7 +197,7 @@
     col = lax.broadcasted_iota(jnp.int32, (G, G), 1)
     sun = jnp.sum(jnp.where(row == col, sun_ref[...], 0.0), axis=1, keepdims=True)
     solar_ref[...] = jnp.broadcast_to(sun, (G, CB))
-    for copy in copies[7:]:
+    for copy in copies[8:]:
         copy.wait()
 
 
@@ -213,13 +230,12 @@
         scratch_shapes=[
             pltpu.VMEM((FINE_BLOCKS, CB), jnp.int32),
             pltpu.VMEM((FINE_BLOCKS, CB), F32),
-            pltpu.VMEM((FINE_BLOCKS, 2, CB), F32),
+            pltpu.VMEM((2, FINE_BLOCKS, CB), F32),
             pltpu.VMEM((F, 2 * G), BF16),
             pltpu.VMEM((NB, CB), BF16),
             pltpu.VMEM((NB, CB), jnp.int32),
             pltpu.VMEM((1, G), F32),
-            pltpu.VMEM((3, FINE_BLOCKS, CB), F32),
-            pltpu.SemaphoreType.DMA((10,)),
+            pltpu.SemaphoreType.DMA((11,)),
         ],
         compiler_params=params(4),
         name="surface",
@@ -271,14 +287,12 @@
     product = (gamma_one - gamma_two) * (gamma_one + gamma_two)
     root = product * lax.rsqrt(product)
     damping = jnp.exp2(RATE * (root * soft))
-    plus = gamma_one + root
-    minus = gamma_one - root
     damped_sq = damping * damping
-    divisor = plus - minus * damped_sq
-    mirrored = plus * damped_sq - minus
-    reflect = gamma_two - gamma_two * damped_sq
+    lost = 1.0 - damped_sq
+    even = root + root * damped_sq
+    odd = gamma_one * lost
     transmit = (root + root) * damping
-    return e_dir, gamma_two, divisor, mirrored, reflect, transmit
+    return e_dir, gamma_two, even + odd, even - odd, gamma_two * lost, transmit
 
 
 def mix_all(gas_ref, lanes, wide_ref):
@@ -373,61 +387,95 @@
 STATE = (3, G, CB)
 
 
-def down_kernel(block):
+def down_kernel(blocks):
     def kernel(gas_ref, wide_ref, column_ref, solar_ref, after_ref, coef_ref, esum_ref, state_ref):
         del after_ref
-        eliminate(block, gas_ref, wide_ref, column_ref, solar_ref, coef_ref, esum_ref, state_ref)
+        for i, block in enumerate(blocks):
+            eliminate(
+                block,
+                gas_ref,
+                wide_ref,
+                column_ref,
+                solar_ref,
+                coef_ref.at[i],
+                esum_ref.at[i],
+                state_ref.at[i],
+            )
 
     return kernel
 
 
-def down(block, gas, wide, column, solar, after):
+def down(blocks, gas, wide, column, solar, after):
+    count = len(blocks)
     return pl.pallas_call(
-        down_kernel(block),
+        down_kernel(blocks),
         in_specs=[IN_VMEM] * 4 + [UNREAD],
         out_specs=[IN_VMEM] * 3,
-        out_shape=[shape(COEF), shape(ESUM), shape(STATE)],
-        compiler_params=params(6),
+        out_shape=[shape((count,) + x) for x in (COEF, ESUM, STATE)],
+        compiler_params=params(24),
         cost_estimate=pl.CostEstimate(
-            flops=200000000, transcendentals=0, bytes_accessed=4000000
+            flops=200000000 * count, transcendentals=0, bytes_accessed=4000000
         ),
         name="down",
     )(gas, wide, column, solar, after)
 
 
-EARLY = (0, NB - 1, 1)
-
-
-def up_kernel(*refs):
-    parts, (keep_ref, got_ref, column_ref), flux_refs, (albedo_ref,) = (
-        [refs[3 * i : 3 * i + 3] for i in range(3)],
-        refs[9:12],
-        refs[12:15],
-        refs[15:16],
-    )
+WINDOWS = ((0,), (NB - 1, 1), (2, 3, 4))
+LATE = (5, 6)
+
+
+def ground(albedo_ref, column_ref, block):
+    row = slice(block, block + 1)
+    return albedo_ref[0, row, :], albedo_ref[1, row, :], column_ref[4, row, :]
+
+
+def up_kernel(
+    coef_a,
+    esum_a,
+    state_a,
+    coef_b,
+    esum_b,
+    state_b,
+    keep_ref,
+    got_ref,
+    column_ref,
+    first_ref,
+    final_ref,
+    near_ref,
+    far_ref,
+    albedo_ref,
+):
     for s in range(2):
         albedo_ref[s] = keep_ref[0, s].astype(F32) + got_ref[0, s].astype(F32)
-    for block, part, flux_ref in zip(EARLY, parts, flux_refs):
-        at = slice(block, block + 1)
-        substitute(
-            *part, albedo_ref[0, at, :], albedo_ref[1, at, :], column_ref[4, at, :], flux_ref
-        )
+    substitute(
+        coef_a.at[0], esum_a.at[0], state_a.at[0], *ground(albedo_ref, column_ref, 0), first_ref
+    )
+    substitute(
+        coef_b.at[0],
+        esum_b.at[0],
+        state_b.at[0],
+        *ground(albedo_ref, column_ref, NB - 1),
+        final_ref,
+    )
+    even = lax.axis_index("blk") % 2 == 0
+    near_ref[...] = jnp.where(even, final_ref[...], first_ref[...])
+    far_ref[...] = jnp.where(even, first_ref[...], final_ref[...])
 
 
 def up(parts, keep, got, column):
     return pl.pallas_call(
         up_kernel,
-        in_specs=[IN_VMEM] * 12,
-        out_specs=[IN_VMEM] * 4,
-        out_shape=[shape((ROWS, CB))] * 3 + [shape((2, NB, CB))],
+        in_specs=[IN_VMEM] * 9,
+        out_specs=[IN_VMEM] * 5,
+        out_shape=[shape((ROWS, CB))] * 4 + [shape((2, NB, CB))],
         compiler_params=params(2),
         cost_estimate=pl.CostEstimate(flops=4000000, transcendentals=0, bytes_accessed=4000000),
         name="up",
-    )(*[x for part in parts for x in part], keep, got, column)
+    )(*parts[0], *parts[1], keep, got, column)
 
 
 def correct(block, before, own, after, neighbour_ref, side_ref, out_ref):
-    lanes = block_lanes(block)
+    lanes = slice(block * CB, (block + 1) * CB)
     at_lane, firsts, lasts, weights = [], [], [], []
     for k in range(3):
         at = jnp.broadcast_to(neighbour_ref[k : k + 1, lanes], (8, CB))
@@ -437,7 +485,7 @@
         lasts.append(place == 2)
         weights.append(jnp.broadcast_to(side_ref[k : k + 1, lanes], (8, CB)))
     for row in range(0, ROWS, 8):
-        rows = [part[row : row + 8, :] for part in (before, own, after)]
+        rows = [part(row) for part in (before, own, after)]
         total = rows[1]
         for k in range(3):
             low, mid, high = [
@@ -450,6 +498,10 @@
             out_ref[l, :, lanes] = total[2 * l - row : 2 * l - row + 2]
 
 
+def rows_of(ref):
+    return lambda row: ref[row : row + 8, :]
+
+
 def inner_kernel(
     gas_ref,
     wide_ref,
@@ -458,7 +510,12 @@
     albedo_ref,
     first_ref,
     final_ref,
-    second_ref,
+    coef_b,
+    esum_b,
+    state_b,
+    coef_c,
+    esum_c,
+    state_c,
     neighbour_ref,
     side_ref,
     out_ref,
@@ -468,89 +525,80 @@
     state_ref,
     flux_ref,
 ):
-    flux_ref[0] = first_ref[...]
-    flux_ref[1] = second_ref[...]
-    flux_ref[NB - 1] = final_ref[...]
+    kept = {1: (coef_b.at[1], esum_b.at[1], state_b.at[1])}
+    for i, n in enumerate(WINDOWS[2]):
+        kept[n] = coef_c.at[i], esum_c.at[i], state_c.at[i]
+    for i, n in enumerate(LATE):
+        kept[n] = coef_ref.at[i], esum_ref.at[i], state_ref.at[i]
+    flux = {0: first_ref, 1: near_ref.at[0], NB - 2: near_ref.at[1], NB - 1: final_ref}
+    for n in range(2, NB - 2):
+        flux[n] = flux_ref.at[n - 2]
 
     def start(n):
-        at = n % 2
-        eliminate(
-            n,
-            gas_ref,
-            wide_ref,
-            column_ref,
-            solar_ref,
-            coef_ref.at[at],
-            esum_ref.at[at],
-            state_ref.at[at],
-        )
+        eliminate(n, gas_ref, wide_ref, column_ref, solar_ref, *kept[n])
 
     def finish(n):
-        at = n % 2
-        row = pl.ds(n, 1)
-        substitute(
-            coef_ref.at[at],
-            esum_ref.at[at],
-            state_ref.at[at],
-            albedo_ref[0, row, :],
-            albedo_ref[1, row, :],
-            column_ref[4, row, :],
-            flux_ref.at[n],
-        )
+        substitute(*kept[n], *ground(albedo_ref, column_ref, n), flux[n])
 
     def side(n):
-        correct(
-            n,
-            flux_ref.at[(n + NB - 1) % NB],
-            flux_ref.at[n],
-            flux_ref.at[n + 1],
-            neighbour_ref,
-            side_ref,
-            out_ref,
-        )
-
-    start(2)
-
-    def turn(n, carry):
-        start(n)
-        finish(n - 1)
-        side(n - 3)
-        return carry
-
-    lax.fori_loop(3, NB - 1, turn, 0)
-    finish(NB - 2)
-    for n in range(NB - 4, NB - 1):
-        side(n)
-    near_ref[0] = flux_ref[1]
-    near_ref[1] = flux_ref[NB - 2]
-
-
-def inner(gas, wide, column, solar, albedo, first, final, second, neighbours, side_weight):
+        before, own, after = [rows_of(flux[n + i]) for i in (-1, 0, 1)]
+        correct(n, before, own, after, neighbour_ref, side_ref, out_ref)
+
+    start(5)
+    finish(1)
+    finish(2)
+    side(1)
+    start(6)
+    finish(3)
+    finish(4)
+    side(2)
+    side(3)
+    finish(5)
+    finish(6)
+    side(4)
+    side(5)
+    side(6)
+
+
+def inner(gas, wide, column, solar, albedo, first, final, parts, neighbours, side_weight):
+    count = len(LATE)
     return pl.pallas_call(
         inner_kernel,
-        in_specs=[IN_VMEM] * 10,
+        in_specs=[IN_VMEM] * 15,
         out_specs=[IN_VMEM] * 2,
         out_shape=[shape((LEV + 1, 2, COLS)), shape((2, ROWS, CB))],
         scratch_shapes=[
-            pltpu.VMEM((2,) + COEF, F32),
-            pltpu.VMEM((2,) + ESUM, F32),
-            pltpu.VMEM((2,) + STATE, F32),
-            pltpu.VMEM((NB, ROWS, CB), F32),
+            pltpu.VMEM((count,) + COEF, F32),
+            pltpu.VMEM((count,) + ESUM, F32),
+            pltpu.VMEM((count,) + STATE, F32),
+            pltpu.VMEM((NB - 4, ROWS, CB), F32),
         ],
-        compiler_params=params(10),
+        compiler_params=params(24),
         cost_estimate=pl.CostEstimate(
             flops=2000000000, transcendentals=0, bytes_accessed=4000000
         ),
         name="inner",
-    )(gas, wide, column, solar, albedo, first, final, second, neighbours, side_weight)
+    )(
+        gas,
+        wide,
+        column,
+        solar,
+        albedo,
+        first,
+        final,
+        *parts[1],
+        *parts[2],
+        neighbours,
+        side_weight,
+    )
 
 
 def edge_side_kernel(
-    low_ref,
-    high_ref,
+    near_got,
+    far_got,
     first_ref,
     final_ref,
-    near_ref,
+    inside_ref,
     neighbour_ref,
     side_ref,
     full_ref,
@@ -558,29 +606,41 @@
     edge_ref,
     sems,
 ):
-    middle = pl.ds(CB, COLS - 2 * CB)
-    copies = [
-        pltpu.make_async_copy(full_ref.at[:, :, middle], out_hbm.at[:, :, middle], sems.at[0])
-    ]
+    def copy(source, lanes, i):
+        return pltpu.make_async_copy(
+            source.at[:, :, lanes], out_hbm.at[:, :, lanes], sems.at[i]
+        )
+
+    copies = [copy(full_ref, pl.ds(CB, COLS - 2 * CB), 0)]
     copies[0].start()
-    edges = (
-        (0, low_ref, first_ref, near_ref.at[0]),
-        (NB - 1, near_ref.at[1], final_ref, high_ref),
-    )
-    for i, (block, before, own, after) in enumerate(edges):
-        correct(block, before, own, after, neighbour_ref, side_ref, edge_ref)
-        lanes = pl.ds(block * CB, CB)
-        copies.append(
-            pltpu.make_async_copy(
-                edge_ref.at[:, :, lanes], out_hbm.at[:, :, lanes], sems.at[1 + i]
-            )
-        )
+    even = lax.axis_index("blk") % 2 == 0
+    near, far = rows_of(near_got), rows_of(far_got)
+    correct(
+        0,
+        lambda row: jnp.where(even, far(row), near(row)),
+        rows_of(first_ref),
+        rows_of(inside_ref.at[0]),
+        neighbour_ref,
+        side_ref,
+        edge_ref,
+    )
+    correct(
+        NB - 1,
+        rows_of(inside_ref.at[1]),
+        rows_of(final_ref),
+        lambda row: jnp.where(even, near(row), far(row)),
+        neighbour_ref,
+        side_ref,
+        edge_ref,
+    )
+    for i, block in enumerate((0, NB - 1)):
+        copies.append(copy(edge_ref, pl.ds(block * CB, CB), 1 + i))
         copies[-1].start()
-    for copy in copies:
-        copy.wait()
-
-
-def edge_side(low, high, first, final, near, neighbours, side_weight, full):
+    for started in copies:
+        started.wait()
+
+
+def edge_side(near_got, far_got, first, final, inside, neighbours, side_weight, full):
     return pl.pallas_call(
         edge_side_kernel,
         in_specs=[IN_VMEM] * 8,
@@ -592,7 +652,7 @@
         ],
         compiler_params=params(4),
         name="edge_side",
-    )(low, high, first, final, near, neighbours, side_weight, full)
+    )(near_got, far_got, first, final, inside, neighbours, side_weight, full)
 
 
 def exchange(x, bit):
@@ -625,19 +685,20 @@
         gas_state,
     )
     parts = []
-    for i, block in enumerate(EARLY):
+    for i, blocks in enumerate(WINDOWS):
         got = exchange(send, 1 << i)
-        parts.append(down(block, gas, wide, column, solar, keep))
+        parts.append(down(blocks, gas, wide, column, solar, keep))
         if i < 2:
             send, keep = merge(keep, got, parts[-1][2])
-    first, final, second, albedo = up(parts, keep, got, column)
+    first, final, near, far, albedo = up(parts, keep, got, column)
+    near_got = exchange(near, 1)
     count = lax.axis_size("blk")
-    low = lax.ppermute(final, "blk", [(i, (i + 1) % count) for i in range(count)])
-    high = lax.ppermute(first, "blk", [((i + 1) % count, i) for i in range(count)])
-    full, near = inner(
-        gas, wide, column, solar, albedo, first, final, second, beside, weights
-    )
-    done = edge_side(low, high, first, final, near, beside, weights, full)
+    beyond = [(i, (i + (1 if i % 2 else -1)) % count) for i in range(count)]
+    far_got = lax.ppermute(far, "blk", beyond)
+    full, inside = inner(
+        gas, wide, column, solar, albedo, first, final, parts, beside, weights
+    )
+    done = edge_side(near_got, far_got, first, final, inside, beside, weights, full)
     return done.transpose(1, 0, 2)
 
 

time: 25.3 us -> 19.8 us (0.78)
  Pallas kernels: 15.4 us -> 12.5 us
  starting transfers between devices: 9.3 us -> 6.82 us
    ppermute x2 -> x1, starting transfers between devices: 3.4 us -> 0.37 us  [local(): far_got = lax.ppermute(far, 'blk', beyond)]
    pallas_call x5, Pallas kernels: 11.6 us -> 9.91 us  [the longest x3 6.37 us: down(): pl.pallas_call(down_kernel(blocks), in_specs=[IN_VMEM] * 4 + [UNREAD], ou...]
    pallas_call x1, Pallas kernels: 2.81 us -> 1.54 us  [surface(): pl.pallas_call(surface_kernel, in_specs=[IN_HBM] * 10, out_specs=[IN_VMEM...]
    ppermute x3 -> x4, starting transfers between devices: 5.91 us -> 6.44 us  [exchange(): return lax.ppermute(x, 'blk', [(i, i ^ bit) for i in range(count)])]
  transfers between devices with their start and end apart: 5 -> 5, of which waited for: 0 -> 0; matrix products, arithmetic and copies ran while one was open for 0% -> 0% of each run, Pallas kernels for 45% -> 49%
where the time goes in v1:
time: 19.8 us; the launch traced here: 19.5 us
  Pallas kernels  12.5 us (63%)
  starting transfers between devices  6.82 us (34%)
    ppermute x4, starting transfers between devices, exchange(): return lax.ppermute(x, 'blk', [(i, i ^ bit) for i in range(count)])  6.44 us
    pallas_call x3, Pallas kernels, down(): pl.pallas_call(down_kernel(blocks), in_specs=[IN_VMEM] * 4 + [UNREAD], ou...  6.37 us
    pallas_call x1, Pallas kernels, inner(): pl.pallas_call(inner_kernel, in_specs=[IN_VMEM] * 15, out_specs=[IN_VMEM]...  3.24 us
    pallas_call x1, Pallas kernels, surface(): pl.pallas_call(surface_kernel, in_specs=[IN_HBM] * 10, out_specs=[IN_VMEM...  1.54 us
    pallas_call x1, Pallas kernels, edge_side(): pl.pallas_call(edge_side_kernel, in_specs=[IN_VMEM] * 8, out_specs=IN_HBM...  1.08 us
  transfers between devices with their start and end apart: 5, of which 0 were waited for; matrix products, arithmetic and copies ran while one was open for 0% of the time, Pallas kernels for 49%

profile of v1, /device:TPU:1, one launch (start us, length us, event | category | flops | bytes accessed | tf_op | source)
XLA Modules:
  0.0 19.5 jit_solution(5830779940744189732)
XLA Ops:
  0.0 1.5 %surface.1 = (bf16[4,2,8,128]{3,2,1,0:T(8,128)(2,1)S(1)}, bf16[4,2,8,128]{3,2,1,0:T(8,128)(2,1)S(1)}, bf16[16,32,1024]{2,1,0:T(8,128)(2,1)S(1)}, bf16[512,256]{1...) custom-call(s32[32,128]{1,0:T(8,128)} %bitcast.11, ...), custom_call_target="tpu_custom_call" | custom-call | tf_op jit(solution)/shard_map/surface/pallas_call | solution.py:216
  1.6 1.5 %collective-permute-start = (bf16[4,2,8,128]{3,2,1,0:T(8,128)(2,1)S(1)}, bf16[4,2,8,128]{3,2,1,0:T(8,128)(2,1)S(1)}, u32[]{:S(2)}, u32[]{:S(2)}) collective-permute-start(bf16[4,2,8,128]{3,2,1,0:T(8,128)(2,1)S(1)} %get-tuple-element.41), channel_id=1, source_target_pairs={{0,16},{16,0},{32,48},{48,32},{64,80},{80,64},{96,112},{112,96},{1... | collective-permute-start | bytes 49160 | tf_op jit(solution)/shard_map/ppermute | solution.py:660
  3.1 1.1 %down.3 = (f32[1,32,3,32,128]{4,3,2,1,0:T(8,128)S(1)}, f32[1,33,8,128]{3,2,1,0:T(8,128)S(1)}, f32[1,3,32,128]{3,2,1,0:T(8,128)S(1)}) custom-call(bf16[16,32,1024]{2,1,0:T(8,128)(2,1)S(1)} %get-tuple-element.33.gas_ref, bf16[512,256]{1,0:T(8,128)(2,1)S(1)} %get-tuple-element.34.wide_ref, f32[5,8,128]{2,1,0:T(8,128)S(1)} %get-tuple-element.35.column_ref, ...), custom_call_target="tpu_custom_call" | custom-call | flops 200000000 | bytes 4000000 | tf_op jit(solution)/shard_map/down/pallas_call | solution.py:410
  4.2 0.0 collective-permute-done.got_ref
  4.2 1.5 %collective-permute-start.1 = (bf16[2,2,8,128]{3,2,1,0:T(8,128)(2,1)S(1)}, bf16[2,2,8,128]{3,2,1,0:T(8,128)(2,1)S(1)}, u32[]{:S(2)}, u32[]{:S(2)}) collective-permute-start(bf16[2,2,8,128]{3,2,1,0:T(8,128)(2,1)S(1)} %get-tuple-element.46), channel_id=1, source_target_pairs={{0,32},{16,48},{32,0},{48,16},{64,96},{80,112},{96,64},{112,80},{1... | collective-permute-start | bytes 24584 | tf_op jit(solution)/shard_map/ppermute | solution.py:660
  5.7 2.1 %down.4 = (f32[2,32,3,32,128]{4,3,2,1,0:T(8,128)S(1)}, f32[2,33,8,128]{3,2,1,0:T(8,128)S(1)}, f32[2,3,32,128]{3,2,1,0:T(8,128)S(1)}) custom-call(bf16[16,32,1024]{2,1,0:T(8,128)(2,1)S(1)} %get-tuple-element.33.gas_ref, bf16[512,256]{1,0:T(8,128)(2,1)S(1)} %get-tuple-element.34.wide_ref, f32[5,8,128]{2,1,0:T(8,128)S(1)} %get-tuple-element.35.column_ref, ...), custom_call_target="tpu_custom_call" | custom-call | flops 400000000 | bytes 4000000 | tf_op jit(solution)/shard_map/down/pallas_call | solution.py:410
  7.8 0.0 collective-permute-done.1.got_ref
  7.8 2.7 %collective-permute-start.2 = (bf16[1,2,8,128]{3,2,1,0:T(8,128)(2,1)S(1)}, bf16[1,2,8,128]{3,2,1,0:T(8,128)(2,1)S(1)}, u32[]{:S(2)}, u32[]{:S(2)}) collective-permute-start(bf16[1,2,8,128]{3,2,1,0:T(8,128)(2,1)S(1)} %get-tuple-element.48), channel_id=1, source_target_pairs={{0,64},{16,80},{32,96},{48,112},{64,0},{80,16},{96,32},{112,48},{1... | collective-permute-start | bytes 12296 | tf_op jit(solution)/shard_map/ppermute | solution.py:660
  10.5 3.1 %down.5 = (f32[3,32,3,32,128]{4,3,2,1,0:T(8,128)S(1)}, f32[3,33,8,128]{3,2,1,0:T(8,128)S(1)}, f32[3,3,32,128]{3,2,1,0:T(8,128)S(1)}) custom-call(bf16[16,32,1024]{2,1,0:T(8,128)(2,1)S(1)} %get-tuple-element.33.gas_ref, bf16[512,256]{1,0:T(8,128)(2,1)S(1)} %get-tuple-element.34.wide_ref, f32[5,8,128]{2,1,0:T(8,128)S(1)} %get-tuple-element.35.column_ref, ...), custom_call_target="tpu_custom_call" | custom-call | flops 600000000 | bytes 4000000 | tf_op jit(solution)/shard_map/down/pallas_call | solution.py:410
  13.6 0.0 collective-permute-done.2.got_ref
  13.7 0.3 %up.1 = (f32[72,128]{1,0:T(8,128)S(1)}, f32[72,128]{1,0:T(8,128)S(1)}, f32[72,128]{1,0:T(8,128)S(1)}, f32[72,128]{1,0:T(8,128)S(1)}, f32[2,8,128]{2,1,0:T(8,128)S(1)}) custom-call(f32[1,32,3,32,128]{4,3,2,1,0:T(8,128)S(1)} %get-tuple-element.38.coef_a, f32[1,33,8,128]{3,2,1,0:T(8,128)S(1)} %get-tuple-element.39.esum_a, ...), custom_call_target="tpu_custom_call" | custom-call | flops 4000000 | bytes 4000000 | tf_op jit(solution)/shard_map/up/pallas_call | solution.py:466
  14.0 0.8 %collective-permute-start.3 = (f32[72,128]{1,0:T(8,128)S(1)}, f32[72,128]{1,0:T(8,128)S(1)}, u32[]{:S(2)}, u32[]{:S(2)}) collective-permute-start(f32[72,128]{1,0:T(8,128)S(1)} %get-tuple-element.49), channel_id=1, source_target_pairs={{0,16},{16,0},{32,48},{48,32},{64,80},{80,64},{96,112},{112,96},{1... | collective-permute-start | bytes 110600 | tf_op jit(solution)/shard_map/ppermute | solution.py:660
  14.7 0.4 %collective-permute-start.4 = (f32[72,128]{1,0:T(8,128)S(1)}, f32[72,128]{1,0:T(8,128)S(1)}, u32[]{:S(2)}, u32[]{:S(2)}) collective-permute-start(f32[72,128]{1,0:T(8,128)S(1)} %get-tuple-element.50), channel_id=1, source_target_pairs={{0,112},{16,32},{32,16},{48,64},{64,48},{80,96},{96,80},{112,0},{1... | collective-permute-start | bytes 110600 | tf_op jit(solution)/shard_map/ppermute | solution.py:697
  15.1 3.2 %inner.1 = (f32[33,2,1024]{2,1,0:T(2,128)S(1)}, f32[2,72,128]{2,1,0:T(8,128)S(1)}) custom-call(bf16[16,32,1024]{2,1,0:T(8,128)(2,1)S(1)} %get-tuple-element.33.gas_ref, bf16[512,256]{1,0:T(8,128)(2,1)S(1)} %get-tuple-element.34.wide_ref, f32[5,8,128]{2,1,0:T(8,128)S(1)} %get-tuple-element.35.column_ref, f32[32,128]{1,0:T(8,128)S(1)} %get-tuple-element.36.solar_ref, ...), custom_call_target="tpu_custom_call" | custom-call | flops 2000000000 | bytes 4000000 | tf_op jit(solution)/shard_map/inner/pallas_call | solution.py:565
  18.4 0.0 collective-permute-done.3.near_got
  18.4 0.0 collective-permute-done.4.far_got
  18.4 1.1 %edge_side.1 = f32[33,2,1024]{2,1,0:T(2,128)} custom-call(f32[72,128]{1,0:T(8,128)S(1)} %collective-permute-done.3.near_got, f32[72,128]{1,0:T(8,128)S(1)} %collective-permute-done.4.far_got, f32[72,128]{1,0:T(8,128)S(1)} %get-tuple-element.51.first_ref, f32[72,128]{1,0:T(8,128)S(1)} %get-tuple-element.52.final_ref, ...), custom_call_target="tpu_custom_call" | custom-call | tf_op jit(solution)/shard_map/edge_side/pallas_call | solution.py:644
  (2 shorter events, 0.0 us)
Async XLA Ops:
  1.6 2.6 %collective-permute-start = (bf16[4,2,8,128]{3,2,1,0:T(8,128)(2,1)S(1)}, bf16[4,2,8,128]{3,2,1,0:T(8,128)(2,1)S(1)}, u32[]{:S(2)}, u32[]{:S(2)}) collective-permute-start(bf16[4,2,8,128]{3,2,1,0:T(8,128)(2,1)S(1)} %get-tuple-element.41), channel_id=1, source_target_pairs={{0,16},{16,0},{32,48},{48,32},{64,80},{80,64},{96,112},{112,96},{1... | collective-permute-start | bytes 49160 | tf_op jit(solution)/shard_map/ppermute | solution.py:660
  4.2 3.6 %collective-permute-start.1 = (bf16[2,2,8,128]{3,2,1,0:T(8,128)(2,1)S(1)}, bf16[2,2,8,128]{3,2,1,0:T(8,128)(2,1)S(1)}, u32[]{:S(2)}, u32[]{:S(2)}) collective-permute-start(bf16[2,2,8,128]{3,2,1,0:T(8,128)(2,1)S(1)} %get-tuple-element.46), channel_id=1, source_target_pairs={{0,32},{16,48},{32,0},{48,16},{64,96},{80,112},{96,64},{112,80},{1... | collective-permute-start | bytes 24584 | tf_op jit(solution)/shard_map/ppermute | solution.py:660
  7.8 5.8 %collective-permute-start.2 = (bf16[1,2,8,128]{3,2,1,0:T(8,128)(2,1)S(1)}, bf16[1,2,8,128]{3,2,1,0:T(8,128)(2,1)S(1)}, u32[]{:S(2)}, u32[]{:S(2)}) collective-permute-start(bf16[1,2,8,128]{3,2,1,0:T(8,128)(2,1)S(1)} %get-tuple-element.48), channel_id=1, source_target_pairs={{0,64},{16,80},{32,96},{48,112},{64,0},{80,16},{96,32},{112,48},{1... | collective-permute-start | bytes 12296 | tf_op jit(solution)/shard_map/ppermute | solution.py:660
  14.0 4.4 %collective-permute-start.3 = (f32[72,128]{1,0:T(8,128)S(1)}, f32[72,128]{1,0:T(8,128)S(1)}, u32[]{:S(2)}, u32[]{:S(2)}) collective-permute-start(f32[72,128]{1,0:T(8,128)S(1)} %get-tuple-element.49), channel_id=1, source_target_pairs={{0,16},{16,0},{32,48},{48,32},{64,80},{80,64},{96,112},{112,96},{1... | collective-permute-start | bytes 110600 | tf_op jit(solution)/shard_map/ppermute | solution.py:660
  14.7 3.6 %collective-permute-start.4 = (f32[72,128]{1,0:T(8,128)S(1)}, f32[72,128]{1,0:T(8,128)S(1)}, u32[]{:S(2)}, u32[]{:S(2)}) collective-permute-start(f32[72,128]{1,0:T(8,128)S(1)} %get-tuple-element.50), channel_id=1, source_target_pairs={{0,112},{16,32},{32,16},{48,64},{64,48},{80,96},{96,80},{112,0},{1... | collective-permute-start | bytes 110600 | tf_op jit(solution)/shard_map/ppermute | solution.py:697

commit v2 on v1

--- a/solution.py
+++ b/solution.py
@@ -46,10 +46,6 @@
 
 def sum_tiles(x):
     return (x[0:8] + x[8:16]) + (x[16:24] + x[24:32])
-
-
-def block_lanes(block):
-    return pl.ds(pl.multiple_of(block * CB, CB), CB)
 
 
 def place_albedo(parent_ref, area_ref, albedo_ref, mine):
@@ -129,11 +125,26 @@
 
 def column_constants(cosine, lit, column_ref):
     back = 0.5 * (1.0 - ASYM * cosine)
+    rising = back * SCATTER
     column_ref[0] = -TAU_SCALE / cosine
-    column_ref[1] = back * SCATTER
-    column_ref[2] = (1.0 - back) * SCATTER
+    column_ref[1] = (1.0 - back) / back
+    column_ref[2] = 1.0 / rising
     column_ref[3] = cosine
-    column_ref[4] = lit
+    column_ref[4] = lit * rising
+
+
+WINDOWS = ((0,), (NB - 1, 1), (2, 3, 4, 5))
+LATE = 6
+GAS = (F, LEV, CB)
+
+
+def gas_copies(gas_hbm, gas_ref, blocks, sems):
+    return [
+        pltpu.make_async_copy(
+            gas_hbm.at[:, :, pl.ds(block * CB, CB)], gas_ref.at[i], sems.at[i]
+        )
+        for i, block in enumerate(blocks)
+    ]
 
 
 def surface_kernel(
@@ -144,8 +155,6 @@
     cosine_hbm,
     lit_hbm,
     solar_hbm,
-    neighbour_hbm,
-    side_hbm,
     gas_hbm,
     send_ref,
     keep_ref,
@@ -153,8 +162,6 @@
     wide_ref,
     column_ref,
     solar_ref,
-    neighbour_ref,
-    side_ref,
     parent_ref,
     area_ref,
     albedo_ref,
@@ -173,17 +180,15 @@
         (cosine_hbm, cosine_ref),
         (lit_hbm, lit_ref),
         (solar_hbm, sun_ref),
-        (neighbour_hbm, neighbour_ref),
-        (side_hbm, side_ref),
-        (gas_hbm, gas_ref),
     )
     copies = [
         pltpu.make_async_copy(source, target, sems.at[i])
         for i, (source, target) in enumerate(pairs)
     ]
+    later = gas_copies(gas_hbm, gas_ref, WINDOWS[0], sems.at[pl.ds(8, 1)])
+    for copy in copies + later:
+        copy.start()
     for copy in copies:
-        copy.start()
-    for copy in copies[:8]:
         copy.wait()
     mine = lax.axis_index("blk")
     placed = place_albedo(parent_ref, area_ref, albedo_ref, mine)
@@ -197,7 +202,7 @@
     col = lax.broadcasted_iota(jnp.int32, (G, G), 1)
     sun = jnp.sum(jnp.where(row == col, sun_ref[...], 0.0), axis=1, keepdims=True)
     solar_ref[...] = jnp.broadcast_to(sun, (G, CB))
-    for copy in copies[8:]:
+    for copy in later:
         copy.wait()
 
 
@@ -209,23 +214,19 @@
     cos_zenith,
     daylit,
     solar_weight,
-    neighbours,
-    side_weight,
     gas_state,
 ):
     return pl.pallas_call(
         surface_kernel,
-        in_specs=[IN_HBM] * 10,
-        out_specs=[IN_VMEM] * 8,
+        in_specs=[IN_HBM] * 8,
+        out_specs=[IN_VMEM] * 6,
         out_shape=[
             shape((NBLK // 2, 2, NB, CB), BF16),
             shape((NBLK // 2, 2, NB, CB), BF16),
-            shape((F, LEV, COLS), BF16),
+            shape((len(WINDOWS[0]),) + GAS, BF16),
             shape((2 * G * STEP, 2 * F * STEP), BF16),
             shape((5, NB, CB)),
             shape((G, CB)),
-            shape((3, COLS), jnp.int32),
-            shape((3, COLS)),
         ],
         scratch_shapes=[
             pltpu.VMEM((FINE_BLOCKS, CB), jnp.int32),
@@ -235,7 +236,7 @@
             pltpu.VMEM((NB, CB), BF16),
             pltpu.VMEM((NB, CB), jnp.int32),
             pltpu.VMEM((1, G), F32),
-            pltpu.SemaphoreType.DMA((11,)),
+            pltpu.SemaphoreType.DMA((9,)),
         ],
         compiler_params=params(4),
         name="surface",
@@ -250,8 +251,6 @@
                 cos_zenith.reshape(NB, CB),
                 daylit.reshape(NB, CB),
                 solar_weight.reshape(1, G),
-                neighbours,
-                side_weight,
                 gas_state,
             )
         ]
@@ -295,10 +294,10 @@
     return e_dir, gamma_two, even + odd, even - odd, gamma_two * lost, transmit
 
 
-def mix_all(gas_ref, lanes, wide_ref):
+def mix_all(gas_ref, wide_ref):
     products = []
     for step in range(LEV // STEP):
-        gas = gas_ref[:, step * STEP : (step + 1) * STEP, lanes].reshape(F * STEP, CB)
+        gas = gas_ref[:, step * STEP : (step + 1) * STEP, :].reshape(F * STEP, CB)
         products.append(
             jnp.dot(
                 wide_ref[...],
@@ -310,9 +309,9 @@
 
 
 def eliminate(block, gas_ref, wide_ref, column_ref, solar_ref, coef_ref, esum_ref, state_ref):
-    products = mix_all(gas_ref, block_lanes(block), wide_ref)
-    slant_rate, rising, falling, cosine = [
-        column_ref[i, pl.ds(block, 1), :] for i in range(4)
+    products = mix_all(gas_ref, wide_ref)
+    slant_rate, falling, scale, cosine = [
+        column_ref[i, block : block + 1, :] for i in range(4)
     ]
     direct = solar_ref[...] * cosine
     above = jnp.zeros((G, CB), F32)
@@ -323,22 +322,21 @@
         e_dir, gamma_two, divisor, mirrored, reflect, transmit = layer_terms(
             mix[at : at + G], mix[at + G : at + 2 * G], slant_rate
         )
-        esum_ref[l] = sum_tiles(direct + source)
+        esum_ref[l] = sum_tiles(direct) * scale + sum_tiles(source)
         below = direct * e_dir
         scattered = gamma_two * (direct - below)
-        up_source = scattered * rising
         inverse = pl.reciprocal(divisor - above * reflect, approx=False)
-        incident = (source + above * up_source) * inverse
+        incident = (source + above * scattered) * inverse
         coef_ref[l, 0] = above
         coef_ref[l, 1] = transmit * inverse
-        coef_ref[l, 2] = up_source + reflect * incident
+        coef_ref[l, 2] = scattered + reflect * incident
         source = scattered * falling + transmit * incident
         above = (reflect + above * mirrored) * inverse
         direct = below
-    esum_ref[LEV] = sum_tiles(direct + source)
+    esum_ref[LEV] = sum_tiles(direct) * scale + sum_tiles(source)
     state_ref[0] = above
     state_ref[1] = source
-    state_ref[2] = direct
+    state_ref[2] = direct * scale
 
 
 def add_sublanes(rows):
@@ -387,13 +385,26 @@
 STATE = (3, G, CB)
 
 
-def down_kernel(blocks):
-    def kernel(gas_ref, wide_ref, column_ref, solar_ref, after_ref, coef_ref, esum_ref, state_ref):
-        del after_ref
+def down_kernel(blocks, following, with_sides):
+    def kernel(*refs):
+        gas_ref, wide_ref, column_ref, solar_ref, _, gas_hbm = refs[:6]
+        refs = refs[6:]
+        pairs = ()
+        if with_sides:
+            pairs, refs = refs[:2], refs[2:]
+        coef_ref, esum_ref, state_ref, next_ref = refs[:4]
+        sems = refs[-1]
+        copies = gas_copies(gas_hbm, next_ref, following, sems)
+        for i, source in enumerate(pairs):
+            copies.append(
+                pltpu.make_async_copy(source, refs[4 + i], sems.at[len(following) + i])
+            )
+        for copy in copies:
+            copy.start()
         for i, block in enumerate(blocks):
             eliminate(
                 block,
-                gas_ref,
+                gas_ref.at[i],
                 wide_ref,
                 column_ref,
                 solar_ref,
@@ -401,27 +412,29 @@
                 esum_ref.at[i],
                 state_ref.at[i],
             )
+        for copy in copies:
+            copy.wait()
 
     return kernel
 
 
-def down(blocks, gas, wide, column, solar, after):
+def down(blocks, following, gas, wide, column, solar, after, gas_state, sides=()):
     count = len(blocks)
+    pinned = [pltpu.with_memory_space_constraint(x, pltpu.HBM) for x in (gas_state, *sides)]
     return pl.pallas_call(
-        down_kernel(blocks),
-        in_specs=[IN_VMEM] * 4 + [UNREAD],
-        out_specs=[IN_VMEM] * 3,
-        out_shape=[shape((count,) + x) for x in (COEF, ESUM, STATE)],
+        down_kernel(blocks, following, bool(sides)),
+        in_specs=[IN_VMEM] * 4 + [UNREAD] + [IN_HBM] * len(pinned),
+        out_specs=[IN_VMEM] * (4 + len(sides)),
+        out_shape=[shape((count,) + x) for x in (COEF, ESUM, STATE)]
+        + [shape((len(following),) + GAS, BF16)]
+        + [shape(x.shape, x.dtype) for x in sides],
+        scratch_shapes=[pltpu.SemaphoreType.DMA((len(following) + len(sides),))],
         compiler_params=params(24),
         cost_estimate=pl.CostEstimate(
             flops=200000000 * count, transcendentals=0, bytes_accessed=4000000
         ),
         name="down",
-    )(gas, wide, column, solar, after)
-
-
-WINDOWS = ((0,), (NB - 1, 1), (2, 3, 4))
-LATE = (5, 6)
+    )(gas, wide, column, solar, after, *pinned)
 
 
 def ground(albedo_ref, column_ref, block):
@@ -474,28 +487,60 @@
     )(*parts[0], *parts[1], keep, got, column)
 
 
-def correct(block, before, own, after, neighbour_ref, side_ref, out_ref):
+def neighbour_rows(block, neighbour_ref, side_ref):
     lanes = slice(block * CB, (block + 1) * CB)
-    at_lane, firsts, lasts, weights = [], [], [], []
+    at_lane, places, weights = [], [], []
     for k in range(3):
         at = jnp.broadcast_to(neighbour_ref[k : k + 1, lanes], (8, CB))
-        place = ((at >> 7) - block + 1) & (NB - 1)
+        places.append(((at >> 7) - block + 1) & (NB - 1))
         at_lane.append(at & (CB - 1))
-        firsts.append(place == 0)
-        lasts.append(place == 2)
         weights.append(jnp.broadcast_to(side_ref[k : k + 1, lanes], (8, CB)))
-    for row in range(0, ROWS, 8):
-        rows = [part(row) for part in (before, own, after)]
-        total = rows[1]
-        for k in range(3):
-            low, mid, high = [
-                jnp.take_along_axis(x, at_lane[k], axis=1, mode="promise_in_bounds")
-                for x in rows
-            ]
-            beside = jnp.where(firsts[k], low, jnp.where(lasts[k], high, mid))
-            total = total + weights[k] * (beside - rows[1])
+    return at_lane, places, weights
+
+
+def pick(x, at_lane):
+    return jnp.take_along_axis(x, at_lane, axis=1, mode="promise_in_bounds")
+
+
+def correct(block, before, own, after, neighbour_ref, side_ref, put):
+    at_lane, places, weights = neighbour_rows(block, neighbour_ref, side_ref)
+    for k in range(3):
+        for code, part in ((0, before), (2, after)):
+            if part is None:
+                weights[k] = jnp.where(places[k] == code, 0.0, weights[k])
+    totals = {row: own(row) for row in range(0, ROWS, 8)}
+    for k in range(3):
+        for row in totals:
+            here = own(row)
+            beside = pick(here, at_lane[k])
+            for code, part in ((0, before), (2, after)):
+                if part is not None:
+                    beside = jnp.where(places[k] == code, pick(part(row), at_lane[k]), beside)
+            totals[row] = totals[row] + weights[k] * (beside - here)
+    for row, total in totals.items():
+        put(row, total)
+
+
+def correct_rest(block, code, outer, own, partial, neighbour_ref, side_ref, put):
+    at_lane, places, weights = neighbour_rows(block, neighbour_ref, side_ref)
+    weights = [jnp.where(places[k] == code, weights[k], 0.0) for k in range(3)]
+    totals = {row: partial(row) for row in range(0, ROWS, 8)}
+    for k in range(3):
+        for row in totals:
+            beside = pick(outer(row), at_lane[k])
+            totals[row] = totals[row] + weights[k] * (beside - own(row))
+    for row, total in totals.items():
+        put(row, total)
+
+
+def put_levels(out_ref, block):
+    lanes = slice(block * CB, (block + 1) * CB)
+
+    def put(row, total):
         for l in range(row // 2, min(row // 2 + 4, LEV + 1)):
             out_ref[l, :, lanes] = total[2 * l - row : 2 * l - row + 2]
+
+    return put
 
 
 def rows_of(ref):
@@ -519,59 +564,57 @@
     neighbour_ref,
     side_ref,
     out_ref,
-    near_ref,
+    partial_ref,
     coef_ref,
     esum_ref,
     state_ref,
     flux_ref,
 ):
-    kept = {1: (coef_b.at[1], esum_b.at[1], state_b.at[1])}
+    kept = {
+        1: (coef_b.at[1], esum_b.at[1], state_b.at[1]),
+        LATE: (coef_ref, esum_ref, state_ref),
+    }
     for i, n in enumerate(WINDOWS[2]):
         kept[n] = coef_c.at[i], esum_c.at[i], state_c.at[i]
-    for i, n in enumerate(LATE):
-        kept[n] = coef_ref.at[i], esum_ref.at[i], state_ref.at[i]
-    flux = {0: first_ref, 1: near_ref.at[0], NB - 2: near_ref.at[1], NB - 1: final_ref}
-    for n in range(2, NB - 2):
-        flux[n] = flux_ref.at[n - 2]
-
-    def start(n):
-        eliminate(n, gas_ref, wide_ref, column_ref, solar_ref, *kept[n])
+    flux = {0: first_ref, NB - 1: final_ref}
+    for n in range(1, NB - 1):
+        flux[n] = flux_ref.at[n - 1]
 
     def finish(n):
         substitute(*kept[n], *ground(albedo_ref, column_ref, n), flux[n])
 
     def side(n):
-        before, own, after = [rows_of(flux[n + i]) for i in (-1, 0, 1)]
-        correct(n, before, own, after, neighbour_ref, side_ref, out_ref)
-
-    start(5)
-    finish(1)
-    finish(2)
-    side(1)
-    start(6)
-    finish(3)
-    finish(4)
-    side(2)
-    side(3)
-    finish(5)
-    finish(6)
-    side(4)
-    side(5)
-    side(6)
+        before, own, after = [
+            rows_of(flux[n + i]) if n + i in flux else None for i in (-1, 0, 1)
+        ]
+        if n in (0, NB - 1):
+            partial = partial_ref.at[n // (NB - 1)]
+
+            def put(row, total):
+                partial[row : row + 8, :] = total
+
+        else:
+            put = put_levels(out_ref, n)
+        correct(n, before, own, after, neighbour_ref, side_ref, put)
+
+    eliminate(LATE, gas_ref.at[0], wide_ref, column_ref, solar_ref, *kept[LATE])
+    for n in (1, 2, 3, LATE, 5, 4):
+        finish(n)
+    for n in range(NB):
+        side(n)
 
 
 def inner(gas, wide, column, solar, albedo, first, final, parts, neighbours, side_weight):
-    count = len(LATE)
     return pl.pallas_call(
         inner_kernel,
         in_specs=[IN_VMEM] * 15,
         out_specs=[IN_VMEM] * 2,
         out_shape=[shape((LEV + 1, 2, COLS)), shape((2, ROWS, CB))],
         scratch_shapes=[
-            pltpu.VMEM((count,) + COEF, F32),
-            pltpu.VMEM((count,) + ESUM, F32),
-            pltpu.VMEM((count,) + STATE, F32),
-            pltpu.VMEM((NB - 4, ROWS, CB), F32),
+            pltpu.VMEM(COEF, F32),
+            pltpu.VMEM(ESUM, F32),
+            pltpu.VMEM(STATE, F32),
+            pltpu.VMEM((NB - 2, ROWS, CB), F32),
         ],
         compiler_params=params(24),
         cost_estimate=pl.CostEstimate(
@@ -598,7 +641,7 @@
     far_got,
     first_ref,
     final_ref,
-    inside_ref,
+    partial_ref,
     neighbour_ref,
     side_ref,
     full_ref,
@@ -615,24 +658,21 @@
     copies[0].start()
     even = lax.axis_index("blk") % 2 == 0
     near, far = rows_of(near_got), rows_of(far_got)
-    correct(
-        0,
-        lambda row: jnp.where(even, far(row), near(row)),
-        rows_of(first_ref),
-        rows_of(inside_ref.at[0]),
-        neighbour_ref,
-        side_ref,
-        edge_ref,
-    )
-    correct(
-        NB - 1,
-        rows_of(inside_ref.at[1]),
-        rows_of(final_ref),
-        lambda row: jnp.where(even, near(row), far(row)),
-        neighbour_ref,
-        side_ref,
-        edge_ref,
-    )
+    edges = (
+        (0, 0, lambda row: jnp.where(even, far(row), near(row)), first_ref),
+        (NB - 1, 2, lambda row: jnp.where(even, near(row), far(row)), final_ref),
+    )
+    for i, (block, code, outer, own) in enumerate(edges):
+        correct_rest(
+            block,
+            code,
+            outer,
+            rows_of(own),
+            rows_of(partial_ref.at[i]),
+            neighbour_ref,
+            side_ref,
+            put_levels(edge_ref, block),
+        )
     for i, block in enumerate((0, NB - 1)):
         copies.append(copy(edge_ref, pl.ds(block * CB, CB), 1 + i))
         copies[-1].start()
@@ -640,7 +680,7 @@
         started.wait()
 
 
-def edge_side(near_got, far_got, first, final, inside, neighbours, side_weight, full):
+def edge_side(near_got, far_got, first, final, partial, neighbours, side_weight, full):
     return pl.pallas_call(
         edge_side_kernel,
         in_specs=[IN_VMEM] * 8,
@@ -652,7 +692,7 @@
         ],
         compiler_params=params(4),
         name="edge_side",
-    )(near_got, far_got, first, final, inside, neighbours, side_weight, full)
+    )(near_got, far_got, first, final, partial, neighbours, side_weight, full)
 
 
 def exchange(x, bit):
@@ -672,7 +712,7 @@
     neighbours,
     side_weight,
 ):
-    send, keep, gas, wide, column, solar, beside, weights = surface(
+    send, keep, gas, wide, column, solar = surface(
         parent_of,
         fine_area,
         fine_albedo,
@@ -680,25 +720,30 @@
         cos_zenith,
         daylit,
         solar_weight,
-        neighbours,
-        side_weight,
         gas_state,
     )
     parts = []
     for i, blocks in enumerate(WINDOWS):
         got = exchange(send, 1 << i)
-        parts.append(down(blocks, gas, wide, column, solar, keep))
+        following = WINDOWS[i + 1] if i < 2 else (LATE,)
+        sides = (neighbours, side_weight) if i == 1 else ()
+        coef, esum, state, gas, *rest = down(
+            blocks, following, gas, wide, column, solar, keep, gas_state, sides
+        )
+        parts.append((coef, esum, state))
+        if i == 1:
+            beside, weights = rest
         if i < 2:
-            send, keep = merge(keep, got, parts[-1][2])
+            send, keep = merge(keep, got, state)
     first, final, near, far, albedo = up(parts, keep, got, column)
     near_got = exchange(near, 1)
     count = lax.axis_size("blk")
     beyond = [(i, (i + (1 if i % 2 else -1)) % count) for i in range(count)]
     far_got = lax.ppermute(far, "blk", beyond)
-    full, inside = inner(
+    full, partial = inner(
         gas, wide, column, solar, albedo, first, final, parts, beside, weights
     )
-    done = edge_side(near_got, far_got, first, final, inside, beside, weights, full)
+    done = edge_side(near_got, far_got, first, final, partial, beside, weights, full)
     return done.transpose(1, 0, 2)
 
 

time: 19.8 us -> 20.4 us (1.030)
  waiting for transfers between devices: 0.01 us -> 0.78 us
    pallas_call x4, Pallas kernels: 7.91 us -> 9.26 us  [the longest x3 7.75 us: down(): pl.pallas_call(down_kernel(blocks, following, bool(sides)), in_specs=[IN_...]
    pallas_call x1, Pallas kernels: 3.24 us -> 2.29 us  [inner(): pl.pallas_call(inner_kernel, in_specs=[IN_VMEM] * 15, out_specs=[IN_VMEM]...]
    ppermute x1, waiting for transfers between devices: 0.01 us -> 0.77 us  [local(): far_got = lax.ppermute(far, 'blk', beyond)]
    pallas_call x1, Pallas kernels: 1.08 us -> 0.81 us  [edge_side(): pl.pallas_call(edge_side_kernel, in_specs=[IN_VMEM] * 8, out_specs=IN_HBM...]
  transfers between devices with their start and end apart: 5 -> 5, of which waited for: 0 -> 1; matrix products, arithmetic and copies ran while one was open for 0% -> 0% of each run, Pallas kernels for 49% -> 50%
where the time goes in v2:
time: 20.4 us; the launch traced here: 20.2 us
  Pallas kernels  12.7 us (62%)
  starting transfers between devices  6.63 us (32%)
  waiting for transfers between devices  0.78 us (4%)
    pallas_call x3, Pallas kernels, down(): pl.pallas_call(down_kernel(blocks, following, bool(sides)), in_specs=[IN_...  7.75 us
    ppermute x4, starting transfers between devices, exchange(): return lax.ppermute(x, 'blk', [(i, i ^ bit) for i in range(count)])  6.32 us
    pallas_call x1, Pallas kernels, inner(): pl.pallas_call(inner_kernel, in_specs=[IN_VMEM] * 15, out_specs=[IN_VMEM]...  2.29 us
    pallas_call x1, Pallas kernels, surface(): pl.pallas_call(surface_kernel, in_specs=[IN_HBM] * 8, out_specs=[IN_VMEM]...  1.51 us
    pallas_call x1, Pallas kernels, edge_side(): pl.pallas_call(edge_side_kernel, in_specs=[IN_VMEM] * 8, out_specs=IN_HBM...  0.81 us
    ppermute x1, waiting for transfers between devices, local(): far_got = lax.ppermute(far, 'blk', beyond)  0.77 us
  transfers between devices with their start and end apart: 5, of which 1 were waited for; matrix products, arithmetic and copies ran while one was open for 0% of the time, Pallas kernels for 50%

profile of v2, /device:TPU:1, one launch (start us, length us, event | category | flops | bytes accessed | tf_op | source)
XLA Modules:
  0.0 20.2 jit_solution(7119437795618726152)
XLA Ops:
  0.0 1.5 %surface.1 = (bf16[4,2,8,128]{3,2,1,0:T(8,128)(2,1)S(1)}, bf16[4,2,8,128]{3,2,1,0:T(8,128)(2,1)S(1)}, bf16[1,16,32,128]{3,2,1,0:T(8,128)(2,1)S(1)}, bf16[512,256...) custom-call(s32[32,128]{1,0:T(8,128)} %bitcast.11, f32[32,128]{1,0:T(8,128)} %bitcast.12, ...), custom_call_target="tpu_custom_call" | custom-call | tf_op jit(solution)/shard_map/surface/pallas_call | solution.py:219
  1.5 1.5 %collective-permute-start = (bf16[4,2,8,128]{3,2,1,0:T(8,128)(2,1)S(1)}, bf16[4,2,8,128]{3,2,1,0:T(8,128)(2,1)S(1)}, u32[]{:S(2)}, u32[]{:S(2)}) collective-permute-start(bf16[4,2,8,128]{3,2,1,0:T(8,128)(2,1)S(1)} %get-tuple-element.45), channel_id=1, source_target_pairs={{0,16},{16,0},{32,48},{48,32},{64,80},{80,64},{96,112},{112,96},{1... | collective-permute-start | bytes 49160 | tf_op jit(solution)/shard_map/ppermute | solution.py:700
  3.0 1.3 %down.3 = (f32[1,32,3,32,128]{4,3,2,1,0:T(8,128)S(1)}, f32[1,33,8,128]{3,2,1,0:T(8,128)S(1)}, f32[1,3,32,128]{3,2,1,0:T(8,128)S(1)}, bf16[2,16,32,128]{3,2,1,0:T(8,128)(2,1)S(1)}) custom-call(bf16[1,16,32,128]{3,2,1,0:T(8,128)(2,1)S(1)} %get-tuple-element.36.refs_0_, bf16[512,256]{1,0:T(8,128)(2,1)S(1)} %get-tuple-element.37.refs_1_.wide_ref, ...), custom_call_target="tpu_custom_call" | custom-call | flops 200000000 | bytes 4000000 | tf_op jit(solution)/shard_map/down/pallas_call | solution.py:424
  4.3 0.0 collective-permute-done.got_ref
  4.4 1.5 %collective-permute-start.1 = (bf16[2,2,8,128]{3,2,1,0:T(8,128)(2,1)S(1)}, bf16[2,2,8,128]{3,2,1,0:T(8,128)(2,1)S(1)}, u32[]{:S(2)}, u32[]{:S(2)}) collective-permute-start(bf16[2,2,8,128]{3,2,1,0:T(8,128)(2,1)S(1)} %get-tuple-element.50), channel_id=1, source_target_pairs={{0,32},{16,48},{32,0},{48,16},{64,96},{80,112},{96,64},{112,80},{1... | collective-permute-start | bytes 24584 | tf_op jit(solution)/shard_map/ppermute | solution.py:700
  5.8 2.3 %down.4 = (f32[2,32,3,32,128]{4,3,2,1,0:T(8,128)S(1)}, f32[2,33,8,128]{3,2,1,0:T(8,128)S(1)}, f32[2,3,32,128]{3,2,1,0:T(8,128)S(1)}, bf16[4,16,32,128]{3,2,1,0:T...) custom-call(bf16[2,16,32,128]{3,2,1,0:T(8,128)(2,1)S(1)} %get-tuple-element.44.refs_0_, ...), custom_call_target="tpu_custom_call" | custom-call | flops 400000000 | bytes 4000000 | tf_op jit(solution)/shard_map/down/pallas_call | solution.py:424
  8.2 0.0 collective-permute-done.1.got_ref
  8.2 2.7 %collective-permute-start.2 = (bf16[1,2,8,128]{3,2,1,0:T(8,128)(2,1)S(1)}, bf16[1,2,8,128]{3,2,1,0:T(8,128)(2,1)S(1)}, u32[]{:S(2)}, u32[]{:S(2)}) collective-permute-start(bf16[1,2,8,128]{3,2,1,0:T(8,128)(2,1)S(1)} %get-tuple-element.52), channel_id=1, source_target_pairs={{0,64},{16,80},{32,96},{48,112},{64,0},{80,16},{96,32},{112,48},{1... | collective-permute-start | bytes 12296 | tf_op jit(solution)/shard_map/ppermute | solution.py:700
  10.9 4.1 %down.5 = (f32[4,32,3,32,128]{4,3,2,1,0:T(8,128)S(1)}, f32[4,33,8,128]{3,2,1,0:T(8,128)S(1)}, f32[4,3,32,128]{3,2,1,0:T(8,128)S(1)}, bf16[1,16,32,128]{3,2,1,0:T(8,128)(2,1)S(1)}) custom-call(bf16[4,16,32,128]{3,2,1,0:T(8,128)(2,1)S(1)} %get-tuple-element.57.refs_0_, bf16[512,256]{1,0:T(8,128)(2,1)S(1)} %get-tuple-element.37.refs_1_.wide_ref, ...), custom_call_target="tpu_custom_call" | custom-call | flops 800000000 | bytes 4000000 | tf_op jit(solution)/shard_map/down/pallas_call | solution.py:424
  15.0 0.0 collective-permute-done.2.got_ref
  15.0 0.3 %up.1 = (f32[72,128]{1,0:T(8,128)S(1)}, f32[72,128]{1,0:T(8,128)S(1)}, f32[72,128]{1,0:T(8,128)S(1)}, f32[72,128]{1,0:T(8,128)S(1)}, f32[2,8,128]{2,1,0:T(8,128)S(1)}) custom-call(f32[1,32,3,32,128]{4,3,2,1,0:T(8,128)S(1)} %get-tuple-element.41.coef_a, f32[1,33,8,128]{3,2,1,0:T(8,128)S(1)} %get-tuple-element.42.esum_a, ...), custom_call_target="tpu_custom_call" | custom-call | flops 4000000 | bytes 4000000 | tf_op jit(solution)/shard_map/up/pallas_call | solution.py:479
  15.3 0.7 %collective-permute-start.3 = (f32[72,128]{1,0:T(8,128)S(1)}, f32[72,128]{1,0:T(8,128)S(1)}, u32[]{:S(2)}, u32[]{:S(2)}) collective-permute-start(f32[72,128]{1,0:T(8,128)S(1)} %get-tuple-element.53), channel_id=1, source_target_pairs={{0,16},{16,0},{32,48},{48,32},{64,80},{80,64},{96,112},{112,96},{1... | collective-permute-start | bytes 110600 | tf_op jit(solution)/shard_map/ppermute | solution.py:700
  16.0 0.3 %collective-permute-start.4 = (f32[72,128]{1,0:T(8,128)S(1)}, f32[72,128]{1,0:T(8,128)S(1)}, u32[]{:S(2)}, u32[]{:S(2)}) collective-permute-start(f32[72,128]{1,0:T(8,128)S(1)} %get-tuple-element.54), channel_id=1, source_target_pairs={{0,112},{16,32},{32,16},{48,64},{64,48},{80,96},{96,80},{112,0},{1... | collective-permute-start | bytes 110600 | tf_op jit(solution)/shard_map/ppermute | solution.py:742
  16.3 2.3 %inner.1 = (f32[33,2,1024]{2,1,0:T(2,128)S(1)}, f32[2,72,128]{2,1,0:T(8,128)S(1)}) custom-call(bf16[1,16,32,128]{3,2,1,0:T(8,128)(2,1)S(1)} %get-tuple-element.58.gas_ref, bf16[512,256]{1,0:T(8,128)(2,1)S(1)} %get-tuple-element.37.refs_1_.wide_ref, f32[5,8,128]{2,1,0:T(8,128)S(1)} %get-tuple-element.38.refs_2_.column_ref, ...), custom_call_target="tpu_custom_call" | custom-call | flops 2000000000 | bytes 4000000 | tf_op jit(solution)/shard_map/inner/pallas_call | solution.py:608
  18.6 0.0 collective-permute-done.3.near_got
  18.6 0.8 %collective-permute-done.4.far_got = f32[72,128]{1,0:T(8,128)S(1)} collective-permute-done((f32[72,128]{1,0:T(8,128)S(1)}, f32[72,128]{1,0:T(8,128)S(1)}, u32[]{:S(2)}, u32[]{:S(2)}) %collective-permute-start.4) | collective-permute-done | bytes 36896 | tf_op jit(solution)/shard_map/ppermute | solution.py:742
  19.4 0.8 %edge_side.1 = f32[33,2,1024]{2,1,0:T(2,128)} custom-call(f32[72,128]{1,0:T(8,128)S(1)} %collective-permute-done.3.near_got, f32[72,128]{1,0:T(8,128)S(1)} %collective-permute-done.4.far_got, f32[72,128]{1,0:T(8,128)S(1)} %get-tuple-element.55.first_ref, f32[72,128]{1,0:T(8,128)S(1)} %get-tuple-element.56.final_ref, ...), custom_call_target="tpu_custom_call" | custom-call | tf_op jit(solution)/shard_map/edge_side/pallas_call | solution.py:684
  (2 shorter events, 0.0 us)
Async XLA Ops:
  1.5 2.8 %collective-permute-start = (bf16[4,2,8,128]{3,2,1,0:T(8,128)(2,1)S(1)}, bf16[4,2,8,128]{3,2,1,0:T(8,128)(2,1)S(1)}, u32[]{:S(2)}, u32[]{:S(2)}) collective-permute-start(bf16[4,2,8,128]{3,2,1,0:T(8,128)(2,1)S(1)} %get-tuple-element.45), channel_id=1, source_target_pairs={{0,16},{16,0},{32,48},{48,32},{64,80},{80,64},{96,112},{112,96},{1... | collective-permute-start | bytes 49160 | tf_op jit(solution)/shard_map/ppermute | solution.py:700
  4.4 3.8 %collective-permute-start.1 = (bf16[2,2,8,128]{3,2,1,0:T(8,128)(2,1)S(1)}, bf16[2,2,8,128]{3,2,1,0:T(8,128)(2,1)S(1)}, u32[]{:S(2)}, u32[]{:S(2)}) collective-permute-start(bf16[2,2,8,128]{3,2,1,0:T(8,128)(2,1)S(1)} %get-tuple-element.50), channel_id=1, source_target_pairs={{0,32},{16,48},{32,0},{48,16},{64,96},{80,112},{96,64},{112,80},{1... | collective-permute-start | bytes 24584 | tf_op jit(solution)/shard_map/ppermute | solution.py:700
  8.2 6.8 %collective-permute-start.2 = (bf16[1,2,8,128]{3,2,1,0:T(8,128)(2,1)S(1)}, bf16[1,2,8,128]{3,2,1,0:T(8,128)(2,1)S(1)}, u32[]{:S(2)}, u32[]{:S(2)}) collective-permute-start(bf16[1,2,8,128]{3,2,1,0:T(8,128)(2,1)S(1)} %get-tuple-element.52), channel_id=1, source_target_pairs={{0,64},{16,80},{32,96},{48,112},{64,0},{80,16},{96,32},{112,48},{1... | collective-permute-start | bytes 12296 | tf_op jit(solution)/shard_map/ppermute | solution.py:700
  15.3 3.3 %collective-permute-start.3 = (f32[72,128]{1,0:T(8,128)S(1)}, f32[72,128]{1,0:T(8,128)S(1)}, u32[]{:S(2)}, u32[]{:S(2)}) collective-permute-start(f32[72,128]{1,0:T(8,128)S(1)} %get-tuple-element.53), channel_id=1, source_target_pairs={{0,16},{16,0},{32,48},{48,32},{64,80},{80,64},{96,112},{112,96},{1... | collective-permute-start | bytes 110600 | tf_op jit(solution)/shard_map/ppermute | solution.py:700
  16.0 3.4 %collective-permute-start.4 = (f32[72,128]{1,0:T(8,128)S(1)}, f32[72,128]{1,0:T(8,128)S(1)}, u32[]{:S(2)}, u32[]{:S(2)}) collective-permute-start(f32[72,128]{1,0:T(8,128)S(1)} %get-tuple-element.54), channel_id=1, source_target_pairs={{0,112},{16,32},{32,16},{48,64},{64,48},{80,96},{96,80},{112,0},{1... | collective-permute-start | bytes 110600 | tf_op jit(solution)/shard_map/ppermute | solution.py:742

commit v3 on v2

--- a/solution.py
+++ b/solution.py
@@ -133,18 +133,8 @@
     column_ref[4] = lit * rising
 
 
-WINDOWS = ((0,), (NB - 1, 1), (2, 3, 4, 5))
-LATE = 6
-GAS = (F, LEV, CB)
-
-
-def gas_copies(gas_hbm, gas_ref, blocks, sems):
-    return [
-        pltpu.make_async_copy(
-            gas_hbm.at[:, :, pl.ds(block * CB, CB)], gas_ref.at[i], sems.at[i]
-        )
-        for i, block in enumerate(blocks)
-    ]
+WINDOWS = ((0,), (NB - 1, 1), (2, 3, 4))
+LATE = (5, 6)
 
 
 def surface_kernel(
@@ -155,6 +145,8 @@
     cosine_hbm,
     lit_hbm,
     solar_hbm,
+    neighbour_hbm,
+    side_hbm,
     gas_hbm,
     send_ref,
     keep_ref,
@@ -162,6 +154,8 @@
     wide_ref,
     column_ref,
     solar_ref,
+    neighbour_ref,
+    side_ref,
     parent_ref,
     area_ref,
     albedo_ref,
@@ -180,15 +174,17 @@
         (cosine_hbm, cosine_ref),
         (lit_hbm, lit_ref),
         (solar_hbm, sun_ref),
+        (neighbour_hbm, neighbour_ref),
+        (side_hbm, side_ref),
+        (gas_hbm, gas_ref),
     )
     copies = [
         pltpu.make_async_copy(source, target, sems.at[i])
         for i, (source, target) in enumerate(pairs)
     ]
-    later = gas_copies(gas_hbm, gas_ref, WINDOWS[0], sems.at[pl.ds(8, 1)])
-    for copy in copies + later:
+    for copy in copies:
         copy.start()
-    for copy in copies:
+    for copy in copies[:8]:
         copy.wait()
     mine = lax.axis_index("blk")
     placed = place_albedo(parent_ref, area_ref, albedo_ref, mine)
@@ -202,7 +198,7 @@
     col = lax.broadcasted_iota(jnp.int32, (G, G), 1)
     sun = jnp.sum(jnp.where(row == col, sun_ref[...], 0.0), axis=1, keepdims=True)
     solar_ref[...] = jnp.broadcast_to(sun, (G, CB))
-    for copy in later:
+    for copy in copies[8:]:
         copy.wait()
 
 
@@ -214,19 +210,23 @@
     cos_zenith,
     daylit,
     solar_weight,
+    neighbours,
+    side_weight,
     gas_state,
 ):
     return pl.pallas_call(
         surface_kernel,
-        in_specs=[IN_HBM] * 8,
-        out_specs=[IN_VMEM] * 6,
+        in_specs=[IN_HBM] * 10,
+        out_specs=[IN_VMEM] * 8,
         out_shape=[
             shape((NBLK // 2, 2, NB, CB), BF16),
             shape((NBLK // 2, 2, NB, CB), BF16),
-            shape((len(WINDOWS[0]),) + GAS, BF16),
+            shape((F, LEV, COLS), BF16),
             shape((2 * G * STEP, 2 * F * STEP), BF16),
             shape((5, NB, CB)),
             shape((G, CB)),
+            shape((3, COLS), jnp.int32),
+            shape((3, COLS)),
         ],
         scratch_shapes=[
             pltpu.VMEM((FINE_BLOCKS, CB), jnp.int32),
@@ -236,7 +236,7 @@
             pltpu.VMEM((NB, CB), BF16),
             pltpu.VMEM((NB, CB), jnp.int32),
             pltpu.VMEM((1, G), F32),
-            pltpu.SemaphoreType.DMA((9,)),
+            pltpu.SemaphoreType.DMA((11,)),
         ],
         compiler_params=params(4),
         name="surface",
@@ -251,6 +251,8 @@
                 cos_zenith.reshape(NB, CB),
                 daylit.reshape(NB, CB),
                 solar_weight.reshape(1, G),
+                neighbours,
+                side_weight,
                 gas_state,
             )
         ]
@@ -294,10 +296,10 @@
     return e_dir, gamma_two, even + odd, even - odd, gamma_two * lost, transmit
 
 
-def mix_all(gas_ref, wide_ref):
+def mix_all(gas_ref, lanes, wide_ref):
     products = []
     for step in range(LEV // STEP):
-        gas = gas_ref[:, step * STEP : (step + 1) * STEP, :].reshape(F * STEP, CB)
+        gas = gas_ref[:, step * STEP : (step + 1) * STEP, lanes].reshape(F * STEP, CB)
         products.append(
             jnp.dot(
                 wide_ref[...],
@@ -309,7 +311,7 @@
 
 
 def eliminate(block, gas_ref, wide_ref, column_ref, solar_ref, coef_ref, esum_ref, state_ref):
-    products = mix_all(gas_ref, wide_ref)
+    products = mix_all(gas_ref, slice(block * CB, (block + 1) * CB), wide_ref)
     slant_rate, falling, scale, cosine = [
         column_ref[i, block : block + 1, :] for i in range(4)
     ]
@@ -385,26 +387,13 @@
 STATE = (3, G, CB)
 
 
-def down_kernel(blocks, following, with_sides):
-    def kernel(*refs):
-        gas_ref, wide_ref, column_ref, solar_ref, _, gas_hbm = refs[:6]
-        refs = refs[6:]
-        pairs = ()
-        if with_sides:
-            pairs, refs = refs[:2], refs[2:]
-        coef_ref, esum_ref, state_ref, next_ref = refs[:4]
-        sems = refs[-1]
-        copies = gas_copies(gas_hbm, next_ref, following, sems)
-        for i, source in enumerate(pairs):
-            copies.append(
-                pltpu.make_async_copy(source, refs[4 + i], sems.at[len(following) + i])
-            )
-        for copy in copies:
-            copy.start()
+def down_kernel(blocks):
+    def kernel(gas_ref, wide_ref, column_ref, solar_ref, after_ref, coef_ref, esum_ref, state_ref):
+        del after_ref
         for i, block in enumerate(blocks):
             eliminate(
                 block,
-                gas_ref.at[i],
+                gas_ref,
                 wide_ref,
                 column_ref,
                 solar_ref,
@@ -412,29 +401,23 @@
                 esum_ref.at[i],
                 state_ref.at[i],
             )
-        for copy in copies:
-            copy.wait()
 
     return kernel
 
 
-def down(blocks, following, gas, wide, column, solar, after, gas_state, sides=()):
+def down(blocks, gas, wide, column, solar, after):
     count = len(blocks)
-    pinned = [pltpu.with_memory_space_constraint(x, pltpu.HBM) for x in (gas_state, *sides)]
     return pl.pallas_call(
-        down_kernel(blocks, following, bool(sides)),
-        in_specs=[IN_VMEM] * 4 + [UNREAD] + [IN_HBM] * len(pinned),
-        out_specs=[IN_VMEM] * (4 + len(sides)),
-        out_shape=[shape((count,) + x) for x in (COEF, ESUM, STATE)]
-        + [shape((len(following),) + GAS, BF16)]
-        + [shape(x.shape, x.dtype) for x in sides],
-        scratch_shapes=[pltpu.SemaphoreType.DMA((len(following) + len(sides),))],
+        down_kernel(blocks),
+        in_specs=[IN_VMEM] * 4 + [UNREAD],
+        out_specs=[IN_VMEM] * 3,
+        out_shape=[shape((count,) + x) for x in (COEF, ESUM, STATE)],
         compiler_params=params(24),
         cost_estimate=pl.CostEstimate(
             flops=200000000 * count, transcendentals=0, bytes_accessed=4000000
         ),
         name="down",
-    )(gas, wide, column, solar, after, *pinned)
+    )(gas, wide, column, solar, after)
 
 
 def ground(albedo_ref, column_ref, block):
@@ -570,12 +553,11 @@
     state_ref,
     flux_ref,
 ):
-    kept = {
-        1: (coef_b.at[1], esum_b.at[1], state_b.at[1]),
-        LATE: (coef_ref, esum_ref, state_ref),
-    }
+    kept = {1: (coef_b.at[1], esum_b.at[1], state_b.at[1])}
     for i, n in enumerate(WINDOWS[2]):
         kept[n] = coef_c.at[i], esum_c.at[i], state_c.at[i]
+    for i, n in enumerate(LATE):
+        kept[n] = coef_ref.at[i], esum_ref.at[i], state_ref.at[i]
     flux = {0: first_ref, NB - 1: final_ref}
     for n in range(1, NB - 1):
         flux[n] = flux_ref.at[n - 1]
@@ -597,8 +579,9 @@
             put = put_levels(out_ref, n)
         correct(n, before, own, after, neighbour_ref, side_ref, put)
 
-    eliminate(LATE, gas_ref.at[0], wide_ref, column_ref, solar_ref, *kept[LATE])
-    for n in (1, 2, 3, LATE, 5, 4):
+    for n in LATE:
+        eliminate(n, gas_ref, wide_ref, column_ref, solar_ref, *kept[n])
+    for n in range(1, NB - 1):
         finish(n)
     for n in range(NB):
         side(n)
@@ -611,9 +594,9 @@
         out_specs=[IN_VMEM] * 2,
         out_shape=[shape((LEV + 1, 2, COLS)), shape((2, ROWS, CB))],
         scratch_shapes=[
-            pltpu.VMEM(COEF, F32),
-            pltpu.VMEM(ESUM, F32),
-            pltpu.VMEM(STATE, F32),
+            pltpu.VMEM((len(LATE),) + COEF, F32),
+            pltpu.VMEM((len(LATE),) + ESUM, F32),
+            pltpu.VMEM((len(LATE),) + STATE, F32),
             pltpu.VMEM((NB - 2, ROWS, CB), F32),
         ],
         compiler_params=params(24),
@@ -712,7 +695,7 @@
     neighbours,
     side_weight,
 ):
-    send, keep, gas, wide, column, solar = surface(
+    send, keep, gas, wide, column, solar, beside, weights = surface(
         parent_of,
         fine_area,
         fine_albedo,
@@ -720,25 +703,21 @@
         cos_zenith,
         daylit,
         solar_weight,
+        neighbours,
+        side_weight,
         gas_state,
     )
     parts = []
     for i, blocks in enumerate(WINDOWS):
         got = exchange(send, 1 << i)
-        following = WINDOWS[i + 1] if i < 2 else (LATE,)
-        sides = (neighbours, side_weight) if i == 1 else ()
-        coef, esum, state, gas, *rest = down(
-            blocks, following, gas, wide, column, solar, keep, gas_state, sides
-        )
-        parts.append((coef, esum, state))
-        if i == 1:
-            beside, weights = rest
+        parts.append(down(blocks, gas, wide, column, solar, keep))
         if i < 2:
-            send, keep = merge(keep, got, state)
+            send, keep = merge(keep, got, parts[-1][2])
     first, final, near, far, albedo = up(parts, keep, got, column)
     near_got = exchange(near, 1)
     count = lax.axis_size("blk")
-    beyond = [(i, (i + (1 if i % 2 else -1)) % count) for i in range(count)]
+    beyond = [(i, i + (1 if i % 2 else -1)) for i in range(1, count - 1)]
+    beyond += [(i, i) for i in (0, count - 1)]
     far_got = lax.ppermute(far, "blk", beyond)
     full, partial = inner(
         gas, wide, column, solar, albedo, first, final, parts, beside, weights

time: 20.4 us -> 21.1 us (1.034)
  starting transfers between devices: 6.63 us -> 8.71 us
  waiting for transfers between devices: 0.78 us -> 0.01 us
  Pallas kernels: 12.7 us -> 12.1 us
    ppermute x1, starting transfers between devices: 0.31 us -> 2.2 us  [local(): far_got = lax.ppermute(far, 'blk', beyond)]
    pallas_call x4, Pallas kernels: 9.26 us -> 7.82 us  [the longest x3 6.29 us: down(): pl.pallas_call(down_kernel(blocks), in_specs=[IN_VMEM] * 4 + [UNREAD], ou...]
    pallas_call x1, Pallas kernels: 2.29 us -> 3.1 us  [inner(): pl.pallas_call(inner_kernel, in_specs=[IN_VMEM] * 15, out_specs=[IN_VMEM]...]
    ppermute x1, waiting for transfers between devices: 0.77 us -> 0.01 us  [local(): far_got = lax.ppermute(far, 'blk', beyond)]
  transfers between devices with their start and end apart: 5 -> 5, of which waited for: 1 -> 0; matrix products, arithmetic and copies ran while one was open for 0% -> 0% of each run, Pallas kernels for 50% -> 45%
where the time goes in v3:
time: 21.1 us; the launch traced here: 20.9 us
  Pallas kernels  12.1 us (57%)
  starting transfers between devices  8.71 us (41%)
    ppermute x4, starting transfers between devices, exchange(): return lax.ppermute(x, 'blk', [(i, i ^ bit) for i in range(count)])  6.51 us
    pallas_call x3, Pallas kernels, down(): pl.pallas_call(down_kernel(blocks), in_specs=[IN_VMEM] * 4 + [UNREAD], ou...  6.29 us
    pallas_call x1, Pallas kernels, inner(): pl.pallas_call(inner_kernel, in_specs=[IN_VMEM] * 15, out_specs=[IN_VMEM]...  3.1 us
    ppermute x1, starting transfers between devices, local(): far_got = lax.ppermute(far, 'blk', beyond)  2.2 us
    pallas_call x1, Pallas kernels, surface(): pl.pallas_call(surface_kernel, in_specs=[IN_HBM] * 10, out_specs=[IN_VMEM...  1.53 us
    pallas_call x1, Pallas kernels, edge_side(): pl.pallas_call(edge_side_kernel, in_specs=[IN_VMEM] * 8, out_specs=IN_HBM...  0.82 us
  transfers between devices with their start and end apart: 5, of which 0 were waited for; matrix products, arithmetic and copies ran while one was open for 0% of the time, Pallas kernels for 45%

profile of v3, /device:TPU:1, one launch (start us, length us, event | category | flops | bytes accessed | tf_op | source)
XLA Modules:
  0.0 20.9 jit_solution(15084649490319762270)
XLA Ops:
  0.0 1.5 %surface.1 = (bf16[4,2,8,128]{3,2,1,0:T(8,128)(2,1)S(1)}, bf16[4,2,8,128]{3,2,1,0:T(8,128)(2,1)S(1)}, bf16[16,32,1024]{2,1,0:T(8,128)(2,1)S(1)}, bf16[512,256]{1...) custom-call(s32[32,128]{1,0:T(8,128)} %bitcast.11, ...), custom_call_target="tpu_custom_call" | custom-call | tf_op jit(solution)/shard_map/surface/pallas_call | solution.py:217
  1.5 1.5 %collective-permute-start = (bf16[4,2,8,128]{3,2,1,0:T(8,128)(2,1)S(1)}, bf16[4,2,8,128]{3,2,1,0:T(8,128)(2,1)S(1)}, u32[]{:S(2)}, u32[]{:S(2)}) collective-permute-start(bf16[4,2,8,128]{3,2,1,0:T(8,128)(2,1)S(1)} %get-tuple-element.41), channel_id=1, source_target_pairs={{0,16},{16,0},{32,48},{48,32},{64,80},{80,64},{96,112},{112,96},{1... | collective-permute-start | bytes 49160 | tf_op jit(solution)/shard_map/ppermute | solution.py:683
  3.0 1.1 %down.3 = (f32[1,32,3,32,128]{4,3,2,1,0:T(8,128)S(1)}, f32[1,33,8,128]{3,2,1,0:T(8,128)S(1)}, f32[1,3,32,128]{3,2,1,0:T(8,128)S(1)}) custom-call(bf16[16,32,1024]{2,1,0:T(8,128)(2,1)S(1)} %get-tuple-element.33.gas_ref, bf16[512,256]{1,0:T(8,128)(2,1)S(1)} %get-tuple-element.34.wide_ref, f32[5,8,128]{2,1,0:T(8,128)S(1)} %get-tuple-element.35.column_ref, ...), custom_call_target="tpu_custom_call" | custom-call | flops 200000000 | bytes 4000000 | tf_op jit(solution)/shard_map/down/pallas_call | solution.py:410
  4.2 0.0 collective-permute-done.got_ref
  4.2 1.5 %collective-permute-start.1 = (bf16[2,2,8,128]{3,2,1,0:T(8,128)(2,1)S(1)}, bf16[2,2,8,128]{3,2,1,0:T(8,128)(2,1)S(1)}, u32[]{:S(2)}, u32[]{:S(2)}) collective-permute-start(bf16[2,2,8,128]{3,2,1,0:T(8,128)(2,1)S(1)} %get-tuple-element.46), channel_id=1, source_target_pairs={{0,32},{16,48},{32,0},{48,16},{64,96},{80,112},{96,64},{112,80},{1... | collective-permute-start | bytes 24584 | tf_op jit(solution)/shard_map/ppermute | solution.py:683
  5.7 2.1 %down.4 = (f32[2,32,3,32,128]{4,3,2,1,0:T(8,128)S(1)}, f32[2,33,8,128]{3,2,1,0:T(8,128)S(1)}, f32[2,3,32,128]{3,2,1,0:T(8,128)S(1)}) custom-call(bf16[16,32,1024]{2,1,0:T(8,128)(2,1)S(1)} %get-tuple-element.33.gas_ref, bf16[512,256]{1,0:T(8,128)(2,1)S(1)} %get-tuple-element.34.wide_ref, f32[5,8,128]{2,1,0:T(8,128)S(1)} %get-tuple-element.35.column_ref, ...), custom_call_target="tpu_custom_call" | custom-call | flops 400000000 | bytes 4000000 | tf_op jit(solution)/shard_map/down/pallas_call | solution.py:410
  7.8 0.0 collective-permute-done.1.got_ref
  7.8 2.7 %collective-permute-start.2 = (bf16[1,2,8,128]{3,2,1,0:T(8,128)(2,1)S(1)}, bf16[1,2,8,128]{3,2,1,0:T(8,128)(2,1)S(1)}, u32[]{:S(2)}, u32[]{:S(2)}) collective-permute-start(bf16[1,2,8,128]{3,2,1,0:T(8,128)(2,1)S(1)} %get-tuple-element.48), channel_id=1, source_target_pairs={{0,64},{16,80},{32,96},{48,112},{64,0},{80,16},{96,32},{112,48},{1... | collective-permute-start | bytes 12296 | tf_op jit(solution)/shard_map/ppermute | solution.py:683
  10.5 3.1 %down.5 = (f32[3,32,3,32,128]{4,3,2,1,0:T(8,128)S(1)}, f32[3,33,8,128]{3,2,1,0:T(8,128)S(1)}, f32[3,3,32,128]{3,2,1,0:T(8,128)S(1)}) custom-call(bf16[16,32,1024]{2,1,0:T(8,128)(2,1)S(1)} %get-tuple-element.33.gas_ref, bf16[512,256]{1,0:T(8,128)(2,1)S(1)} %get-tuple-element.34.wide_ref, f32[5,8,128]{2,1,0:T(8,128)S(1)} %get-tuple-element.35.column_ref, ...), custom_call_target="tpu_custom_call" | custom-call | flops 600000000 | bytes 4000000 | tf_op jit(solution)/shard_map/down/pallas_call | solution.py:410
  13.6 0.0 collective-permute-done.2.got_ref
  13.6 0.3 %up.1 = (f32[72,128]{1,0:T(8,128)S(1)}, f32[72,128]{1,0:T(8,128)S(1)}, f32[72,128]{1,0:T(8,128)S(1)}, f32[72,128]{1,0:T(8,128)S(1)}, f32[2,8,128]{2,1,0:T(8,128)S(1)}) custom-call(f32[1,32,3,32,128]{4,3,2,1,0:T(8,128)S(1)} %get-tuple-element.38.coef_a, f32[1,33,8,128]{3,2,1,0:T(8,128)S(1)} %get-tuple-element.39.esum_a, ...), custom_call_target="tpu_custom_call" | custom-call | flops 4000000 | bytes 4000000 | tf_op jit(solution)/shard_map/up/pallas_call | solution.py:462
  13.9 0.8 %collective-permute-start.3 = (f32[72,128]{1,0:T(8,128)S(1)}, f32[72,128]{1,0:T(8,128)S(1)}, u32[]{:S(2)}, u32[]{:S(2)}) collective-permute-start(f32[72,128]{1,0:T(8,128)S(1)} %get-tuple-element.49), channel_id=1, source_target_pairs={{0,16},{16,0},{32,48},{48,32},{64,80},{80,64},{96,112},{112,96},{1... | collective-permute-start | bytes 110600 | tf_op jit(solution)/shard_map/ppermute | solution.py:683
  14.7 2.2 %collective-permute-start.4 = (f32[72,128]{1,0:T(8,128)S(1)}, f32[72,128]{1,0:T(8,128)S(1)}, u32[]{:S(2)}, u32[]{:S(2)}) collective-permute-start(f32[72,128]{1,0:T(8,128)S(1)} %get-tuple-element.50), channel_id=1, source_target_pairs={{16,32},{32,16},{48,64},{64,48},{80,96},{96,80},{0,0},{112,112},{1... | collective-permute-start | bytes 110600 | tf_op jit(solution)/shard_map/ppermute | solution.py:721
  16.9 3.1 %inner.1 = (f32[33,2,1024]{2,1,0:T(2,128)S(1)}, f32[2,72,128]{2,1,0:T(8,128)S(1)}) custom-call(bf16[16,32,1024]{2,1,0:T(8,128)(2,1)S(1)} %get-tuple-element.33.gas_ref, bf16[512,256]{1,0:T(8,128)(2,1)S(1)} %get-tuple-element.34.wide_ref, f32[5,8,128]{2,1,0:T(8,128)S(1)} %get-tuple-element.35.column_ref, f32[32,128]{1,0:T(8,128)S(1)} %get-tuple-element.36.solar_ref, ...), custom_call_target="tpu_custom_call" | custom-call | flops 2000000000 | bytes 4000000 | tf_op jit(solution)/shard_map/inner/pallas_call | solution.py:591
  20.0 0.0 collective-permute-done.3.near_got
  20.0 0.0 collective-permute-done.4.far_got
  20.0 0.8 %edge_side.1 = f32[33,2,1024]{2,1,0:T(2,128)} custom-call(f32[72,128]{1,0:T(8,128)S(1)} %collective-permute-done.3.near_got, f32[72,128]{1,0:T(8,128)S(1)} %collective-permute-done.4.far_got, f32[72,128]{1,0:T(8,128)S(1)} %get-tuple-element.51.first_ref, f32[72,128]{1,0:T(8,128)S(1)} %get-tuple-element.52.final_ref, ...), custom_call_target="tpu_custom_call" | custom-call | tf_op jit(solution)/shard_map/edge_side/pallas_call | solution.py:667
  (2 shorter events, 0.0 us)
Async XLA Ops:
  1.5 2.6 %collective-permute-start = (bf16[4,2,8,128]{3,2,1,0:T(8,128)(2,1)S(1)}, bf16[4,2,8,128]{3,2,1,0:T(8,128)(2,1)S(1)}, u32[]{:S(2)}, u32[]{:S(2)}) collective-permute-start(bf16[4,2,8,128]{3,2,1,0:T(8,128)(2,1)S(1)} %get-tuple-element.41), channel_id=1, source_target_pairs={{0,16},{16,0},{32,48},{48,32},{64,80},{80,64},{96,112},{112,96},{1... | collective-permute-start | bytes 49160 | tf_op jit(solution)/shard_map/ppermute | solution.py:683
  4.2 3.6 %collective-permute-start.1 = (bf16[2,2,8,128]{3,2,1,0:T(8,128)(2,1)S(1)}, bf16[2,2,8,128]{3,2,1,0:T(8,128)(2,1)S(1)}, u32[]{:S(2)}, u32[]{:S(2)}) collective-permute-start(bf16[2,2,8,128]{3,2,1,0:T(8,128)(2,1)S(1)} %get-tuple-element.46), channel_id=1, source_target_pairs={{0,32},{16,48},{32,0},{48,16},{64,96},{80,112},{96,64},{112,80},{1... | collective-permute-start | bytes 24584 | tf_op jit(solution)/shard_map/ppermute | solution.py:683
  7.8 5.8 %collective-permute-start.2 = (bf16[1,2,8,128]{3,2,1,0:T(8,128)(2,1)S(1)}, bf16[1,2,8,128]{3,2,1,0:T(8,128)(2,1)S(1)}, u32[]{:S(2)}, u32[]{:S(2)}) collective-permute-start(bf16[1,2,8,128]{3,2,1,0:T(8,128)(2,1)S(1)} %get-tuple-element.48), channel_id=1, source_target_pairs={{0,64},{16,80},{32,96},{48,112},{64,0},{80,16},{96,32},{112,48},{1... | collective-permute-start | bytes 12296 | tf_op jit(solution)/shard_map/ppermute | solution.py:683
  13.9 6.2 %collective-permute-start.3 = (f32[72,128]{1,0:T(8,128)S(1)}, f32[72,128]{1,0:T(8,128)S(1)}, u32[]{:S(2)}, u32[]{:S(2)}) collective-permute-start(f32[72,128]{1,0:T(8,128)S(1)} %get-tuple-element.49), channel_id=1, source_target_pairs={{0,16},{16,0},{32,48},{48,32},{64,80},{80,64},{96,112},{112,96},{1... | collective-permute-start | bytes 110600 | tf_op jit(solution)/shard_map/ppermute | solution.py:683
  14.7 5.3 %collective-permute-start.4 = (f32[72,128]{1,0:T(8,128)S(1)}, f32[72,128]{1,0:T(8,128)S(1)}, u32[]{:S(2)}, u32[]{:S(2)}) collective-permute-start(f32[72,128]{1,0:T(8,128)S(1)} %get-tuple-element.50), channel_id=1, source_target_pairs={{16,32},{32,16},{48,64},{64,48},{80,96},{96,80},{0,0},{112,112},{1... | collective-permute-start | bytes 110600 | tf_op jit(solution)/shard_map/ppermute | solution.py:721

commit v4 on v3

--- a/solution.py
+++ b/solution.py
@@ -683,6 +683,18 @@
     return lax.ppermute(x, "blk", [(i, i ^ bit) for i in range(count)])
 
 
+def beyond(x):
+    count, bands = lax.axis_size("blk"), lax.axis_size("grp")
+    pairs = []
+    for i in range(count):
+        for band in range(bands):
+            if i in (0, count - 1):
+                pairs.append((i * bands + band, i * bands + (band ^ 1)))
+            else:
+                pairs.append((i * bands + band, (i + (1 if i % 2 else -1)) * bands + band))
+    return lax.ppermute(x, ("blk", "grp"), pairs)
+
+
 def local(
     gas_state,
     cos_zenith,
@@ -715,10 +727,7 @@
             send, keep = merge(keep, got, parts[-1][2])
     first, final, near, far, albedo = up(parts, keep, got, column)
     near_got = exchange(near, 1)
-    count = lax.axis_size("blk")
-    beyond = [(i, i + (1 if i % 2 else -1)) for i in range(1, count - 1)]
-    beyond += [(i, i) for i in (0, count - 1)]
-    far_got = lax.ppermute(far, "blk", beyond)
+    far_got = beyond(far)
     full, partial = inner(
         gas, wide, column, solar, albedo, first, final, parts, beside, weights
     )

time: 21.1 us -> 19.4 us (0.919)
  starting transfers between devices: 8.71 us -> 6.88 us
    ppermute x1, starting transfers between devices: 2.2 us -> 0.37 us  [beyond(): return lax.ppermute(x, ('blk', 'grp'), pairs)]
  transfers between devices with their start and end apart: 5 -> 5, of which waited for: 0 -> 1; matrix products, arithmetic and copies ran while one was open for 0% -> 0% of each run, Pallas kernels for 45% -> 49%
where the time goes in v4:
time: 19.4 us; the launch traced here: 19.2 us
  Pallas kernels  12 us (62%)
  starting transfers between devices  6.88 us (35%)
    ppermute x4, starting transfers between devices, exchange(): return lax.ppermute(x, 'blk', [(i, i ^ bit) for i in range(count)])  6.51 us
    pallas_call x3, Pallas kernels, down(): pl.pallas_call(down_kernel(blocks), in_specs=[IN_VMEM] * 4 + [UNREAD], ou...  6.29 us
    pallas_call x1, Pallas kernels, inner(): pl.pallas_call(inner_kernel, in_specs=[IN_VMEM] * 15, out_specs=[IN_VMEM]...  3.09 us
    pallas_call x1, Pallas kernels, surface(): pl.pallas_call(surface_kernel, in_specs=[IN_HBM] * 10, out_specs=[IN_VMEM...  1.53 us
    pallas_call x1, Pallas kernels, edge_side(): pl.pallas_call(edge_side_kernel, in_specs=[IN_VMEM] * 8, out_specs=IN_HBM...  0.81 us
  transfers between devices with their start and end apart: 5, of which 1 were waited for; matrix products, arithmetic and copies ran while one was open for 0% of the time, Pallas kernels for 49%

profile of v4, /device:TPU:1, one launch (start us, length us, event | category | flops | bytes accessed | tf_op | source)
XLA Modules:
  0.0 19.2 jit_solution(16468730839962072102)
XLA Ops:
  0.0 1.5 %surface.1 = (bf16[4,2,8,128]{3,2,1,0:T(8,128)(2,1)S(1)}, bf16[4,2,8,128]{3,2,1,0:T(8,128)(2,1)S(1)}, bf16[16,32,1024]{2,1,0:T(8,128)(2,1)S(1)}, bf16[512,256]{1...) custom-call(s32[32,128]{1,0:T(8,128)} %bitcast.11, ...), custom_call_target="tpu_custom_call" | custom-call | tf_op jit(solution)/shard_map/surface/pallas_call | solution.py:217
  1.5 1.5 %collective-permute-start = (bf16[4,2,8,128]{3,2,1,0:T(8,128)(2,1)S(1)}, bf16[4,2,8,128]{3,2,1,0:T(8,128)(2,1)S(1)}, u32[]{:S(2)}, u32[]{:S(2)}) collective-permute-start(bf16[4,2,8,128]{3,2,1,0:T(8,128)(2,1)S(1)} %get-tuple-element.41), channel_id=1, source_target_pairs={{0,16},{16,0},{32,48},{48,32},{64,80},{80,64},{96,112},{112,96},{1... | collective-permute-start | bytes 49160 | tf_op jit(solution)/shard_map/ppermute | solution.py:683
  3.0 1.1 %down.3 = (f32[1,32,3,32,128]{4,3,2,1,0:T(8,128)S(1)}, f32[1,33,8,128]{3,2,1,0:T(8,128)S(1)}, f32[1,3,32,128]{3,2,1,0:T(8,128)S(1)}) custom-call(bf16[16,32,1024]{2,1,0:T(8,128)(2,1)S(1)} %get-tuple-element.33.gas_ref, bf16[512,256]{1,0:T(8,128)(2,1)S(1)} %get-tuple-element.34.wide_ref, f32[5,8,128]{2,1,0:T(8,128)S(1)} %get-tuple-element.35.column_ref, ...), custom_call_target="tpu_custom_call" | custom-call | flops 200000000 | bytes 4000000 | tf_op jit(solution)/shard_map/down/pallas_call | solution.py:410
  4.2 0.0 collective-permute-done.got_ref
  4.2 1.5 %collective-permute-start.1 = (bf16[2,2,8,128]{3,2,1,0:T(8,128)(2,1)S(1)}, bf16[2,2,8,128]{3,2,1,0:T(8,128)(2,1)S(1)}, u32[]{:S(2)}, u32[]{:S(2)}) collective-permute-start(bf16[2,2,8,128]{3,2,1,0:T(8,128)(2,1)S(1)} %get-tuple-element.46), channel_id=1, source_target_pairs={{0,32},{16,48},{32,0},{48,16},{64,96},{80,112},{96,64},{112,80},{1... | collective-permute-start | bytes 24584 | tf_op jit(solution)/shard_map/ppermute | solution.py:683
  5.7 2.1 %down.4 = (f32[2,32,3,32,128]{4,3,2,1,0:T(8,128)S(1)}, f32[2,33,8,128]{3,2,1,0:T(8,128)S(1)}, f32[2,3,32,128]{3,2,1,0:T(8,128)S(1)}) custom-call(bf16[16,32,1024]{2,1,0:T(8,128)(2,1)S(1)} %get-tuple-element.33.gas_ref, bf16[512,256]{1,0:T(8,128)(2,1)S(1)} %get-tuple-element.34.wide_ref, f32[5,8,128]{2,1,0:T(8,128)S(1)} %get-tuple-element.35.column_ref, ...), custom_call_target="tpu_custom_call" | custom-call | flops 400000000 | bytes 4000000 | tf_op jit(solution)/shard_map/down/pallas_call | solution.py:410
  7.8 0.0 collective-permute-done.1.got_ref
  7.8 2.7 %collective-permute-start.2 = (bf16[1,2,8,128]{3,2,1,0:T(8,128)(2,1)S(1)}, bf16[1,2,8,128]{3,2,1,0:T(8,128)(2,1)S(1)}, u32[]{:S(2)}, u32[]{:S(2)}) collective-permute-start(bf16[1,2,8,128]{3,2,1,0:T(8,128)(2,1)S(1)} %get-tuple-element.48), channel_id=1, source_target_pairs={{0,64},{16,80},{32,96},{48,112},{64,0},{80,16},{96,32},{112,48},{1... | collective-permute-start | bytes 12296 | tf_op jit(solution)/shard_map/ppermute | solution.py:683
  10.5 3.1 %down.5 = (f32[3,32,3,32,128]{4,3,2,1,0:T(8,128)S(1)}, f32[3,33,8,128]{3,2,1,0:T(8,128)S(1)}, f32[3,3,32,128]{3,2,1,0:T(8,128)S(1)}) custom-call(bf16[16,32,1024]{2,1,0:T(8,128)(2,1)S(1)} %get-tuple-element.33.gas_ref, bf16[512,256]{1,0:T(8,128)(2,1)S(1)} %get-tuple-element.34.wide_ref, f32[5,8,128]{2,1,0:T(8,128)S(1)} %get-tuple-element.35.column_ref, ...), custom_call_target="tpu_custom_call" | custom-call | flops 600000000 | bytes 4000000 | tf_op jit(solution)/shard_map/down/pallas_call | solution.py:410
  13.6 0.0 collective-permute-done.2.got_ref
  13.6 0.3 %up.1 = (f32[72,128]{1,0:T(8,128)S(1)}, f32[72,128]{1,0:T(8,128)S(1)}, f32[72,128]{1,0:T(8,128)S(1)}, f32[72,128]{1,0:T(8,128)S(1)}, f32[2,8,128]{2,1,0:T(8,128)S(1)}) custom-call(f32[1,32,3,32,128]{4,3,2,1,0:T(8,128)S(1)} %get-tuple-element.38.coef_a, f32[1,33,8,128]{3,2,1,0:T(8,128)S(1)} %get-tuple-element.39.esum_a, ...), custom_call_target="tpu_custom_call" | custom-call | flops 4000000 | bytes 4000000 | tf_op jit(solution)/shard_map/up/pallas_call | solution.py:462
  13.9 0.8 %collective-permute-start.3 = (f32[72,128]{1,0:T(8,128)S(1)}, f32[72,128]{1,0:T(8,128)S(1)}, u32[]{:S(2)}, u32[]{:S(2)}) collective-permute-start(f32[72,128]{1,0:T(8,128)S(1)} %get-tuple-element.49), channel_id=1, source_target_pairs={{0,16},{16,0},{32,48},{48,32},{64,80},{80,64},{96,112},{112,96},{1... | collective-permute-start | bytes 110600 | tf_op jit(solution)/shard_map/ppermute | solution.py:683
  14.7 0.4 %collective-permute-start.4 = (f32[72,128]{1,0:T(8,128)S(1)}, f32[72,128]{1,0:T(8,128)S(1)}, u32[]{:S(2)}, u32[]{:S(2)}) collective-permute-start(f32[72,128]{1,0:T(8,128)S(1)} %get-tuple-element.50), channel_id=1, source_target_pairs={{0,1},{1,0},{2,3},{3,2},{4,5},{5,4},{6,7},{7,6},{8,9},{9,8},{10,11... | collective-permute-start | bytes 110600 | tf_op jit(solution)/shard_map/ppermute | solution.py:695
  15.1 3.1 %inner.1 = (f32[33,2,1024]{2,1,0:T(2,128)S(1)}, f32[2,72,128]{2,1,0:T(8,128)S(1)}) custom-call(bf16[16,32,1024]{2,1,0:T(8,128)(2,1)S(1)} %get-tuple-element.33.gas_ref, bf16[512,256]{1,0:T(8,128)(2,1)S(1)} %get-tuple-element.34.wide_ref, f32[5,8,128]{2,1,0:T(8,128)S(1)} %get-tuple-element.35.column_ref, f32[32,128]{1,0:T(8,128)S(1)} %get-tuple-element.36.solar_ref, ...), custom_call_target="tpu_custom_call" | custom-call | flops 2000000000 | bytes 4000000 | tf_op jit(solution)/shard_map/inner/pallas_call | solution.py:591
  18.2 0.0 collective-permute-done.3.near_got
  18.2 0.2 collective-permute-done.4.far_got
  18.4 0.8 %edge_side.1 = f32[33,2,1024]{2,1,0:T(2,128)} custom-call(f32[72,128]{1,0:T(8,128)S(1)} %collective-permute-done.3.near_got, f32[72,128]{1,0:T(8,128)S(1)} %collective-permute-done.4.far_got, f32[72,128]{1,0:T(8,128)S(1)} %get-tuple-element.51.first_ref, f32[72,128]{1,0:T(8,128)S(1)} %get-tuple-element.52.final_ref, ...), custom_call_target="tpu_custom_call" | custom-call | tf_op jit(solution)/shard_map/edge_side/pallas_call | solution.py:667
  (2 shorter events, 0.0 us)
Async XLA Ops:
  1.5 2.6 %collective-permute-start = (bf16[4,2,8,128]{3,2,1,0:T(8,128)(2,1)S(1)}, bf16[4,2,8,128]{3,2,1,0:T(8,128)(2,1)S(1)}, u32[]{:S(2)}, u32[]{:S(2)}) collective-permute-start(bf16[4,2,8,128]{3,2,1,0:T(8,128)(2,1)S(1)} %get-tuple-element.41), channel_id=1, source_target_pairs={{0,16},{16,0},{32,48},{48,32},{64,80},{80,64},{96,112},{112,96},{1... | collective-permute-start | bytes 49160 | tf_op jit(solution)/shard_map/ppermute | solution.py:683
  4.2 3.6 %collective-permute-start.1 = (bf16[2,2,8,128]{3,2,1,0:T(8,128)(2,1)S(1)}, bf16[2,2,8,128]{3,2,1,0:T(8,128)(2,1)S(1)}, u32[]{:S(2)}, u32[]{:S(2)}) collective-permute-start(bf16[2,2,8,128]{3,2,1,0:T(8,128)(2,1)S(1)} %get-tuple-element.46), channel_id=1, source_target_pairs={{0,32},{16,48},{32,0},{48,16},{64,96},{80,112},{96,64},{112,80},{1... | collective-permute-start | bytes 24584 | tf_op jit(solution)/shard_map/ppermute | solution.py:683
  7.8 5.8 %collective-permute-start.2 = (bf16[1,2,8,128]{3,2,1,0:T(8,128)(2,1)S(1)}, bf16[1,2,8,128]{3,2,1,0:T(8,128)(2,1)S(1)}, u32[]{:S(2)}, u32[]{:S(2)}) collective-permute-start(bf16[1,2,8,128]{3,2,1,0:T(8,128)(2,1)S(1)} %get-tuple-element.48), channel_id=1, source_target_pairs={{0,64},{16,80},{32,96},{48,112},{64,0},{80,16},{96,32},{112,48},{1... | collective-permute-start | bytes 12296 | tf_op jit(solution)/shard_map/ppermute | solution.py:683
  13.9 4.3 %collective-permute-start.3 = (f32[72,128]{1,0:T(8,128)S(1)}, f32[72,128]{1,0:T(8,128)S(1)}, u32[]{:S(2)}, u32[]{:S(2)}) collective-permute-start(f32[72,128]{1,0:T(8,128)S(1)} %get-tuple-element.49), channel_id=1, source_target_pairs={{0,16},{16,0},{32,48},{48,32},{64,80},{80,64},{96,112},{112,96},{1... | collective-permute-start | bytes 110600 | tf_op jit(solution)/shard_map/ppermute | solution.py:683
  14.7 3.7 %collective-permute-start.4 = (f32[72,128]{1,0:T(8,128)S(1)}, f32[72,128]{1,0:T(8,128)S(1)}, u32[]{:S(2)}, u32[]{:S(2)}) collective-permute-start(f32[72,128]{1,0:T(8,128)S(1)} %get-tuple-element.50), channel_id=1, source_target_pairs={{0,1},{1,0},{2,3},{3,2},{4,5},{5,4},{6,7},{7,6},{8,9},{9,8},{10,11... | collective-permute-start | bytes 110600 | tf_op jit(solution)/shard_map/ppermute | solution.py:695

commit v5 on v4

--- a/solution.py
+++ b/solution.py
@@ -689,7 +689,7 @@
     for i in range(count):
         for band in range(bands):
             if i in (0, count - 1):
-                pairs.append((i * bands + band, i * bands + (band ^ 1)))
+                pairs.append((i * bands + band, i * bands + (band ^ 4)))
             else:
                 pairs.append((i * bands + band, (i + (1 if i % 2 else -1)) * bands + band))
     return lax.ppermute(x, ("blk", "grp"), pairs)
@@ -726,8 +726,8 @@
         if i < 2:
             send, keep = merge(keep, got, parts[-1][2])
     first, final, near, far, albedo = up(parts, keep, got, column)
+    far_got = beyond(far)
     near_got = exchange(near, 1)
-    far_got = beyond(far)
     full, partial = inner(
         gas, wide, column, solar, albedo, first, final, parts, beside, weights
     )

time: 19.4 us -> 19.4 us (level)
  no operation moved by 1% of the time
where the time goes in v5:
time: 19.4 us; the launch traced here: 19.2 us
  Pallas kernels  12 us (62%)
  starting transfers between devices  6.88 us (35%)
    ppermute x4, starting transfers between devices, exchange(): return lax.ppermute(x, 'blk', [(i, i ^ bit) for i in range(count)])  6.51 us
    pallas_call x3, Pallas kernels, down(): pl.pallas_call(down_kernel(blocks), in_specs=[IN_VMEM] * 4 + [UNREAD], ou...  6.29 us
    pallas_call x1, Pallas kernels, inner(): pl.pallas_call(inner_kernel, in_specs=[IN_VMEM] * 15, out_specs=[IN_VMEM]...  3.09 us
    pallas_call x1, Pallas kernels, surface(): pl.pallas_call(surface_kernel, in_specs=[IN_HBM] * 10, out_specs=[IN_VMEM...  1.53 us
    pallas_call x1, Pallas kernels, edge_side(): pl.pallas_call(edge_side_kernel, in_specs=[IN_VMEM] * 8, out_specs=IN_HBM...  0.81 us
  transfers between devices with their start and end apart: 5, of which 1 were waited for; matrix products, arithmetic and copies ran while one was open for 0% of the time, Pallas kernels for 49%

profile of v5, /device:TPU:1, one launch (start us, length us, event | category | flops | bytes accessed | tf_op | source)
XLA Modules:
  0.0 19.2 jit_solution(13790452953367760461)
XLA Ops:
  0.0 1.5 %surface.1 = (bf16[4,2,8,128]{3,2,1,0:T(8,128)(2,1)S(1)}, bf16[4,2,8,128]{3,2,1,0:T(8,128)(2,1)S(1)}, bf16[16,32,1024]{2,1,0:T(8,128)(2,1)S(1)}, bf16[512,256]{1...) custom-call(s32[32,128]{1,0:T(8,128)} %bitcast.11, ...), custom_call_target="tpu_custom_call" | custom-call | tf_op jit(solution)/shard_map/surface/pallas_call | solution.py:217
  1.5 1.5 %collective-permute-start = (bf16[4,2,8,128]{3,2,1,0:T(8,128)(2,1)S(1)}, bf16[4,2,8,128]{3,2,1,0:T(8,128)(2,1)S(1)}, u32[]{:S(2)}, u32[]{:S(2)}) collective-permute-start(bf16[4,2,8,128]{3,2,1,0:T(8,128)(2,1)S(1)} %get-tuple-element.41), channel_id=1, source_target_pairs={{0,16},{16,0},{32,48},{48,32},{64,80},{80,64},{96,112},{112,96},{1... | collective-permute-start | bytes 49160 | tf_op jit(solution)/shard_map/ppermute | solution.py:683
  3.0 1.1 %down.3 = (f32[1,32,3,32,128]{4,3,2,1,0:T(8,128)S(1)}, f32[1,33,8,128]{3,2,1,0:T(8,128)S(1)}, f32[1,3,32,128]{3,2,1,0:T(8,128)S(1)}) custom-call(bf16[16,32,1024]{2,1,0:T(8,128)(2,1)S(1)} %get-tuple-element.33.gas_ref, bf16[512,256]{1,0:T(8,128)(2,1)S(1)} %get-tuple-element.34.wide_ref, f32[5,8,128]{2,1,0:T(8,128)S(1)} %get-tuple-element.35.column_ref, ...), custom_call_target="tpu_custom_call" | custom-call | flops 200000000 | bytes 4000000 | tf_op jit(solution)/shard_map/down/pallas_call | solution.py:410
  4.2 0.0 collective-permute-done.got_ref
  4.2 1.5 %collective-permute-start.1 = (bf16[2,2,8,128]{3,2,1,0:T(8,128)(2,1)S(1)}, bf16[2,2,8,128]{3,2,1,0:T(8,128)(2,1)S(1)}, u32[]{:S(2)}, u32[]{:S(2)}) collective-permute-start(bf16[2,2,8,128]{3,2,1,0:T(8,128)(2,1)S(1)} %get-tuple-element.46), channel_id=1, source_target_pairs={{0,32},{16,48},{32,0},{48,16},{64,96},{80,112},{96,64},{112,80},{1... | collective-permute-start | bytes 24584 | tf_op jit(solution)/shard_map/ppermute | solution.py:683
  5.7 2.1 %down.4 = (f32[2,32,3,32,128]{4,3,2,1,0:T(8,128)S(1)}, f32[2,33,8,128]{3,2,1,0:T(8,128)S(1)}, f32[2,3,32,128]{3,2,1,0:T(8,128)S(1)}) custom-call(bf16[16,32,1024]{2,1,0:T(8,128)(2,1)S(1)} %get-tuple-element.33.gas_ref, bf16[512,256]{1,0:T(8,128)(2,1)S(1)} %get-tuple-element.34.wide_ref, f32[5,8,128]{2,1,0:T(8,128)S(1)} %get-tuple-element.35.column_ref, ...), custom_call_target="tpu_custom_call" | custom-call | flops 400000000 | bytes 4000000 | tf_op jit(solution)/shard_map/down/pallas_call | solution.py:410
  7.8 0.0 collective-permute-done.1.got_ref
  7.8 2.7 %collective-permute-start.2 = (bf16[1,2,8,128]{3,2,1,0:T(8,128)(2,1)S(1)}, bf16[1,2,8,128]{3,2,1,0:T(8,128)(2,1)S(1)}, u32[]{:S(2)}, u32[]{:S(2)}) collective-permute-start(bf16[1,2,8,128]{3,2,1,0:T(8,128)(2,1)S(1)} %get-tuple-element.48), channel_id=1, source_target_pairs={{0,64},{16,80},{32,96},{48,112},{64,0},{80,16},{96,32},{112,48},{1... | collective-permute-start | bytes 12296 | tf_op jit(solution)/shard_map/ppermute | solution.py:683
  10.5 3.1 %down.5 = (f32[3,32,3,32,128]{4,3,2,1,0:T(8,128)S(1)}, f32[3,33,8,128]{3,2,1,0:T(8,128)S(1)}, f32[3,3,32,128]{3,2,1,0:T(8,128)S(1)}) custom-call(bf16[16,32,1024]{2,1,0:T(8,128)(2,1)S(1)} %get-tuple-element.33.gas_ref, bf16[512,256]{1,0:T(8,128)(2,1)S(1)} %get-tuple-element.34.wide_ref, f32[5,8,128]{2,1,0:T(8,128)S(1)} %get-tuple-element.35.column_ref, ...), custom_call_target="tpu_custom_call" | custom-call | flops 600000000 | bytes 4000000 | tf_op jit(solution)/shard_map/down/pallas_call | solution.py:410
  13.6 0.0 collective-permute-done.2.got_ref
  13.6 0.3 %up.1 = (f32[72,128]{1,0:T(8,128)S(1)}, f32[72,128]{1,0:T(8,128)S(1)}, f32[72,128]{1,0:T(8,128)S(1)}, f32[72,128]{1,0:T(8,128)S(1)}, f32[2,8,128]{2,1,0:T(8,128)S(1)}) custom-call(f32[1,32,3,32,128]{4,3,2,1,0:T(8,128)S(1)} %get-tuple-element.38.coef_a, f32[1,33,8,128]{3,2,1,0:T(8,128)S(1)} %get-tuple-element.39.esum_a, ...), custom_call_target="tpu_custom_call" | custom-call | flops 4000000 | bytes 4000000 | tf_op jit(solution)/shard_map/up/pallas_call | solution.py:462
  13.9 0.8 %collective-permute-start.3 = (f32[72,128]{1,0:T(8,128)S(1)}, f32[72,128]{1,0:T(8,128)S(1)}, u32[]{:S(2)}, u32[]{:S(2)}) collective-permute-start(f32[72,128]{1,0:T(8,128)S(1)} %get-tuple-element.49), channel_id=1, source_target_pairs={{0,16},{16,0},{32,48},{48,32},{64,80},{80,64},{96,112},{112,96},{1... | collective-permute-start | bytes 110600 | tf_op jit(solution)/shard_map/ppermute | solution.py:683
  14.7 0.4 %collective-permute-start.4 = (f32[72,128]{1,0:T(8,128)S(1)}, f32[72,128]{1,0:T(8,128)S(1)}, u32[]{:S(2)}, u32[]{:S(2)}) collective-permute-start(f32[72,128]{1,0:T(8,128)S(1)} %get-tuple-element.50), channel_id=1, source_target_pairs={{0,4},{1,5},{2,6},{3,7},{4,0},{5,1},{6,2},{7,3},{8,12},{9,13},{10,... | collective-permute-start | bytes 110600 | tf_op jit(solution)/shard_map/ppermute | solution.py:695
  15.1 3.1 %inner.1 = (f32[33,2,1024]{2,1,0:T(2,128)S(1)}, f32[2,72,128]{2,1,0:T(8,128)S(1)}) custom-call(bf16[16,32,1024]{2,1,0:T(8,128)(2,1)S(1)} %get-tuple-element.33.gas_ref, bf16[512,256]{1,0:T(8,128)(2,1)S(1)} %get-tuple-element.34.wide_ref, f32[5,8,128]{2,1,0:T(8,128)S(1)} %get-tuple-element.35.column_ref, f32[32,128]{1,0:T(8,128)S(1)} %get-tuple-element.36.solar_ref, ...), custom_call_target="tpu_custom_call" | custom-call | flops 2000000000 | bytes 4000000 | tf_op jit(solution)/shard_map/inner/pallas_call | solution.py:591
  18.2 0.0 collective-permute-done.3.near_got
  18.2 0.2 collective-permute-done.4.far_got
  18.4 0.8 %edge_side.1 = f32[33,2,1024]{2,1,0:T(2,128)} custom-call(f32[72,128]{1,0:T(8,128)S(1)} %collective-permute-done.3.near_got, f32[72,128]{1,0:T(8,128)S(1)} %collective-permute-done.4.far_got, f32[72,128]{1,0:T(8,128)S(1)} %get-tuple-element.51.first_ref, f32[72,128]{1,0:T(8,128)S(1)} %get-tuple-element.52.final_ref, ...), custom_call_target="tpu_custom_call" | custom-call | tf_op jit(solution)/shard_map/edge_side/pallas_call | solution.py:667
  (2 shorter events, 0.0 us)
Async XLA Ops:
  1.5 2.6 %collective-permute-start = (bf16[4,2,8,128]{3,2,1,0:T(8,128)(2,1)S(1)}, bf16[4,2,8,128]{3,2,1,0:T(8,128)(2,1)S(1)}, u32[]{:S(2)}, u32[]{:S(2)}) collective-permute-start(bf16[4,2,8,128]{3,2,1,0:T(8,128)(2,1)S(1)} %get-tuple-element.41), channel_id=1, source_target_pairs={{0,16},{16,0},{32,48},{48,32},{64,80},{80,64},{96,112},{112,96},{1... | collective-permute-start | bytes 49160 | tf_op jit(solution)/shard_map/ppermute | solution.py:683
  4.2 3.6 %collective-permute-start.1 = (bf16[2,2,8,128]{3,2,1,0:T(8,128)(2,1)S(1)}, bf16[2,2,8,128]{3,2,1,0:T(8,128)(2,1)S(1)}, u32[]{:S(2)}, u32[]{:S(2)}) collective-permute-start(bf16[2,2,8,128]{3,2,1,0:T(8,128)(2,1)S(1)} %get-tuple-element.46), channel_id=1, source_target_pairs={{0,32},{16,48},{32,0},{48,16},{64,96},{80,112},{96,64},{112,80},{1... | collective-permute-start | bytes 24584 | tf_op jit(solution)/shard_map/ppermute | solution.py:683
  7.8 5.8 %collective-permute-start.2 = (bf16[1,2,8,128]{3,2,1,0:T(8,128)(2,1)S(1)}, bf16[1,2,8,128]{3,2,1,0:T(8,128)(2,1)S(1)}, u32[]{:S(2)}, u32[]{:S(2)}) collective-permute-start(bf16[1,2,8,128]{3,2,1,0:T(8,128)(2,1)S(1)} %get-tuple-element.48), channel_id=1, source_target_pairs={{0,64},{16,80},{32,96},{48,112},{64,0},{80,16},{96,32},{112,48},{1... | collective-permute-start | bytes 12296 | tf_op jit(solution)/shard_map/ppermute | solution.py:683
  13.9 4.3 %collective-permute-start.3 = (f32[72,128]{1,0:T(8,128)S(1)}, f32[72,128]{1,0:T(8,128)S(1)}, u32[]{:S(2)}, u32[]{:S(2)}) collective-permute-start(f32[72,128]{1,0:T(8,128)S(1)} %get-tuple-element.49), channel_id=1, source_target_pairs={{0,16},{16,0},{32,48},{48,32},{64,80},{80,64},{96,112},{112,96},{1... | collective-permute-start | bytes 110600 | tf_op jit(solution)/shard_map/ppermute | solution.py:683
  14.7 3.7 %collective-permute-start.4 = (f32[72,128]{1,0:T(8,128)S(1)}, f32[72,128]{1,0:T(8,128)S(1)}, u32[]{:S(2)}, u32[]{:S(2)}) collective-permute-start(f32[72,128]{1,0:T(8,128)S(1)} %get-tuple-element.50), channel_id=1, source_target_pairs={{0,4},{1,5},{2,6},{3,7},{4,0},{5,1},{6,2},{7,3},{8,12},{9,13},{10,... | collective-permute-start | bytes 110600 | tf_op jit(solution)/shard_map/ppermute | solution.py:695

commit v6 on v5

--- a/solution.py
+++ b/solution.py
@@ -620,8 +620,8 @@
 
 
 def edge_side_kernel(
+    far_got,
     near_got,
-    far_got,
     first_ref,
     final_ref,
     partial_ref,
@@ -663,7 +663,7 @@
         started.wait()
 
 
-def edge_side(near_got, far_got, first, final, partial, neighbours, side_weight, full):
+def edge_side(far_got, near_got, first, final, partial, neighbours, side_weight, full):
     return pl.pallas_call(
         edge_side_kernel,
         in_specs=[IN_VMEM] * 8,
@@ -675,7 +675,7 @@
         ],
         compiler_params=params(4),
         name="edge_side",
-    )(near_got, far_got, first, final, partial, neighbours, side_weight, full)
+    )(far_got, near_got, first, final, partial, neighbours, side_weight, full)
 
 
 def exchange(x, bit):
@@ -731,7 +731,7 @@
     full, partial = inner(
         gas, wide, column, solar, albedo, first, final, parts, beside, weights
     )
-    done = edge_side(near_got, far_got, first, final, partial, beside, weights, full)
+    done = edge_side(far_got, near_got, first, final, partial, beside, weights, full)
     return done.transpose(1, 0, 2)
 
 

time: 19.4 us -> 20.3 us (1.046)
  starting transfers between devices: 6.88 us -> 8 us
    ppermute x1, starting transfers between devices: 0.37 us -> 1.12 us  [beyond(): return lax.ppermute(x, ('blk', 'grp'), pairs)]
    ppermute x4, starting transfers between devices: 6.51 us -> 6.88 us  [exchange(): return lax.ppermute(x, 'blk', [(i, i ^ bit) for i in range(count)])]
  transfers between devices with their start and end apart: 5 -> 5, of which waited for: 1 -> 0; matrix products, arithmetic and copies ran while one was open for 0% -> 0% of each run, Pallas kernels for 49% -> 47%
where the time goes in v6:
time: 20.3 us; the launch traced here: 20.1 us
  Pallas kernels  12 us (59%)
  starting transfers between devices  8 us (39%)
    ppermute x4, starting transfers between devices, exchange(): return lax.ppermute(x, 'blk', [(i, i ^ bit) for i in range(count)])  6.88 us
    pallas_call x3, Pallas kernels, down(): pl.pallas_call(down_kernel(blocks), in_specs=[IN_VMEM] * 4 + [UNREAD], ou...  6.29 us
    pallas_call x1, Pallas kernels, inner(): pl.pallas_call(inner_kernel, in_specs=[IN_VMEM] * 15, out_specs=[IN_VMEM]...  3.1 us
    pallas_call x1, Pallas kernels, surface(): pl.pallas_call(surface_kernel, in_specs=[IN_HBM] * 10, out_specs=[IN_VMEM...  1.53 us
    ppermute x1, starting transfers between devices, beyond(): return lax.ppermute(x, ('blk', 'grp'), pairs)  1.12 us
    pallas_call x1, Pallas kernels, edge_side(): pl.pallas_call(edge_side_kernel, in_specs=[IN_VMEM] * 8, out_specs=IN_HBM...  0.82 us
  transfers between devices with their start and end apart: 5, of which 0 were waited for; matrix products, arithmetic and copies ran while one was open for 0% of the time, Pallas kernels for 47%

profile of v6, /device:TPU:1, one launch (start us, length us, event | category | flops | bytes accessed | tf_op | source)
XLA Modules:
  0.0 20.1 jit_solution(5626180483779441720)
XLA Ops:
  0.0 1.5 %surface.1 = (bf16[4,2,8,128]{3,2,1,0:T(8,128)(2,1)S(1)}, bf16[4,2,8,128]{3,2,1,0:T(8,128)(2,1)S(1)}, bf16[16,32,1024]{2,1,0:T(8,128)(2,1)S(1)}, bf16[512,256]{1...) custom-call(s32[32,128]{1,0:T(8,128)} %bitcast.11, ...), custom_call_target="tpu_custom_call" | custom-call | tf_op jit(solution)/shard_map/surface/pallas_call | solution.py:217
  1.5 1.5 %collective-permute-start = (bf16[4,2,8,128]{3,2,1,0:T(8,128)(2,1)S(1)}, bf16[4,2,8,128]{3,2,1,0:T(8,128)(2,1)S(1)}, u32[]{:S(2)}, u32[]{:S(2)}) collective-permute-start(bf16[4,2,8,128]{3,2,1,0:T(8,128)(2,1)S(1)} %get-tuple-element.41), channel_id=1, source_target_pairs={{0,16},{16,0},{32,48},{48,32},{64,80},{80,64},{96,112},{112,96},{1... | collective-permute-start | bytes 49160 | tf_op jit(solution)/shard_map/ppermute | solution.py:683
  3.0 1.1 %down.3 = (f32[1,32,3,32,128]{4,3,2,1,0:T(8,128)S(1)}, f32[1,33,8,128]{3,2,1,0:T(8,128)S(1)}, f32[1,3,32,128]{3,2,1,0:T(8,128)S(1)}) custom-call(bf16[16,32,1024]{2,1,0:T(8,128)(2,1)S(1)} %get-tuple-element.33.gas_ref, bf16[512,256]{1,0:T(8,128)(2,1)S(1)} %get-tuple-element.34.wide_ref, f32[5,8,128]{2,1,0:T(8,128)S(1)} %get-tuple-element.35.column_ref, ...), custom_call_target="tpu_custom_call" | custom-call | flops 200000000 | bytes 4000000 | tf_op jit(solution)/shard_map/down/pallas_call | solution.py:410
  4.2 0.0 collective-permute-done.got_ref
  4.2 1.5 %collective-permute-start.1 = (bf16[2,2,8,128]{3,2,1,0:T(8,128)(2,1)S(1)}, bf16[2,2,8,128]{3,2,1,0:T(8,128)(2,1)S(1)}, u32[]{:S(2)}, u32[]{:S(2)}) collective-permute-start(bf16[2,2,8,128]{3,2,1,0:T(8,128)(2,1)S(1)} %get-tuple-element.46), channel_id=1, source_target_pairs={{0,32},{16,48},{32,0},{48,16},{64,96},{80,112},{96,64},{112,80},{1... | collective-permute-start | bytes 24584 | tf_op jit(solution)/shard_map/ppermute | solution.py:683
  5.7 2.1 %down.4 = (f32[2,32,3,32,128]{4,3,2,1,0:T(8,128)S(1)}, f32[2,33,8,128]{3,2,1,0:T(8,128)S(1)}, f32[2,3,32,128]{3,2,1,0:T(8,128)S(1)}) custom-call(bf16[16,32,1024]{2,1,0:T(8,128)(2,1)S(1)} %get-tuple-element.33.gas_ref, bf16[512,256]{1,0:T(8,128)(2,1)S(1)} %get-tuple-element.34.wide_ref, f32[5,8,128]{2,1,0:T(8,128)S(1)} %get-tuple-element.35.column_ref, ...), custom_call_target="tpu_custom_call" | custom-call | flops 400000000 | bytes 4000000 | tf_op jit(solution)/shard_map/down/pallas_call | solution.py:410
  7.8 0.0 collective-permute-done.1.got_ref
  7.8 2.7 %collective-permute-start.2 = (bf16[1,2,8,128]{3,2,1,0:T(8,128)(2,1)S(1)}, bf16[1,2,8,128]{3,2,1,0:T(8,128)(2,1)S(1)}, u32[]{:S(2)}, u32[]{:S(2)}) collective-permute-start(bf16[1,2,8,128]{3,2,1,0:T(8,128)(2,1)S(1)} %get-tuple-element.48), channel_id=1, source_target_pairs={{0,64},{16,80},{32,96},{48,112},{64,0},{80,16},{96,32},{112,48},{1... | collective-permute-start | bytes 12296 | tf_op jit(solution)/shard_map/ppermute | solution.py:683
  10.5 3.1 %down.5 = (f32[3,32,3,32,128]{4,3,2,1,0:T(8,128)S(1)}, f32[3,33,8,128]{3,2,1,0:T(8,128)S(1)}, f32[3,3,32,128]{3,2,1,0:T(8,128)S(1)}) custom-call(bf16[16,32,1024]{2,1,0:T(8,128)(2,1)S(1)} %get-tuple-element.33.gas_ref, bf16[512,256]{1,0:T(8,128)(2,1)S(1)} %get-tuple-element.34.wide_ref, f32[5,8,128]{2,1,0:T(8,128)S(1)} %get-tuple-element.35.column_ref, ...), custom_call_target="tpu_custom_call" | custom-call | flops 600000000 | bytes 4000000 | tf_op jit(solution)/shard_map/down/pallas_call | solution.py:410
  13.6 0.0 collective-permute-done.2.got_ref
  13.6 0.3 %up.1 = (f32[72,128]{1,0:T(8,128)S(1)}, f32[72,128]{1,0:T(8,128)S(1)}, f32[72,128]{1,0:T(8,128)S(1)}, f32[72,128]{1,0:T(8,128)S(1)}, f32[2,8,128]{2,1,0:T(8,128)S(1)}) custom-call(f32[1,32,3,32,128]{4,3,2,1,0:T(8,128)S(1)} %get-tuple-element.38.coef_a, f32[1,33,8,128]{3,2,1,0:T(8,128)S(1)} %get-tuple-element.39.esum_a, ...), custom_call_target="tpu_custom_call" | custom-call | flops 4000000 | bytes 4000000 | tf_op jit(solution)/shard_map/up/pallas_call | solution.py:462
  13.9 1.1 %collective-permute-start.3 = (f32[72,128]{1,0:T(8,128)S(1)}, f32[72,128]{1,0:T(8,128)S(1)}, u32[]{:S(2)}, u32[]{:S(2)}) collective-permute-start(f32[72,128]{1,0:T(8,128)S(1)} %get-tuple-element.49), channel_id=1, source_target_pairs={{0,4},{1,5},{2,6},{3,7},{4,0},{5,1},{6,2},{7,3},{8,12},{9,13},{10,... | collective-permute-start | bytes 110600 | tf_op jit(solution)/shard_map/ppermute | solution.py:695
  15.0 1.2 %collective-permute-start.4 = (f32[72,128]{1,0:T(8,128)S(1)}, f32[72,128]{1,0:T(8,128)S(1)}, u32[]{:S(2)}, u32[]{:S(2)}) collective-permute-start(f32[72,128]{1,0:T(8,128)S(1)} %get-tuple-element.50), channel_id=1, source_target_pairs={{0,16},{16,0},{32,48},{48,32},{64,80},{80,64},{96,112},{112,96},{1... | collective-permute-start | bytes 110600 | tf_op jit(solution)/shard_map/ppermute | solution.py:683
  16.2 3.1 %inner.1 = (f32[33,2,1024]{2,1,0:T(2,128)S(1)}, f32[2,72,128]{2,1,0:T(8,128)S(1)}) custom-call(bf16[16,32,1024]{2,1,0:T(8,128)(2,1)S(1)} %get-tuple-element.33.gas_ref, bf16[512,256]{1,0:T(8,128)(2,1)S(1)} %get-tuple-element.34.wide_ref, f32[5,8,128]{2,1,0:T(8,128)S(1)} %get-tuple-element.35.column_ref, f32[32,128]{1,0:T(8,128)S(1)} %get-tuple-element.36.solar_ref, ...), custom_call_target="tpu_custom_call" | custom-call | flops 2000000000 | bytes 4000000 | tf_op jit(solution)/shard_map/inner/pallas_call | solution.py:591
  19.3 0.0 collective-permute-done.3.far_got
  19.3 0.0 collective-permute-done.4.near_got
  19.3 0.8 %edge_side.1 = f32[33,2,1024]{2,1,0:T(2,128)} custom-call(f32[72,128]{1,0:T(8,128)S(1)} %collective-permute-done.3.far_got, f32[72,128]{1,0:T(8,128)S(1)} %collective-permute-done.4.near_got, f32[72,128]{1,0:T(8,128)S(1)} %get-tuple-element.51.first_ref, f32[72,128]{1,0:T(8,128)S(1)} %get-tuple-element.52.final_ref, ...), custom_call_target="tpu_custom_call" | custom-call | tf_op jit(solution)/shard_map/edge_side/pallas_call | solution.py:667
  (2 shorter events, 0.0 us)
Async XLA Ops:
  1.5 2.6 %collective-permute-start = (bf16[4,2,8,128]{3,2,1,0:T(8,128)(2,1)S(1)}, bf16[4,2,8,128]{3,2,1,0:T(8,128)(2,1)S(1)}, u32[]{:S(2)}, u32[]{:S(2)}) collective-permute-start(bf16[4,2,8,128]{3,2,1,0:T(8,128)(2,1)S(1)} %get-tuple-element.41), channel_id=1, source_target_pairs={{0,16},{16,0},{32,48},{48,32},{64,80},{80,64},{96,112},{112,96},{1... | collective-permute-start | bytes 49160 | tf_op jit(solution)/shard_map/ppermute | solution.py:683
  4.2 3.6 %collective-permute-start.1 = (bf16[2,2,8,128]{3,2,1,0:T(8,128)(2,1)S(1)}, bf16[2,2,8,128]{3,2,1,0:T(8,128)(2,1)S(1)}, u32[]{:S(2)}, u32[]{:S(2)}) collective-permute-start(bf16[2,2,8,128]{3,2,1,0:T(8,128)(2,1)S(1)} %get-tuple-element.46), channel_id=1, source_target_pairs={{0,32},{16,48},{32,0},{48,16},{64,96},{80,112},{96,64},{112,80},{1... | collective-permute-start | bytes 24584 | tf_op jit(solution)/shard_map/ppermute | solution.py:683
  7.8 5.8 %collective-permute-start.2 = (bf16[1,2,8,128]{3,2,1,0:T(8,128)(2,1)S(1)}, bf16[1,2,8,128]{3,2,1,0:T(8,128)(2,1)S(1)}, u32[]{:S(2)}, u32[]{:S(2)}) collective-permute-start(bf16[1,2,8,128]{3,2,1,0:T(8,128)(2,1)S(1)} %get-tuple-element.48), channel_id=1, source_target_pairs={{0,64},{16,80},{32,96},{48,112},{64,0},{80,16},{96,32},{112,48},{1... | collective-permute-start | bytes 12296 | tf_op jit(solution)/shard_map/ppermute | solution.py:683
  13.9 5.4 %collective-permute-start.3 = (f32[72,128]{1,0:T(8,128)S(1)}, f32[72,128]{1,0:T(8,128)S(1)}, u32[]{:S(2)}, u32[]{:S(2)}) collective-permute-start(f32[72,128]{1,0:T(8,128)S(1)} %get-tuple-element.49), channel_id=1, source_target_pairs={{0,4},{1,5},{2,6},{3,7},{4,0},{5,1},{6,2},{7,3},{8,12},{9,13},{10,... | collective-permute-start | bytes 110600 | tf_op jit(solution)/shard_map/ppermute | solution.py:695
  15.0 4.3 %collective-permute-start.4 = (f32[72,128]{1,0:T(8,128)S(1)}, f32[72,128]{1,0:T(8,128)S(1)}, u32[]{:S(2)}, u32[]{:S(2)}) collective-permute-start(f32[72,128]{1,0:T(8,128)S(1)} %get-tuple-element.50), channel_id=1, source_target_pairs={{0,16},{16,0},{32,48},{48,32},{64,80},{80,64},{96,112},{112,96},{1... | collective-permute-start | bytes 110600 | tf_op jit(solution)/shard_map/ppermute | solution.py:683

commit v7 on v5

--- a/solution.py
+++ b/solution.py
@@ -133,7 +133,7 @@
     column_ref[4] = lit * rising
 
 
-WINDOWS = ((0,), (NB - 1, 1), (2, 3, 4))
+WINDOWS = ((0,), (NB - 1, 1, 2), (3, 4))
 LATE = (5, 6)
 
 
@@ -553,7 +553,9 @@
     state_ref,
     flux_ref,
 ):
-    kept = {1: (coef_b.at[1], esum_b.at[1], state_b.at[1])}
+    kept = {}
+    for i, n in enumerate(WINDOWS[1]):
+        kept[n] = coef_b.at[i], esum_b.at[i], state_b.at[i]
     for i, n in enumerate(WINDOWS[2]):
         kept[n] = coef_c.at[i], esum_c.at[i], state_c.at[i]
     for i, n in enumerate(LATE):

time: 19.4 us -> 19.2 us (0.990)
  waiting for transfers between devices: 0.19 us -> 0.43 us
  Pallas kernels: 12 us -> 11.8 us
    ppermute x1, waiting for transfers between devices: 0.18 us -> 0.42 us  [beyond(): return lax.ppermute(x, ('blk', 'grp'), pairs)]
  transfers between devices with their start and end apart: 5 -> 5, of which waited for: 1 -> 1; matrix products, arithmetic and copies ran while one was open for 0% -> 0% of each run, Pallas kernels for 49% -> 48%
where the time goes in v7:
time: 19.2 us; the launch traced here: 19 us
  Pallas kernels  11.8 us (61%)
  starting transfers between devices  6.7 us (35%)
  waiting for transfers between devices  0.43 us (2%)
    ppermute x4, starting transfers between devices, exchange(): return lax.ppermute(x, 'blk', [(i, i ^ bit) for i in range(count)])  6.48 us
    pallas_call x3, Pallas kernels, down(): pl.pallas_call(down_kernel(blocks), in_specs=[IN_VMEM] * 4 + [UNREAD], ou...  6.19 us
    pallas_call x1, Pallas kernels, inner(): pl.pallas_call(inner_kernel, in_specs=[IN_VMEM] * 15, out_specs=[IN_VMEM]...  2.99 us
    pallas_call x1, Pallas kernels, surface(): pl.pallas_call(surface_kernel, in_specs=[IN_HBM] * 10, out_specs=[IN_VMEM...  1.53 us
    pallas_call x1, Pallas kernels, edge_side(): pl.pallas_call(edge_side_kernel, in_specs=[IN_VMEM] * 8, out_specs=IN_HBM...  0.81 us
    ppermute x1, waiting for transfers between devices, beyond(): return lax.ppermute(x, ('blk', 'grp'), pairs)  0.42 us
  transfers between devices with their start and end apart: 5, of which 1 were waited for; matrix products, arithmetic and copies ran while one was open for 0% of the time, Pallas kernels for 48%

profile of v7, /device:TPU:1, one launch (start us, length us, event | category | flops | bytes accessed | tf_op | source)
XLA Modules:
  0.0 19.0 jit_solution(15295914051206577061)
XLA Ops:
  0.0 1.5 %surface.1 = (bf16[4,2,8,128]{3,2,1,0:T(8,128)(2,1)S(1)}, bf16[4,2,8,128]{3,2,1,0:T(8,128)(2,1)S(1)}, bf16[16,32,1024]{2,1,0:T(8,128)(2,1)S(1)}, bf16[512,256]{1...) custom-call(s32[32,128]{1,0:T(8,128)} %bitcast.11, ...), custom_call_target="tpu_custom_call" | custom-call | tf_op jit(solution)/shard_map/surface/pallas_call | solution.py:217
  1.5 1.5 %collective-permute-start = (bf16[4,2,8,128]{3,2,1,0:T(8,128)(2,1)S(1)}, bf16[4,2,8,128]{3,2,1,0:T(8,128)(2,1)S(1)}, u32[]{:S(2)}, u32[]{:S(2)}) collective-permute-start(bf16[4,2,8,128]{3,2,1,0:T(8,128)(2,1)S(1)} %get-tuple-element.41), channel_id=1, source_target_pairs={{0,16},{16,0},{32,48},{48,32},{64,80},{80,64},{96,112},{112,96},{1... | collective-permute-start | bytes 49160 | tf_op jit(solution)/shard_map/ppermute | solution.py:685
  3.0 1.1 %down.3 = (f32[1,32,3,32,128]{4,3,2,1,0:T(8,128)S(1)}, f32[1,33,8,128]{3,2,1,0:T(8,128)S(1)}, f32[1,3,32,128]{3,2,1,0:T(8,128)S(1)}) custom-call(bf16[16,32,1024]{2,1,0:T(8,128)(2,1)S(1)} %get-tuple-element.33.gas_ref, bf16[512,256]{1,0:T(8,128)(2,1)S(1)} %get-tuple-element.34.wide_ref, f32[5,8,128]{2,1,0:T(8,128)S(1)} %get-tuple-element.35.column_ref, ...), custom_call_target="tpu_custom_call" | custom-call | flops 200000000 | bytes 4000000 | tf_op jit(solution)/shard_map/down/pallas_call | solution.py:410
  4.2 0.0 collective-permute-done.got_ref
  4.2 1.5 %collective-permute-start.1 = (bf16[2,2,8,128]{3,2,1,0:T(8,128)(2,1)S(1)}, bf16[2,2,8,128]{3,2,1,0:T(8,128)(2,1)S(1)}, u32[]{:S(2)}, u32[]{:S(2)}) collective-permute-start(bf16[2,2,8,128]{3,2,1,0:T(8,128)(2,1)S(1)} %get-tuple-element.46), channel_id=1, source_target_pairs={{0,32},{16,48},{32,0},{48,16},{64,96},{80,112},{96,64},{112,80},{1... | collective-permute-start | bytes 24584 | tf_op jit(solution)/shard_map/ppermute | solution.py:685
  5.6 3.0 %down.4 = (f32[3,32,3,32,128]{4,3,2,1,0:T(8,128)S(1)}, f32[3,33,8,128]{3,2,1,0:T(8,128)S(1)}, f32[3,3,32,128]{3,2,1,0:T(8,128)S(1)}) custom-call(bf16[16,32,1024]{2,1,0:T(8,128)(2,1)S(1)} %get-tuple-element.33.gas_ref, bf16[512,256]{1,0:T(8,128)(2,1)S(1)} %get-tuple-element.34.wide_ref, f32[5,8,128]{2,1,0:T(8,128)S(1)} %get-tuple-element.35.column_ref, ...), custom_call_target="tpu_custom_call" | custom-call | flops 600000000 | bytes 4000000 | tf_op jit(solution)/shard_map/down/pallas_call | solution.py:410
  8.7 0.0 collective-permute-done.1.got_ref
  8.7 2.7 %collective-permute-start.2 = (bf16[1,2,8,128]{3,2,1,0:T(8,128)(2,1)S(1)}, bf16[1,2,8,128]{3,2,1,0:T(8,128)(2,1)S(1)}, u32[]{:S(2)}, u32[]{:S(2)}) collective-permute-start(bf16[1,2,8,128]{3,2,1,0:T(8,128)(2,1)S(1)} %get-tuple-element.48), channel_id=1, source_target_pairs={{0,64},{16,80},{32,96},{48,112},{64,0},{80,16},{96,32},{112,48},{1... | collective-permute-start | bytes 12296 | tf_op jit(solution)/shard_map/ppermute | solution.py:685
  11.4 2.1 %down.5 = (f32[2,32,3,32,128]{4,3,2,1,0:T(8,128)S(1)}, f32[2,33,8,128]{3,2,1,0:T(8,128)S(1)}, f32[2,3,32,128]{3,2,1,0:T(8,128)S(1)}) custom-call(bf16[16,32,1024]{2,1,0:T(8,128)(2,1)S(1)} %get-tuple-element.33.gas_ref, bf16[512,256]{1,0:T(8,128)(2,1)S(1)} %get-tuple-element.34.wide_ref, f32[5,8,128]{2,1,0:T(8,128)S(1)} %get-tuple-element.35.column_ref, ...), custom_call_target="tpu_custom_call" | custom-call | flops 400000000 | bytes 4000000 | tf_op jit(solution)/shard_map/down/pallas_call | solution.py:410
  13.5 0.0 collective-permute-done.2.got_ref
  13.5 0.3 %up.1 = (f32[72,128]{1,0:T(8,128)S(1)}, f32[72,128]{1,0:T(8,128)S(1)}, f32[72,128]{1,0:T(8,128)S(1)}, f32[72,128]{1,0:T(8,128)S(1)}, f32[2,8,128]{2,1,0:T(8,128)S(1)}) custom-call(f32[1,32,3,32,128]{4,3,2,1,0:T(8,128)S(1)} %get-tuple-element.38.coef_a, f32[1,33,8,128]{3,2,1,0:T(8,128)S(1)} %get-tuple-element.39.esum_a, ...), custom_call_target="tpu_custom_call" | custom-call | flops 4000000 | bytes 4000000 | tf_op jit(solution)/shard_map/up/pallas_call | solution.py:462
  13.8 0.8 %collective-permute-start.3 = (f32[72,128]{1,0:T(8,128)S(1)}, f32[72,128]{1,0:T(8,128)S(1)}, u32[]{:S(2)}, u32[]{:S(2)}) collective-permute-start(f32[72,128]{1,0:T(8,128)S(1)} %get-tuple-element.49), channel_id=1, source_target_pairs={{0,16},{16,0},{32,48},{48,32},{64,80},{80,64},{96,112},{112,96},{1... | collective-permute-start | bytes 110600 | tf_op jit(solution)/shard_map/ppermute | solution.py:685
  14.6 0.2 %collective-permute-start.4 = (f32[72,128]{1,0:T(8,128)S(1)}, f32[72,128]{1,0:T(8,128)S(1)}, u32[]{:S(2)}, u32[]{:S(2)}) collective-permute-start(f32[72,128]{1,0:T(8,128)S(1)} %get-tuple-element.50), channel_id=1, source_target_pairs={{0,4},{1,5},{2,6},{3,7},{4,0},{5,1},{6,2},{7,3},{8,12},{9,13},{10,... | collective-permute-start | bytes 110600 | tf_op jit(solution)/shard_map/ppermute | solution.py:697
  14.8 3.0 %inner.1 = (f32[33,2,1024]{2,1,0:T(2,128)S(1)}, f32[2,72,128]{2,1,0:T(8,128)S(1)}) custom-call(bf16[16,32,1024]{2,1,0:T(8,128)(2,1)S(1)} %get-tuple-element.33.gas_ref, bf16[512,256]{1,0:T(8,128)(2,1)S(1)} %get-tuple-element.34.wide_ref, f32[5,8,128]{2,1,0:T(8,128)S(1)} %get-tuple-element.35.column_ref, f32[32,128]{1,0:T(8,128)S(1)} %get-tuple-element.36.solar_ref, ...), custom_call_target="tpu_custom_call" | custom-call | flops 2000000000 | bytes 4000000 | tf_op jit(solution)/shard_map/inner/pallas_call | solution.py:593
  17.8 0.0 collective-permute-done.3.near_got
  17.8 0.4 %collective-permute-done.4.far_got = f32[72,128]{1,0:T(8,128)S(1)} collective-permute-done((f32[72,128]{1,0:T(8,128)S(1)}, f32[72,128]{1,0:T(8,128)S(1)}, u32[]{:S(2)}, u32[]{:S(2)}) %collective-permute-start.4) | collective-permute-done | bytes 36896 | tf_op jit(solution)/shard_map/ppermute | solution.py:697
  18.2 0.8 %edge_side.1 = f32[33,2,1024]{2,1,0:T(2,128)} custom-call(f32[72,128]{1,0:T(8,128)S(1)} %collective-permute-done.3.near_got, f32[72,128]{1,0:T(8,128)S(1)} %collective-permute-done.4.far_got, f32[72,128]{1,0:T(8,128)S(1)} %get-tuple-element.51.first_ref, f32[72,128]{1,0:T(8,128)S(1)} %get-tuple-element.52.final_ref, ...), custom_call_target="tpu_custom_call" | custom-call | tf_op jit(solution)/shard_map/edge_side/pallas_call | solution.py:669
  (2 shorter events, 0.0 us)
Async XLA Ops:
  1.5 2.6 %collective-permute-start = (bf16[4,2,8,128]{3,2,1,0:T(8,128)(2,1)S(1)}, bf16[4,2,8,128]{3,2,1,0:T(8,128)(2,1)S(1)}, u32[]{:S(2)}, u32[]{:S(2)}) collective-permute-start(bf16[4,2,8,128]{3,2,1,0:T(8,128)(2,1)S(1)} %get-tuple-element.41), channel_id=1, source_target_pairs={{0,16},{16,0},{32,48},{48,32},{64,80},{80,64},{96,112},{112,96},{1... | collective-permute-start | bytes 49160 | tf_op jit(solution)/shard_map/ppermute | solution.py:685
  4.2 4.5 %collective-permute-start.1 = (bf16[2,2,8,128]{3,2,1,0:T(8,128)(2,1)S(1)}, bf16[2,2,8,128]{3,2,1,0:T(8,128)(2,1)S(1)}, u32[]{:S(2)}, u32[]{:S(2)}) collective-permute-start(bf16[2,2,8,128]{3,2,1,0:T(8,128)(2,1)S(1)} %get-tuple-element.46), channel_id=1, source_target_pairs={{0,32},{16,48},{32,0},{48,16},{64,96},{80,112},{96,64},{112,80},{1... | collective-permute-start | bytes 24584 | tf_op jit(solution)/shard_map/ppermute | solution.py:685
  8.7 4.8 %collective-permute-start.2 = (bf16[1,2,8,128]{3,2,1,0:T(8,128)(2,1)S(1)}, bf16[1,2,8,128]{3,2,1,0:T(8,128)(2,1)S(1)}, u32[]{:S(2)}, u32[]{:S(2)}) collective-permute-start(bf16[1,2,8,128]{3,2,1,0:T(8,128)(2,1)S(1)} %get-tuple-element.48), channel_id=1, source_target_pairs={{0,64},{16,80},{32,96},{48,112},{64,0},{80,16},{96,32},{112,48},{1... | collective-permute-start | bytes 12296 | tf_op jit(solution)/shard_map/ppermute | solution.py:685
  13.8 4.0 %collective-permute-start.3 = (f32[72,128]{1,0:T(8,128)S(1)}, f32[72,128]{1,0:T(8,128)S(1)}, u32[]{:S(2)}, u32[]{:S(2)}) collective-permute-start(f32[72,128]{1,0:T(8,128)S(1)} %get-tuple-element.49), channel_id=1, source_target_pairs={{0,16},{16,0},{32,48},{48,32},{64,80},{80,64},{96,112},{112,96},{1... | collective-permute-start | bytes 110600 | tf_op jit(solution)/shard_map/ppermute | solution.py:685
  14.6 3.7 %collective-permute-start.4 = (f32[72,128]{1,0:T(8,128)S(1)}, f32[72,128]{1,0:T(8,128)S(1)}, u32[]{:S(2)}, u32[]{:S(2)}) collective-permute-start(f32[72,128]{1,0:T(8,128)S(1)} %get-tuple-element.50), channel_id=1, source_target_pairs={{0,4},{1,5},{2,6},{3,7},{4,0},{5,1},{6,2},{7,3},{8,12},{9,13},{10,... | collective-permute-start | bytes 110600 | tf_op jit(solution)/shard_map/ppermute | solution.py:697

commit v8 on v7

--- a/solution.py
+++ b/solution.py
@@ -89,6 +89,7 @@
     here = area > 0.0
     safe = jnp.where(here, area, 1.0)
     owner = (parent_ref[:, 0:1] >> 7) ^ (mine * NB)
+    owner = owner ^ ((owner >> 1) & (2 * NB))
     slot = lax.broadcasted_iota(jnp.int32, (FINE_BLOCKS, NBLK * NB), 1)
     where_to = jnp.where(owner == slot, 1.0, 0.0).astype(BF16)
     placed = []
@@ -680,9 +681,12 @@
     )(near_got, far_got, first, final, partial, neighbours, side_weight, full)
 
 
-def exchange(x, bit):
+PARTNERS = (1, 2, 6)
+
+
+def exchange(x, mask):
     count = lax.axis_size("blk")
-    return lax.ppermute(x, "blk", [(i, i ^ bit) for i in range(count)])
+    return lax.ppermute(x, "blk", [(i, i ^ mask) for i in range(count)])
 
 
 def beyond(x):
@@ -723,7 +727,7 @@
     )
     parts = []
     for i, blocks in enumerate(WINDOWS):
-        got = exchange(send, 1 << i)
+        got = exchange(send, PARTNERS[i])
         parts.append(down(blocks, gas, wide, column, solar, keep))
         if i < 2:
             send, keep = merge(keep, got, parts[-1][2])

time: 19.2 us -> 18.9 us (0.984)
  starting transfers between devices: 6.7 us -> 6.18 us
  waiting for transfers between devices: 0.43 us -> 0.65 us
    ppermute x4, starting transfers between devices: 6.48 us -> 6.18 us  [exchange(): return lax.ppermute(x, 'blk', [(i, i ^ mask) for i in range(count)])]
    ppermute x1, starting transfers between devices: 0.23 us -> 0.01 us  [beyond(): return lax.ppermute(x, ('blk', 'grp'), pairs)]
    ppermute x1, waiting for transfers between devices: 0.42 us -> 0.64 us  [beyond(): return lax.ppermute(x, ('blk', 'grp'), pairs)]
  transfers between devices with their start and end apart: 5 -> 5, of which waited for: 1 -> 1; matrix products, arithmetic and copies ran while one was open for 0% -> 0% of each run, Pallas kernels for 48% -> 49%
where the time goes in v8:
time: 18.9 us; the launch traced here: 18.8 us
  Pallas kernels  11.8 us (62%)
  starting transfers between devices  6.18 us (33%)
  waiting for transfers between devices  0.65 us (3%)
    pallas_call x3, Pallas kernels, down(): pl.pallas_call(down_kernel(blocks), in_specs=[IN_VMEM] * 4 + [UNREAD], ou...  6.19 us
    ppermute x4, starting transfers between devices, exchange(): return lax.ppermute(x, 'blk', [(i, i ^ mask) for i in range(count)])  6.18 us
    pallas_call x1, Pallas kernels, inner(): pl.pallas_call(inner_kernel, in_specs=[IN_VMEM] * 15, out_specs=[IN_VMEM]...  3 us
    pallas_call x1, Pallas kernels, surface(): pl.pallas_call(surface_kernel, in_specs=[IN_HBM] * 10, out_specs=[IN_VMEM...  1.53 us
    pallas_call x1, Pallas kernels, edge_side(): pl.pallas_call(edge_side_kernel, in_specs=[IN_VMEM] * 8, out_specs=IN_HBM...  0.81 us
    ppermute x1, waiting for transfers between devices, beyond(): return lax.ppermute(x, ('blk', 'grp'), pairs)  0.64 us
  transfers between devices with their start and end apart: 5, of which 1 were waited for; matrix products, arithmetic and copies ran while one was open for 0% of the time, Pallas kernels for 49%

profile of v8, /device:TPU:1, one launch (start us, length us, event | category | flops | bytes accessed | tf_op | source)
XLA Modules:
  0.0 18.8 jit_solution(16267007936001665611)
XLA Ops:
  0.0 1.5 %surface.1 = (bf16[4,2,8,128]{3,2,1,0:T(8,128)(2,1)S(1)}, bf16[4,2,8,128]{3,2,1,0:T(8,128)(2,1)S(1)}, bf16[16,32,1024]{2,1,0:T(8,128)(2,1)S(1)}, bf16[512,256]{1...) custom-call(s32[32,128]{1,0:T(8,128)} %bitcast.11, ...), custom_call_target="tpu_custom_call" | custom-call | tf_op jit(solution)/shard_map/surface/pallas_call | solution.py:218
  1.5 1.5 %collective-permute-start = (bf16[4,2,8,128]{3,2,1,0:T(8,128)(2,1)S(1)}, bf16[4,2,8,128]{3,2,1,0:T(8,128)(2,1)S(1)}, u32[]{:S(2)}, u32[]{:S(2)}) collective-permute-start(bf16[4,2,8,128]{3,2,1,0:T(8,128)(2,1)S(1)} %get-tuple-element.41), channel_id=1, source_target_pairs={{0,16},{16,0},{32,48},{48,32},{64,80},{80,64},{96,112},{112,96},{1... | collective-permute-start | bytes 49160 | tf_op jit(solution)/shard_map/ppermute | solution.py:689
  3.0 1.1 %down.3 = (f32[1,32,3,32,128]{4,3,2,1,0:T(8,128)S(1)}, f32[1,33,8,128]{3,2,1,0:T(8,128)S(1)}, f32[1,3,32,128]{3,2,1,0:T(8,128)S(1)}) custom-call(bf16[16,32,1024]{2,1,0:T(8,128)(2,1)S(1)} %get-tuple-element.33.gas_ref, bf16[512,256]{1,0:T(8,128)(2,1)S(1)} %get-tuple-element.34.wide_ref, f32[5,8,128]{2,1,0:T(8,128)S(1)} %get-tuple-element.35.column_ref, ...), custom_call_target="tpu_custom_call" | custom-call | flops 200000000 | bytes 4000000 | tf_op jit(solution)/shard_map/down/pallas_call | solution.py:411
  4.2 0.0 collective-permute-done.got_ref
  4.2 1.5 %collective-permute-start.1 = (bf16[2,2,8,128]{3,2,1,0:T(8,128)(2,1)S(1)}, bf16[2,2,8,128]{3,2,1,0:T(8,128)(2,1)S(1)}, u32[]{:S(2)}, u32[]{:S(2)}) collective-permute-start(bf16[2,2,8,128]{3,2,1,0:T(8,128)(2,1)S(1)} %get-tuple-element.46), channel_id=1, source_target_pairs={{0,32},{16,48},{32,0},{48,16},{64,96},{80,112},{96,64},{112,80},{1... | collective-permute-start | bytes 24584 | tf_op jit(solution)/shard_map/ppermute | solution.py:689
  5.6 3.0 %down.4 = (f32[3,32,3,32,128]{4,3,2,1,0:T(8,128)S(1)}, f32[3,33,8,128]{3,2,1,0:T(8,128)S(1)}, f32[3,3,32,128]{3,2,1,0:T(8,128)S(1)}) custom-call(bf16[16,32,1024]{2,1,0:T(8,128)(2,1)S(1)} %get-tuple-element.33.gas_ref, bf16[512,256]{1,0:T(8,128)(2,1)S(1)} %get-tuple-element.34.wide_ref, f32[5,8,128]{2,1,0:T(8,128)S(1)} %get-tuple-element.35.column_ref, ...), custom_call_target="tpu_custom_call" | custom-call | flops 600000000 | bytes 4000000 | tf_op jit(solution)/shard_map/down/pallas_call | solution.py:411
  8.7 0.0 collective-permute-done.1.got_ref
  8.7 2.0 %collective-permute-start.2 = (bf16[1,2,8,128]{3,2,1,0:T(8,128)(2,1)S(1)}, bf16[1,2,8,128]{3,2,1,0:T(8,128)(2,1)S(1)}, u32[]{:S(2)}, u32[]{:S(2)}) collective-permute-start(bf16[1,2,8,128]{3,2,1,0:T(8,128)(2,1)S(1)} %get-tuple-element.48), channel_id=1, source_target_pairs={{0,96},{16,112},{32,64},{48,80},{64,32},{80,48},{96,0},{112,16},{1... | collective-permute-start | bytes 12296 | tf_op jit(solution)/shard_map/ppermute | solution.py:689
  10.7 2.1 %down.5 = (f32[2,32,3,32,128]{4,3,2,1,0:T(8,128)S(1)}, f32[2,33,8,128]{3,2,1,0:T(8,128)S(1)}, f32[2,3,32,128]{3,2,1,0:T(8,128)S(1)}) custom-call(bf16[16,32,1024]{2,1,0:T(8,128)(2,1)S(1)} %get-tuple-element.33.gas_ref, bf16[512,256]{1,0:T(8,128)(2,1)S(1)} %get-tuple-element.34.wide_ref, f32[5,8,128]{2,1,0:T(8,128)S(1)} %get-tuple-element.35.column_ref, ...), custom_call_target="tpu_custom_call" | custom-call | flops 400000000 | bytes 4000000 | tf_op jit(solution)/shard_map/down/pallas_call | solution.py:411
  12.7 0.0 collective-permute-done.2.got_ref
  12.7 0.3 %up.1 = (f32[72,128]{1,0:T(8,128)S(1)}, f32[72,128]{1,0:T(8,128)S(1)}, f32[72,128]{1,0:T(8,128)S(1)}, f32[72,128]{1,0:T(8,128)S(1)}, f32[2,8,128]{2,1,0:T(8,128)S(1)}) custom-call(f32[1,32,3,32,128]{4,3,2,1,0:T(8,128)S(1)} %get-tuple-element.38.coef_a, f32[1,33,8,128]{3,2,1,0:T(8,128)S(1)} %get-tuple-element.39.esum_a, ...), custom_call_target="tpu_custom_call" | custom-call | flops 4000000 | bytes 4000000 | tf_op jit(solution)/shard_map/up/pallas_call | solution.py:463
  13.0 1.2 %collective-permute-start.3 = (f32[72,128]{1,0:T(8,128)S(1)}, f32[72,128]{1,0:T(8,128)S(1)}, u32[]{:S(2)}, u32[]{:S(2)}) collective-permute-start(f32[72,128]{1,0:T(8,128)S(1)} %get-tuple-element.49), channel_id=1, source_target_pairs={{0,16},{16,0},{32,48},{48,32},{64,80},{80,64},{96,112},{112,96},{1... | collective-permute-start | bytes 110600 | tf_op jit(solution)/shard_map/ppermute | solution.py:689
  14.3 0.0 collective-permute-start.4
  14.3 3.0 %inner.1 = (f32[33,2,1024]{2,1,0:T(2,128)S(1)}, f32[2,72,128]{2,1,0:T(8,128)S(1)}) custom-call(bf16[16,32,1024]{2,1,0:T(8,128)(2,1)S(1)} %get-tuple-element.33.gas_ref, bf16[512,256]{1,0:T(8,128)(2,1)S(1)} %get-tuple-element.34.wide_ref, f32[5,8,128]{2,1,0:T(8,128)S(1)} %get-tuple-element.35.column_ref, f32[32,128]{1,0:T(8,128)S(1)} %get-tuple-element.36.solar_ref, ...), custom_call_target="tpu_custom_call" | custom-call | flops 2000000000 | bytes 4000000 | tf_op jit(solution)/shard_map/inner/pallas_call | solution.py:594
  17.3 0.0 collective-permute-done.3.near_got
  17.3 0.6 %collective-permute-done.4.far_got = f32[72,128]{1,0:T(8,128)S(1)} collective-permute-done((f32[72,128]{1,0:T(8,128)S(1)}, f32[72,128]{1,0:T(8,128)S(1)}, u32[]{:S(2)}, u32[]{:S(2)}) %collective-permute-start.4) | collective-permute-done | bytes 36896 | tf_op jit(solution)/shard_map/ppermute | solution.py:701
  17.9 0.8 %edge_side.1 = f32[33,2,1024]{2,1,0:T(2,128)} custom-call(f32[72,128]{1,0:T(8,128)S(1)} %collective-permute-done.3.near_got, f32[72,128]{1,0:T(8,128)S(1)} %collective-permute-done.4.far_got, f32[72,128]{1,0:T(8,128)S(1)} %get-tuple-element.51.first_ref, f32[72,128]{1,0:T(8,128)S(1)} %get-tuple-element.52.final_ref, ...), custom_call_target="tpu_custom_call" | custom-call | tf_op jit(solution)/shard_map/edge_side/pallas_call | solution.py:670
  (2 shorter events, 0.0 us)
Async XLA Ops:
  1.5 2.6 %collective-permute-start = (bf16[4,2,8,128]{3,2,1,0:T(8,128)(2,1)S(1)}, bf16[4,2,8,128]{3,2,1,0:T(8,128)(2,1)S(1)}, u32[]{:S(2)}, u32[]{:S(2)}) collective-permute-start(bf16[4,2,8,128]{3,2,1,0:T(8,128)(2,1)S(1)} %get-tuple-element.41), channel_id=1, source_target_pairs={{0,16},{16,0},{32,48},{48,32},{64,80},{80,64},{96,112},{112,96},{1... | collective-permute-start | bytes 49160 | tf_op jit(solution)/shard_map/ppermute | solution.py:689
  4.2 4.5 %collective-permute-start.1 = (bf16[2,2,8,128]{3,2,1,0:T(8,128)(2,1)S(1)}, bf16[2,2,8,128]{3,2,1,0:T(8,128)(2,1)S(1)}, u32[]{:S(2)}, u32[]{:S(2)}) collective-permute-start(bf16[2,2,8,128]{3,2,1,0:T(8,128)(2,1)S(1)} %get-tuple-element.46), channel_id=1, source_target_pairs={{0,32},{16,48},{32,0},{48,16},{64,96},{80,112},{96,64},{112,80},{1... | collective-permute-start | bytes 24584 | tf_op jit(solution)/shard_map/ppermute | solution.py:689
  8.7 4.0 %collective-permute-start.2 = (bf16[1,2,8,128]{3,2,1,0:T(8,128)(2,1)S(1)}, bf16[1,2,8,128]{3,2,1,0:T(8,128)(2,1)S(1)}, u32[]{:S(2)}, u32[]{:S(2)}) collective-permute-start(bf16[1,2,8,128]{3,2,1,0:T(8,128)(2,1)S(1)} %get-tuple-element.48), channel_id=1, source_target_pairs={{0,96},{16,112},{32,64},{48,80},{64,32},{80,48},{96,0},{112,16},{1... | collective-permute-start | bytes 12296 | tf_op jit(solution)/shard_map/ppermute | solution.py:689
  13.0 4.2 %collective-permute-start.3 = (f32[72,128]{1,0:T(8,128)S(1)}, f32[72,128]{1,0:T(8,128)S(1)}, u32[]{:S(2)}, u32[]{:S(2)}) collective-permute-start(f32[72,128]{1,0:T(8,128)S(1)} %get-tuple-element.49), channel_id=1, source_target_pairs={{0,16},{16,0},{32,48},{48,32},{64,80},{80,64},{96,112},{112,96},{1... | collective-permute-start | bytes 110600 | tf_op jit(solution)/shard_map/ppermute | solution.py:689
  14.3 3.7 %collective-permute-start.4 = (f32[72,128]{1,0:T(8,128)S(1)}, f32[72,128]{1,0:T(8,128)S(1)}, u32[]{:S(2)}, u32[]{:S(2)}) collective-permute-start(f32[72,128]{1,0:T(8,128)S(1)} %get-tuple-element.50), channel_id=1, source_target_pairs={{0,4},{1,5},{2,6},{3,7},{4,0},{5,1},{6,2},{7,3},{8,12},{9,13},{10,... | collective-permute-start | bytes 110600 | tf_op jit(solution)/shard_map/ppermute | solution.py:701

commit v9 on v8

--- a/solution.py
+++ b/solution.py
@@ -623,8 +623,8 @@
 
 
 def edge_side_kernel(
+    far_got,
     near_got,
-    far_got,
     first_ref,
     final_ref,
     partial_ref,
@@ -666,7 +666,7 @@
         started.wait()
 
 
-def edge_side(near_got, far_got, first, final, partial, neighbours, side_weight, full):
+def edge_side(far_got, near_got, first, final, partial, neighbours, side_weight, full):
     return pl.pallas_call(
         edge_side_kernel,
         in_specs=[IN_VMEM] * 8,
@@ -678,7 +678,7 @@
         ],
         compiler_params=params(4),
         name="edge_side",
-    )(near_got, far_got, first, final, partial, neighbours, side_weight, full)
+    )(far_got, near_got, first, final, partial, neighbours, side_weight, full)
 
 
 PARTNERS = (1, 2, 6)
@@ -690,15 +690,9 @@
 
 
 def beyond(x):
-    count, bands = lax.axis_size("blk"), lax.axis_size("grp")
-    pairs = []
-    for i in range(count):
-        for band in range(bands):
-            if i in (0, count - 1):
-                pairs.append((i * bands + band, i * bands + (band ^ 4)))
-            else:
-                pairs.append((i * bands + band, (i + (1 if i % 2 else -1)) * bands + band))
-    return lax.ppermute(x, ("blk", "grp"), pairs)
+    count = lax.axis_size("blk")
+    pairs = [(i, (i + (1 if i % 2 else -1)) % count) for i in range(count)]
+    return lax.ppermute(x, "blk", pairs)
 
 
 def local(
@@ -737,7 +731,7 @@
     full, partial = inner(
         gas, wide, column, solar, albedo, first, final, parts, beside, weights
     )
-    done = edge_side(near_got, far_got, first, final, partial, beside, weights, full)
+    done = edge_side(far_got, near_got, first, final, partial, beside, weights, full)
     return done.transpose(1, 0, 2)
 
 

time: 18.9 us -> 19.1 us (1.011)
  starting transfers between devices: 6.18 us -> 7.01 us
  waiting for transfers between devices: 0.65 us -> 0.01 us
    ppermute x1, starting transfers between devices: 0.01 us -> 0.96 us  [beyond(): return lax.ppermute(x, 'blk', pairs)]
    ppermute x1, waiting for transfers between devices: 0.64 us -> 0.01 us  [beyond(): return lax.ppermute(x, 'blk', pairs)]
  transfers between devices with their start and end apart: 5 -> 5, of which waited for: 1 -> 0; matrix products, arithmetic and copies ran while one was open for 0% -> 0% of each run, Pallas kernels for 49% -> 48%
where the time goes in v9:
time: 19.1 us; the launch traced here: 19 us
  Pallas kernels  11.9 us (62%)
  starting transfers between devices  7.01 us (37%)
    pallas_call x3, Pallas kernels, down(): pl.pallas_call(down_kernel(blocks), in_specs=[IN_VMEM] * 4 + [UNREAD], ou...  6.19 us
    ppermute x4, starting transfers between devices, exchange(): return lax.ppermute(x, 'blk', [(i, i ^ mask) for i in range(count)])  6.05 us
    pallas_call x1, Pallas kernels, inner(): pl.pallas_call(inner_kernel, in_specs=[IN_VMEM] * 15, out_specs=[IN_VMEM]...  3 us
    pallas_call x1, Pallas kernels, surface(): pl.pallas_call(surface_kernel, in_specs=[IN_HBM] * 10, out_specs=[IN_VMEM...  1.53 us
    ppermute x1, starting transfers between devices, beyond(): return lax.ppermute(x, 'blk', pairs)  0.96 us
    pallas_call x1, Pallas kernels, edge_side(): pl.pallas_call(edge_side_kernel, in_specs=[IN_VMEM] * 8, out_specs=IN_HBM...  0.82 us
  transfers between devices with their start and end apart: 5, of which 0 were waited for; matrix products, arithmetic and copies ran while one was open for 0% of the time, Pallas kernels for 48%

profile of v9, /device:TPU:1, one launch (start us, length us, event | category | flops | bytes accessed | tf_op | source)
XLA Modules:
  0.0 19.0 jit_solution(8984518686596066453)
XLA Ops:
  0.0 1.5 %surface.1 = (bf16[4,2,8,128]{3,2,1,0:T(8,128)(2,1)S(1)}, bf16[4,2,8,128]{3,2,1,0:T(8,128)(2,1)S(1)}, bf16[16,32,1024]{2,1,0:T(8,128)(2,1)S(1)}, bf16[512,256]{1...) custom-call(s32[32,128]{1,0:T(8,128)} %bitcast.11, ...), custom_call_target="tpu_custom_call" | custom-call | tf_op jit(solution)/shard_map/surface/pallas_call | solution.py:218
  1.5 1.5 %collective-permute-start = (bf16[4,2,8,128]{3,2,1,0:T(8,128)(2,1)S(1)}, bf16[4,2,8,128]{3,2,1,0:T(8,128)(2,1)S(1)}, u32[]{:S(2)}, u32[]{:S(2)}) collective-permute-start(bf16[4,2,8,128]{3,2,1,0:T(8,128)(2,1)S(1)} %get-tuple-element.41), channel_id=1, source_target_pairs={{0,16},{16,0},{32,48},{48,32},{64,80},{80,64},{96,112},{112,96},{1... | collective-permute-start | bytes 49160 | tf_op jit(solution)/shard_map/ppermute | solution.py:689
  3.0 1.1 %down.3 = (f32[1,32,3,32,128]{4,3,2,1,0:T(8,128)S(1)}, f32[1,33,8,128]{3,2,1,0:T(8,128)S(1)}, f32[1,3,32,128]{3,2,1,0:T(8,128)S(1)}) custom-call(bf16[16,32,1024]{2,1,0:T(8,128)(2,1)S(1)} %get-tuple-element.33.gas_ref, bf16[512,256]{1,0:T(8,128)(2,1)S(1)} %get-tuple-element.34.wide_ref, f32[5,8,128]{2,1,0:T(8,128)S(1)} %get-tuple-element.35.column_ref, ...), custom_call_target="tpu_custom_call" | custom-call | flops 200000000 | bytes 4000000 | tf_op jit(solution)/shard_map/down/pallas_call | solution.py:411
  4.2 0.0 collective-permute-done.got_ref
  4.2 1.5 %collective-permute-start.1 = (bf16[2,2,8,128]{3,2,1,0:T(8,128)(2,1)S(1)}, bf16[2,2,8,128]{3,2,1,0:T(8,128)(2,1)S(1)}, u32[]{:S(2)}, u32[]{:S(2)}) collective-permute-start(bf16[2,2,8,128]{3,2,1,0:T(8,128)(2,1)S(1)} %get-tuple-element.46), channel_id=1, source_target_pairs={{0,32},{16,48},{32,0},{48,16},{64,96},{80,112},{96,64},{112,80},{1... | collective-permute-start | bytes 24584 | tf_op jit(solution)/shard_map/ppermute | solution.py:689
  5.6 3.0 %down.4 = (f32[3,32,3,32,128]{4,3,2,1,0:T(8,128)S(1)}, f32[3,33,8,128]{3,2,1,0:T(8,128)S(1)}, f32[3,3,32,128]{3,2,1,0:T(8,128)S(1)}) custom-call(bf16[16,32,1024]{2,1,0:T(8,128)(2,1)S(1)} %get-tuple-element.33.gas_ref, bf16[512,256]{1,0:T(8,128)(2,1)S(1)} %get-tuple-element.34.wide_ref, f32[5,8,128]{2,1,0:T(8,128)S(1)} %get-tuple-element.35.column_ref, ...), custom_call_target="tpu_custom_call" | custom-call | flops 600000000 | bytes 4000000 | tf_op jit(solution)/shard_map/down/pallas_call | solution.py:411
  8.7 0.0 collective-permute-done.1.got_ref
  8.7 2.0 %collective-permute-start.2 = (bf16[1,2,8,128]{3,2,1,0:T(8,128)(2,1)S(1)}, bf16[1,2,8,128]{3,2,1,0:T(8,128)(2,1)S(1)}, u32[]{:S(2)}, u32[]{:S(2)}) collective-permute-start(bf16[1,2,8,128]{3,2,1,0:T(8,128)(2,1)S(1)} %get-tuple-element.48), channel_id=1, source_target_pairs={{0,96},{16,112},{32,64},{48,80},{64,32},{80,48},{96,0},{112,16},{1... | collective-permute-start | bytes 12296 | tf_op jit(solution)/shard_map/ppermute | solution.py:689
  10.7 2.1 %down.5 = (f32[2,32,3,32,128]{4,3,2,1,0:T(8,128)S(1)}, f32[2,33,8,128]{3,2,1,0:T(8,128)S(1)}, f32[2,3,32,128]{3,2,1,0:T(8,128)S(1)}) custom-call(bf16[16,32,1024]{2,1,0:T(8,128)(2,1)S(1)} %get-tuple-element.33.gas_ref, bf16[512,256]{1,0:T(8,128)(2,1)S(1)} %get-tuple-element.34.wide_ref, f32[5,8,128]{2,1,0:T(8,128)S(1)} %get-tuple-element.35.column_ref, ...), custom_call_target="tpu_custom_call" | custom-call | flops 400000000 | bytes 4000000 | tf_op jit(solution)/shard_map/down/pallas_call | solution.py:411
  12.7 0.0 collective-permute-done.2.got_ref
  12.7 0.3 %up.1 = (f32[72,128]{1,0:T(8,128)S(1)}, f32[72,128]{1,0:T(8,128)S(1)}, f32[72,128]{1,0:T(8,128)S(1)}, f32[72,128]{1,0:T(8,128)S(1)}, f32[2,8,128]{2,1,0:T(8,128)S(1)}) custom-call(f32[1,32,3,32,128]{4,3,2,1,0:T(8,128)S(1)} %get-tuple-element.38.coef_a, f32[1,33,8,128]{3,2,1,0:T(8,128)S(1)} %get-tuple-element.39.esum_a, ...), custom_call_target="tpu_custom_call" | custom-call | flops 4000000 | bytes 4000000 | tf_op jit(solution)/shard_map/up/pallas_call | solution.py:463
  13.0 1.0 %collective-permute-start.3 = (f32[72,128]{1,0:T(8,128)S(1)}, f32[72,128]{1,0:T(8,128)S(1)}, u32[]{:S(2)}, u32[]{:S(2)}) collective-permute-start(f32[72,128]{1,0:T(8,128)S(1)} %get-tuple-element.49), channel_id=1, source_target_pairs={{0,112},{16,32},{32,16},{48,64},{64,48},{80,96},{96,80},{112,0},{1... | collective-permute-start | bytes 110600 | tf_op jit(solution)/shard_map/ppermute | solution.py:695
  14.0 1.1 %collective-permute-start.4 = (f32[72,128]{1,0:T(8,128)S(1)}, f32[72,128]{1,0:T(8,128)S(1)}, u32[]{:S(2)}, u32[]{:S(2)}) collective-permute-start(f32[72,128]{1,0:T(8,128)S(1)} %get-tuple-element.50), channel_id=1, source_target_pairs={{0,16},{16,0},{32,48},{48,32},{64,80},{80,64},{96,112},{112,96},{1... | collective-permute-start | bytes 110600 | tf_op jit(solution)/shard_map/ppermute | solution.py:689
  15.1 3.0 %inner.1 = (f32[33,2,1024]{2,1,0:T(2,128)S(1)}, f32[2,72,128]{2,1,0:T(8,128)S(1)}) custom-call(bf16[16,32,1024]{2,1,0:T(8,128)(2,1)S(1)} %get-tuple-element.33.gas_ref, bf16[512,256]{1,0:T(8,128)(2,1)S(1)} %get-tuple-element.34.wide_ref, f32[5,8,128]{2,1,0:T(8,128)S(1)} %get-tuple-element.35.column_ref, f32[32,128]{1,0:T(8,128)S(1)} %get-tuple-element.36.solar_ref, ...), custom_call_target="tpu_custom_call" | custom-call | flops 2000000000 | bytes 4000000 | tf_op jit(solution)/shard_map/inner/pallas_call | solution.py:594
  18.1 0.0 collective-permute-done.3.far_got
  18.1 0.0 collective-permute-done.4.near_got
  18.1 0.8 %edge_side.1 = f32[33,2,1024]{2,1,0:T(2,128)} custom-call(f32[72,128]{1,0:T(8,128)S(1)} %collective-permute-done.3.far_got, f32[72,128]{1,0:T(8,128)S(1)} %collective-permute-done.4.near_got, f32[72,128]{1,0:T(8,128)S(1)} %get-tuple-element.51.first_ref, f32[72,128]{1,0:T(8,128)S(1)} %get-tuple-element.52.final_ref, ...), custom_call_target="tpu_custom_call" | custom-call | tf_op jit(solution)/shard_map/edge_side/pallas_call | solution.py:670
  (2 shorter events, 0.0 us)
Async XLA Ops:
  1.5 2.6 %collective-permute-start = (bf16[4,2,8,128]{3,2,1,0:T(8,128)(2,1)S(1)}, bf16[4,2,8,128]{3,2,1,0:T(8,128)(2,1)S(1)}, u32[]{:S(2)}, u32[]{:S(2)}) collective-permute-start(bf16[4,2,8,128]{3,2,1,0:T(8,128)(2,1)S(1)} %get-tuple-element.41), channel_id=1, source_target_pairs={{0,16},{16,0},{32,48},{48,32},{64,80},{80,64},{96,112},{112,96},{1... | collective-permute-start | bytes 49160 | tf_op jit(solution)/shard_map/ppermute | solution.py:689
  4.2 4.5 %collective-permute-start.1 = (bf16[2,2,8,128]{3,2,1,0:T(8,128)(2,1)S(1)}, bf16[2,2,8,128]{3,2,1,0:T(8,128)(2,1)S(1)}, u32[]{:S(2)}, u32[]{:S(2)}) collective-permute-start(bf16[2,2,8,128]{3,2,1,0:T(8,128)(2,1)S(1)} %get-tuple-element.46), channel_id=1, source_target_pairs={{0,32},{16,48},{32,0},{48,16},{64,96},{80,112},{96,64},{112,80},{1... | collective-permute-start | bytes 24584 | tf_op jit(solution)/shard_map/ppermute | solution.py:689
  8.7 4.0 %collective-permute-start.2 = (bf16[1,2,8,128]{3,2,1,0:T(8,128)(2,1)S(1)}, bf16[1,2,8,128]{3,2,1,0:T(8,128)(2,1)S(1)}, u32[]{:S(2)}, u32[]{:S(2)}) collective-permute-start(bf16[1,2,8,128]{3,2,1,0:T(8,128)(2,1)S(1)} %get-tuple-element.48), channel_id=1, source_target_pairs={{0,96},{16,112},{32,64},{48,80},{64,32},{80,48},{96,0},{112,16},{1... | collective-permute-start | bytes 12296 | tf_op jit(solution)/shard_map/ppermute | solution.py:689
  13.0 5.1 %collective-permute-start.3 = (f32[72,128]{1,0:T(8,128)S(1)}, f32[72,128]{1,0:T(8,128)S(1)}, u32[]{:S(2)}, u32[]{:S(2)}) collective-permute-start(f32[72,128]{1,0:T(8,128)S(1)} %get-tuple-element.49), channel_id=1, source_target_pairs={{0,112},{16,32},{32,16},{48,64},{64,48},{80,96},{96,80},{112,0},{1... | collective-permute-start | bytes 110600 | tf_op jit(solution)/shard_map/ppermute | solution.py:695
  14.0 4.1 %collective-permute-start.4 = (f32[72,128]{1,0:T(8,128)S(1)}, f32[72,128]{1,0:T(8,128)S(1)}, u32[]{:S(2)}, u32[]{:S(2)}) collective-permute-start(f32[72,128]{1,0:T(8,128)S(1)} %get-tuple-element.50), channel_id=1, source_target_pairs={{0,16},{16,0},{32,48},{48,32},{64,80},{80,64},{96,112},{112,96},{1... | collective-permute-start | bytes 110600 | tf_op jit(solution)/shard_map/ppermute | solution.py:689

commit v10 on v8

--- a/solution.py
+++ b/solution.py
@@ -297,22 +297,21 @@
     return e_dir, gamma_two, even + odd, even - odd, gamma_two * lost, transmit
 
 
-def mix_all(gas_ref, lanes, wide_ref):
-    products = []
-    for step in range(LEV // STEP):
-        gas = gas_ref[:, step * STEP : (step + 1) * STEP, lanes].reshape(F * STEP, CB)
-        products.append(
-            jnp.dot(
-                wide_ref[...],
-                jnp.concatenate([gas, gas], axis=0),
-                preferred_element_type=F32,
-            )
-        )
-    return products
-
-
-def eliminate(block, gas_ref, wide_ref, column_ref, solar_ref, coef_ref, esum_ref, state_ref):
-    products = mix_all(gas_ref, slice(block * CB, (block + 1) * CB), wide_ref)
+def mix_step(gas_ref, block, step, wide_ref):
+    lanes = slice(block * CB, (block + 1) * CB)
+    gas = gas_ref[:, step * STEP : (step + 1) * STEP, lanes].reshape(F * STEP, CB)
+    return jnp.dot(
+        wide_ref[...], jnp.concatenate([gas, gas], axis=0), preferred_element_type=F32
+    )
+
+
+def eliminate(
+    block, gas_ref, wide_ref, column_ref, solar_ref, coef_ref, esum_ref, state_ref, first_mix=None
+):
+    products = [
+        mix_step(gas_ref, block, step, wide_ref) if step or first_mix is None else first_mix
+        for step in range(LEV // STEP)
+    ]
     slant_rate, falling, scale, cosine = [
         column_ref[i, block : block + 1, :] for i in range(4)
     ]
@@ -388,9 +387,12 @@
 STATE = (3, G, CB)
 
 
-def down_kernel(blocks):
-    def kernel(gas_ref, wide_ref, column_ref, solar_ref, after_ref, coef_ref, esum_ref, state_ref):
-        del after_ref
+def down_kernel(blocks, has_first, following):
+    def kernel(gas_ref, wide_ref, column_ref, solar_ref, _, *refs):
+        first_ref = None
+        if has_first:
+            first_ref, *refs = refs
+        coef_ref, esum_ref, state_ref, *next_ref = refs
         for i, block in enumerate(blocks):
             eliminate(
                 block,
@@ -401,24 +403,28 @@
                 coef_ref.at[i],
                 esum_ref.at[i],
                 state_ref.at[i],
+                None if i else first_ref,
             )
+        if following is not None:
+            next_ref[0][...] = mix_step(gas_ref, following, 0, wide_ref)
 
     return kernel
 
 
-def down(blocks, gas, wide, column, solar, after):
+def down(blocks, first, following, gas, wide, column, solar, after):
     count = len(blocks)
+    mixes = [] if following is None else [shape((2 * G * STEP, CB))]
     return pl.pallas_call(
-        down_kernel(blocks),
-        in_specs=[IN_VMEM] * 4 + [UNREAD],
-        out_specs=[IN_VMEM] * 3,
-        out_shape=[shape((count,) + x) for x in (COEF, ESUM, STATE)],
+        down_kernel(blocks, bool(first), following),
+        in_specs=[IN_VMEM] * 4 + [UNREAD] + [IN_VMEM] * len(first),
+        out_specs=[IN_VMEM] * (3 + len(mixes)),
+        out_shape=[shape((count,) + x) for x in (COEF, ESUM, STATE)] + mixes,
         compiler_params=params(24),
         cost_estimate=pl.CostEstimate(
             flops=200000000 * count, transcendentals=0, bytes_accessed=4000000
         ),
         name="down",
-    )(gas, wide, column, solar, after)
+    )(gas, wide, column, solar, after, *first)
 
 
 def ground(albedo_ref, column_ref, block):
@@ -725,10 +731,16 @@
         side_weight,
         gas_state,
     )
-    parts = []
+    parts, first_mix = [], []
     for i, blocks in enumerate(WINDOWS):
         got = exchange(send, PARTNERS[i])
-        parts.append(down(blocks, gas, wide, column, solar, keep))
+        following = WINDOWS[i + 1][0] if i < 2 else None
+        *part, first_mix = (
+            *down(blocks, first_mix, following, gas, wide, column, solar, keep),
+            None,
+        )[:4]
+        first_mix = [first_mix]
+        parts.append(part)
         if i < 2:
             send, keep = merge(keep, got, parts[-1][2])
     first, final, near, far, albedo = up(parts, keep, got, column)

time: 18.9 us -> 18.8 us (level)
    pallas_call x3, Pallas kernels: 6.19 us -> 5.94 us  [down(): pl.pallas_call(down_kernel(blocks, bool(first), following), in_specs=[IN_...]
  transfers between devices with their start and end apart: 5 -> 5, of which waited for: 1 -> 1; matrix products, arithmetic and copies ran while one was open for 0% -> 0% of each run, Pallas kernels for 49% -> 48%
where the time goes in v10:
time: 18.8 us; the launch traced here: 18.6 us
  Pallas kernels  11.7 us (62%)
  starting transfers between devices  6.26 us (33%)
  waiting for transfers between devices  0.59 us (3%)
    ppermute x4, starting transfers between devices, exchange(): return lax.ppermute(x, 'blk', [(i, i ^ mask) for i in range(count)])  6.26 us
    pallas_call x3, Pallas kernels, down(): pl.pallas_call(down_kernel(blocks, bool(first), following), in_specs=[IN_...  5.94 us
    pallas_call x1, Pallas kernels, inner(): pl.pallas_call(inner_kernel, in_specs=[IN_VMEM] * 15, out_specs=[IN_VMEM]...  3.06 us
    pallas_call x1, Pallas kernels, surface(): pl.pallas_call(surface_kernel, in_specs=[IN_HBM] * 10, out_specs=[IN_VMEM...  1.53 us
    pallas_call x1, Pallas kernels, edge_side(): pl.pallas_call(edge_side_kernel, in_specs=[IN_VMEM] * 8, out_specs=IN_HBM...  0.81 us
    ppermute x1, waiting for transfers between devices, beyond(): return lax.ppermute(x, ('blk', 'grp'), pairs)  0.58 us
  transfers between devices with their start and end apart: 5, of which 1 were waited for; matrix products, arithmetic and copies ran while one was open for 0% of the time, Pallas kernels for 48%

profile of v10, /device:TPU:1, one launch (start us, length us, event | category | flops | bytes accessed | tf_op | source)
XLA Modules:
  0.0 18.6 jit_solution(1925936058634587867)
XLA Ops:
  0.0 1.5 %surface.1 = (bf16[4,2,8,128]{3,2,1,0:T(8,128)(2,1)S(1)}, bf16[4,2,8,128]{3,2,1,0:T(8,128)(2,1)S(1)}, bf16[16,32,1024]{2,1,0:T(8,128)(2,1)S(1)}, bf16[512,256]{1...) custom-call(s32[32,128]{1,0:T(8,128)} %bitcast.11, ...), custom_call_target="tpu_custom_call" | custom-call | tf_op jit(solution)/shard_map/surface/pallas_call | solution.py:218
  1.5 1.5 %collective-permute-start = (bf16[4,2,8,128]{3,2,1,0:T(8,128)(2,1)S(1)}, bf16[4,2,8,128]{3,2,1,0:T(8,128)(2,1)S(1)}, u32[]{:S(2)}, u32[]{:S(2)}) collective-permute-start(bf16[4,2,8,128]{3,2,1,0:T(8,128)(2,1)S(1)} %get-tuple-element.43), channel_id=1, source_target_pairs={{0,16},{16,0},{32,48},{48,32},{64,80},{80,64},{96,112},{112,96},{1... | collective-permute-start | bytes 49160 | tf_op jit(solution)/shard_map/ppermute | solution.py:695
  3.0 1.1 %down.3 = (f32[1,32,3,32,128]{4,3,2,1,0:T(8,128)S(1)}, f32[1,33,8,128]{3,2,1,0:T(8,128)S(1)}, f32[1,3,32,128]{3,2,1,0:T(8,128)S(1)}, f32[512,128]{1,0:T(8,128)S(1)}) custom-call(bf16[16,32,1024]{2,1,0:T(8,128)(2,1)S(1)} %get-tuple-element.35.gas_ref, bf16[512,256]{1,0:T(8,128)(2,1)S(1)} %get-tuple-element.36.wide_ref, ...), custom_call_target="tpu_custom_call" | custom-call | flops 200000000 | bytes 4000000 | tf_op jit(solution)/shard_map/down/pallas_call | solution.py:417
  4.2 0.0 collective-permute-done.got_ref
  4.2 1.5 %collective-permute-start.1 = (bf16[2,2,8,128]{3,2,1,0:T(8,128)(2,1)S(1)}, bf16[2,2,8,128]{3,2,1,0:T(8,128)(2,1)S(1)}, u32[]{:S(2)}, u32[]{:S(2)}) collective-permute-start(bf16[2,2,8,128]{3,2,1,0:T(8,128)(2,1)S(1)} %get-tuple-element.49), channel_id=1, source_target_pairs={{0,32},{16,48},{32,0},{48,16},{64,96},{80,112},{96,64},{112,80},{1... | collective-permute-start | bytes 24584 | tf_op jit(solution)/shard_map/ppermute | solution.py:695
  5.6 2.8 %down.4 = (f32[3,32,3,32,128]{4,3,2,1,0:T(8,128)S(1)}, f32[3,33,8,128]{3,2,1,0:T(8,128)S(1)}, f32[3,3,32,128]{3,2,1,0:T(8,128)S(1)}, f32[512,128]{1,0:T(8,128)S(1)}) custom-call(bf16[16,32,1024]{2,1,0:T(8,128)(2,1)S(1)} %get-tuple-element.35.gas_ref, bf16[512,256]{1,0:T(8,128)(2,1)S(1)} %get-tuple-element.36.wide_ref, ...), custom_call_target="tpu_custom_call" | custom-call | flops 600000000 | bytes 4000000 | tf_op jit(solution)/shard_map/down/pallas_call | solution.py:417
  8.5 0.0 collective-permute-done.1.got_ref
  8.5 2.0 %collective-permute-start.2 = (bf16[1,2,8,128]{3,2,1,0:T(8,128)(2,1)S(1)}, bf16[1,2,8,128]{3,2,1,0:T(8,128)(2,1)S(1)}, u32[]{:S(2)}, u32[]{:S(2)}) collective-permute-start(bf16[1,2,8,128]{3,2,1,0:T(8,128)(2,1)S(1)} %get-tuple-element.51), channel_id=1, source_target_pairs={{0,96},{16,112},{32,64},{48,80},{64,32},{80,48},{96,0},{112,16},{1... | collective-permute-start | bytes 12296 | tf_op jit(solution)/shard_map/ppermute | solution.py:695
  10.5 2.0 %down.5 = (f32[2,32,3,32,128]{4,3,2,1,0:T(8,128)S(1)}, f32[2,33,8,128]{3,2,1,0:T(8,128)S(1)}, f32[2,3,32,128]{3,2,1,0:T(8,128)S(1)}) custom-call(bf16[16,32,1024]{2,1,0:T(8,128)(2,1)S(1)} %get-tuple-element.35.gas_ref, bf16[512,256]{1,0:T(8,128)(2,1)S(1)} %get-tuple-element.36.wide_ref, f32[5,8,128]{2,1,0:T(8,128)S(1)} %get-tuple-element.37.column_ref, ...), custom_call_target="tpu_custom_call" | custom-call | flops 400000000 | bytes 4000000 | tf_op jit(solution)/shard_map/down/pallas_call | solution.py:417
  12.5 0.0 collective-permute-done.2.got_ref
  12.5 0.3 %up.1 = (f32[72,128]{1,0:T(8,128)S(1)}, f32[72,128]{1,0:T(8,128)S(1)}, f32[72,128]{1,0:T(8,128)S(1)}, f32[72,128]{1,0:T(8,128)S(1)}, f32[2,8,128]{2,1,0:T(8,128)S(1)}) custom-call(f32[1,32,3,32,128]{4,3,2,1,0:T(8,128)S(1)} %get-tuple-element.40.coef_a, f32[1,33,8,128]{3,2,1,0:T(8,128)S(1)} %get-tuple-element.41.esum_a, ...), custom_call_target="tpu_custom_call" | custom-call | flops 4000000 | bytes 4000000 | tf_op jit(solution)/shard_map/up/pallas_call | solution.py:469
  12.8 1.3 %collective-permute-start.3 = (f32[72,128]{1,0:T(8,128)S(1)}, f32[72,128]{1,0:T(8,128)S(1)}, u32[]{:S(2)}, u32[]{:S(2)}) collective-permute-start(f32[72,128]{1,0:T(8,128)S(1)} %get-tuple-element.52), channel_id=1, source_target_pairs={{0,16},{16,0},{32,48},{48,32},{64,80},{80,64},{96,112},{112,96},{1... | collective-permute-start | bytes 110600 | tf_op jit(solution)/shard_map/ppermute | solution.py:695
  14.1 0.0 collective-permute-start.4
  14.1 3.1 %inner.1 = (f32[33,2,1024]{2,1,0:T(2,128)S(1)}, f32[2,72,128]{2,1,0:T(8,128)S(1)}) custom-call(bf16[16,32,1024]{2,1,0:T(8,128)(2,1)S(1)} %get-tuple-element.35.gas_ref, bf16[512,256]{1,0:T(8,128)(2,1)S(1)} %get-tuple-element.36.wide_ref, f32[5,8,128]{2,1,0:T(8,128)S(1)} %get-tuple-element.37.column_ref, f32[32,128]{1,0:T(8,128)S(1)} %get-tuple-element.38.solar_ref, ...), custom_call_target="tpu_custom_call" | custom-call | flops 2000000000 | bytes 4000000 | tf_op jit(solution)/shard_map/inner/pallas_call | solution.py:600
  17.2 0.0 collective-permute-done.3.near_got
  17.2 0.6 %collective-permute-done.4.far_got = f32[72,128]{1,0:T(8,128)S(1)} collective-permute-done((f32[72,128]{1,0:T(8,128)S(1)}, f32[72,128]{1,0:T(8,128)S(1)}, u32[]{:S(2)}, u32[]{:S(2)}) %collective-permute-start.4) | collective-permute-done | bytes 36896 | tf_op jit(solution)/shard_map/ppermute | solution.py:707
  17.8 0.8 %edge_side.1 = f32[33,2,1024]{2,1,0:T(2,128)} custom-call(f32[72,128]{1,0:T(8,128)S(1)} %collective-permute-done.3.near_got, f32[72,128]{1,0:T(8,128)S(1)} %collective-permute-done.4.far_got, f32[72,128]{1,0:T(8,128)S(1)} %get-tuple-element.54.first_ref, f32[72,128]{1,0:T(8,128)S(1)} %get-tuple-element.55.final_ref, ...), custom_call_target="tpu_custom_call" | custom-call | tf_op jit(solution)/shard_map/edge_side/pallas_call | solution.py:676
  (2 shorter events, 0.0 us)
Async XLA Ops:
  1.5 2.6 %collective-permute-start = (bf16[4,2,8,128]{3,2,1,0:T(8,128)(2,1)S(1)}, bf16[4,2,8,128]{3,2,1,0:T(8,128)(2,1)S(1)}, u32[]{:S(2)}, u32[]{:S(2)}) collective-permute-start(bf16[4,2,8,128]{3,2,1,0:T(8,128)(2,1)S(1)} %get-tuple-element.43), channel_id=1, source_target_pairs={{0,16},{16,0},{32,48},{48,32},{64,80},{80,64},{96,112},{112,96},{1... | collective-permute-start | bytes 49160 | tf_op jit(solution)/shard_map/ppermute | solution.py:695
  4.2 4.3 %collective-permute-start.1 = (bf16[2,2,8,128]{3,2,1,0:T(8,128)(2,1)S(1)}, bf16[2,2,8,128]{3,2,1,0:T(8,128)(2,1)S(1)}, u32[]{:S(2)}, u32[]{:S(2)}) collective-permute-start(bf16[2,2,8,128]{3,2,1,0:T(8,128)(2,1)S(1)} %get-tuple-element.49), channel_id=1, source_target_pairs={{0,32},{16,48},{32,0},{48,16},{64,96},{80,112},{96,64},{112,80},{1... | collective-permute-start | bytes 24584 | tf_op jit(solution)/shard_map/ppermute | solution.py:695
  8.5 4.0 %collective-permute-start.2 = (bf16[1,2,8,128]{3,2,1,0:T(8,128)(2,1)S(1)}, bf16[1,2,8,128]{3,2,1,0:T(8,128)(2,1)S(1)}, u32[]{:S(2)}, u32[]{:S(2)}) collective-permute-start(bf16[1,2,8,128]{3,2,1,0:T(8,128)(2,1)S(1)} %get-tuple-element.51), channel_id=1, source_target_pairs={{0,96},{16,112},{32,64},{48,80},{64,32},{80,48},{96,0},{112,16},{1... | collective-permute-start | bytes 12296 | tf_op jit(solution)/shard_map/ppermute | solution.py:695
  12.8 4.4 %collective-permute-start.3 = (f32[72,128]{1,0:T(8,128)S(1)}, f32[72,128]{1,0:T(8,128)S(1)}, u32[]{:S(2)}, u32[]{:S(2)}) collective-permute-start(f32[72,128]{1,0:T(8,128)S(1)} %get-tuple-element.52), channel_id=1, source_target_pairs={{0,16},{16,0},{32,48},{48,32},{64,80},{80,64},{96,112},{112,96},{1... | collective-permute-start | bytes 110600 | tf_op jit(solution)/shard_map/ppermute | solution.py:695
  14.1 3.7 %collective-permute-start.4 = (f32[72,128]{1,0:T(8,128)S(1)}, f32[72,128]{1,0:T(8,128)S(1)}, u32[]{:S(2)}, u32[]{:S(2)}) collective-permute-start(f32[72,128]{1,0:T(8,128)S(1)} %get-tuple-element.53), channel_id=1, source_target_pairs={{0,4},{1,5},{2,6},{3,7},{4,0},{5,1},{6,2},{7,3},{8,12},{9,13},{10,... | collective-permute-start | bytes 110600 | tf_op jit(solution)/shard_map/ppermute | solution.py:707

commit v11 on v10

--- a/solution.py
+++ b/solution.py
@@ -89,7 +89,8 @@
     here = area > 0.0
     safe = jnp.where(here, area, 1.0)
     owner = (parent_ref[:, 0:1] >> 7) ^ (mine * NB)
-    owner = owner ^ ((owner >> 1) & (2 * NB))
+    side, across = owner & (2 * NB), owner & (4 * NB)
+    owner = (owner & (2 * NB - 1)) + (across >> 1) + ((side << 1) ^ across)
     slot = lax.broadcasted_iota(jnp.int32, (FINE_BLOCKS, NBLK * NB), 1)
     where_to = jnp.where(owner == slot, 1.0, 0.0).astype(BF16)
     placed = []
@@ -134,7 +135,7 @@
     column_ref[4] = lit * rising
 
 
-WINDOWS = ((0,), (NB - 1, 1, 2), (3, 4))
+WINDOWS = ((0,), (NB - 1, 1), (2, 3, 4))
 LATE = (5, 6)
 
 
@@ -687,7 +688,7 @@
     )(near_got, far_got, first, final, partial, neighbours, side_weight, full)
 
 
-PARTNERS = (1, 2, 6)
+PARTNERS = (1, 6, 2)
 
 
 def exchange(x, mask):

time: 18.8 us -> 18.6 us (0.989)
  waiting for transfers between devices: 0.59 us -> 0.01 us
  starting transfers between devices: 6.26 us -> 6.6 us
    ppermute x1, starting transfers between devices: 0.01 us -> 1.11 us  [beyond(): return lax.ppermute(x, ('blk', 'grp'), pairs)]
    ppermute x4, starting transfers between devices: 6.26 us -> 5.5 us  [exchange(): return lax.ppermute(x, 'blk', [(i, i ^ mask) for i in range(count)])]
    ppermute x1, waiting for transfers between devices: 0.58 us -> 0.01 us  [beyond(): return lax.ppermute(x, ('blk', 'grp'), pairs)]
  transfers between devices with their start and end apart: 5 -> 5, of which waited for: 1 -> 0; matrix products, arithmetic and copies ran while one was open for 0% -> 0% of each run, Pallas kernels for 48% -> 49%
where the time goes in v11:
time: 18.6 us; the launch traced here: 18.5 us
  Pallas kernels  11.7 us (63%)
  starting transfers between devices  6.6 us (35%)
    pallas_call x3, Pallas kernels, down(): pl.pallas_call(down_kernel(blocks, bool(first), following), in_specs=[IN_...  6 us
    ppermute x4, starting transfers between devices, exchange(): return lax.ppermute(x, 'blk', [(i, i ^ mask) for i in range(count)])  5.5 us
    pallas_call x1, Pallas kernels, inner(): pl.pallas_call(inner_kernel, in_specs=[IN_VMEM] * 15, out_specs=[IN_VMEM]...  3.08 us
    pallas_call x1, Pallas kernels, surface(): pl.pallas_call(surface_kernel, in_specs=[IN_HBM] * 10, out_specs=[IN_VMEM...  1.53 us
    ppermute x1, starting transfers between devices, beyond(): return lax.ppermute(x, ('blk', 'grp'), pairs)  1.11 us
    pallas_call x1, Pallas kernels, edge_side(): pl.pallas_call(edge_side_kernel, in_specs=[IN_VMEM] * 8, out_specs=IN_HBM...  0.82 us
  transfers between devices with their start and end apart: 5, of which 0 were waited for; matrix products, arithmetic and copies ran while one was open for 0% of the time, Pallas kernels for 49%

profile of v11, /device:TPU:1, one launch (start us, length us, event | category | flops | bytes accessed | tf_op | source)
XLA Modules:
  0.0 18.5 jit_solution(11138094508310406609)
XLA Ops:
  0.0 1.5 %surface.1 = (bf16[4,2,8,128]{3,2,1,0:T(8,128)(2,1)S(1)}, bf16[4,2,8,128]{3,2,1,0:T(8,128)(2,1)S(1)}, bf16[16,32,1024]{2,1,0:T(8,128)(2,1)S(1)}, bf16[512,256]{1...) custom-call(s32[32,128]{1,0:T(8,128)} %bitcast.11, ...), custom_call_target="tpu_custom_call" | custom-call | tf_op jit(solution)/shard_map/surface/pallas_call | solution.py:219
  1.5 1.5 %collective-permute-start = (bf16[4,2,8,128]{3,2,1,0:T(8,128)(2,1)S(1)}, bf16[4,2,8,128]{3,2,1,0:T(8,128)(2,1)S(1)}, u32[]{:S(2)}, u32[]{:S(2)}) collective-permute-start(bf16[4,2,8,128]{3,2,1,0:T(8,128)(2,1)S(1)} %get-tuple-element.43), channel_id=1, source_target_pairs={{0,16},{16,0},{32,48},{48,32},{64,80},{80,64},{96,112},{112,96},{1... | collective-permute-start | bytes 49160 | tf_op jit(solution)/shard_map/ppermute | solution.py:696
  3.0 1.1 %down.3 = (f32[1,32,3,32,128]{4,3,2,1,0:T(8,128)S(1)}, f32[1,33,8,128]{3,2,1,0:T(8,128)S(1)}, f32[1,3,32,128]{3,2,1,0:T(8,128)S(1)}, f32[512,128]{1,0:T(8,128)S(1)}) custom-call(bf16[16,32,1024]{2,1,0:T(8,128)(2,1)S(1)} %get-tuple-element.35.gas_ref, bf16[512,256]{1,0:T(8,128)(2,1)S(1)} %get-tuple-element.36.wide_ref, ...), custom_call_target="tpu_custom_call" | custom-call | flops 200000000 | bytes 4000000 | tf_op jit(solution)/shard_map/down/pallas_call | solution.py:418
  4.2 0.0 collective-permute-done.got_ref
  4.2 2.9 %collective-permute-start.1 = (bf16[2,2,8,128]{3,2,1,0:T(8,128)(2,1)S(1)}, bf16[2,2,8,128]{3,2,1,0:T(8,128)(2,1)S(1)}, u32[]{:S(2)}, u32[]{:S(2)}) collective-permute-start(bf16[2,2,8,128]{3,2,1,0:T(8,128)(2,1)S(1)} %get-tuple-element.49), channel_id=1, source_target_pairs={{0,96},{16,112},{32,64},{48,80},{64,32},{80,48},{96,0},{112,16},{1... | collective-permute-start | bytes 24584 | tf_op jit(solution)/shard_map/ppermute | solution.py:696
  7.1 1.9 %down.4 = (f32[2,32,3,32,128]{4,3,2,1,0:T(8,128)S(1)}, f32[2,33,8,128]{3,2,1,0:T(8,128)S(1)}, f32[2,3,32,128]{3,2,1,0:T(8,128)S(1)}, f32[512,128]{1,0:T(8,128)S(1)}) custom-call(bf16[16,32,1024]{2,1,0:T(8,128)(2,1)S(1)} %get-tuple-element.35.gas_ref, bf16[512,256]{1,0:T(8,128)(2,1)S(1)} %get-tuple-element.36.wide_ref, ...), custom_call_target="tpu_custom_call" | custom-call | flops 400000000 | bytes 4000000 | tf_op jit(solution)/shard_map/down/pallas_call | solution.py:418
  9.0 0.0 collective-permute-done.1.got_ref
  9.0 0.1 collective-permute-start.2
  9.1 3.0 %down.5 = (f32[3,32,3,32,128]{4,3,2,1,0:T(8,128)S(1)}, f32[3,33,8,128]{3,2,1,0:T(8,128)S(1)}, f32[3,3,32,128]{3,2,1,0:T(8,128)S(1)}) custom-call(bf16[16,32,1024]{2,1,0:T(8,128)(2,1)S(1)} %get-tuple-element.35.gas_ref, bf16[512,256]{1,0:T(8,128)(2,1)S(1)} %get-tuple-element.36.wide_ref, f32[5,8,128]{2,1,0:T(8,128)S(1)} %get-tuple-element.37.column_ref, ...), custom_call_target="tpu_custom_call" | custom-call | flops 600000000 | bytes 4000000 | tf_op jit(solution)/shard_map/down/pallas_call | solution.py:418
  12.1 0.0 collective-permute-done.2.got_ref
  12.1 0.3 %up.1 = (f32[72,128]{1,0:T(8,128)S(1)}, f32[72,128]{1,0:T(8,128)S(1)}, f32[72,128]{1,0:T(8,128)S(1)}, f32[72,128]{1,0:T(8,128)S(1)}, f32[2,8,128]{2,1,0:T(8,128)S(1)}) custom-call(f32[1,32,3,32,128]{4,3,2,1,0:T(8,128)S(1)} %get-tuple-element.40.coef_a, f32[1,33,8,128]{3,2,1,0:T(8,128)S(1)} %get-tuple-element.41.esum_a, ...), custom_call_target="tpu_custom_call" | custom-call | flops 4000000 | bytes 4000000 | tf_op jit(solution)/shard_map/up/pallas_call | solution.py:470
  12.4 1.0 %collective-permute-start.3 = (f32[72,128]{1,0:T(8,128)S(1)}, f32[72,128]{1,0:T(8,128)S(1)}, u32[]{:S(2)}, u32[]{:S(2)}) collective-permute-start(f32[72,128]{1,0:T(8,128)S(1)} %get-tuple-element.52), channel_id=1, source_target_pairs={{0,16},{16,0},{32,48},{48,32},{64,80},{80,64},{96,112},{112,96},{1... | collective-permute-start | bytes 110600 | tf_op jit(solution)/shard_map/ppermute | solution.py:696
  13.4 1.1 %collective-permute-start.4 = (f32[72,128]{1,0:T(8,128)S(1)}, f32[72,128]{1,0:T(8,128)S(1)}, u32[]{:S(2)}, u32[]{:S(2)}) collective-permute-start(f32[72,128]{1,0:T(8,128)S(1)} %get-tuple-element.53), channel_id=1, source_target_pairs={{0,4},{1,5},{2,6},{3,7},{4,0},{5,1},{6,2},{7,3},{8,12},{9,13},{10,... | collective-permute-start | bytes 110600 | tf_op jit(solution)/shard_map/ppermute | solution.py:708
  14.5 3.1 %inner.1 = (f32[33,2,1024]{2,1,0:T(2,128)S(1)}, f32[2,72,128]{2,1,0:T(8,128)S(1)}) custom-call(bf16[16,32,1024]{2,1,0:T(8,128)(2,1)S(1)} %get-tuple-element.35.gas_ref, bf16[512,256]{1,0:T(8,128)(2,1)S(1)} %get-tuple-element.36.wide_ref, f32[5,8,128]{2,1,0:T(8,128)S(1)} %get-tuple-element.37.column_ref, f32[32,128]{1,0:T(8,128)S(1)} %get-tuple-element.38.solar_ref, ...), custom_call_target="tpu_custom_call" | custom-call | flops 2000000000 | bytes 4000000 | tf_op jit(solution)/shard_map/inner/pallas_call | solution.py:601
  17.6 0.0 collective-permute-done.3.near_got
  17.6 0.0 collective-permute-done.4.far_got
  17.6 0.8 %edge_side.1 = f32[33,2,1024]{2,1,0:T(2,128)} custom-call(f32[72,128]{1,0:T(8,128)S(1)} %collective-permute-done.3.near_got, f32[72,128]{1,0:T(8,128)S(1)} %collective-permute-done.4.far_got, f32[72,128]{1,0:T(8,128)S(1)} %get-tuple-element.54.first_ref, f32[72,128]{1,0:T(8,128)S(1)} %get-tuple-element.55.final_ref, ...), custom_call_target="tpu_custom_call" | custom-call | tf_op jit(solution)/shard_map/edge_side/pallas_call | solution.py:677
  (2 shorter events, 0.0 us)
Async XLA Ops:
  1.5 2.6 %collective-permute-start = (bf16[4,2,8,128]{3,2,1,0:T(8,128)(2,1)S(1)}, bf16[4,2,8,128]{3,2,1,0:T(8,128)(2,1)S(1)}, u32[]{:S(2)}, u32[]{:S(2)}) collective-permute-start(bf16[4,2,8,128]{3,2,1,0:T(8,128)(2,1)S(1)} %get-tuple-element.43), channel_id=1, source_target_pairs={{0,16},{16,0},{32,48},{48,32},{64,80},{80,64},{96,112},{112,96},{1... | collective-permute-start | bytes 49160 | tf_op jit(solution)/shard_map/ppermute | solution.py:696
  4.2 4.8 %collective-permute-start.1 = (bf16[2,2,8,128]{3,2,1,0:T(8,128)(2,1)S(1)}, bf16[2,2,8,128]{3,2,1,0:T(8,128)(2,1)S(1)}, u32[]{:S(2)}, u32[]{:S(2)}) collective-permute-start(bf16[2,2,8,128]{3,2,1,0:T(8,128)(2,1)S(1)} %get-tuple-element.49), channel_id=1, source_target_pairs={{0,96},{16,112},{32,64},{48,80},{64,32},{80,48},{96,0},{112,16},{1... | collective-permute-start | bytes 24584 | tf_op jit(solution)/shard_map/ppermute | solution.py:696
  9.0 3.1 %collective-permute-start.2 = (bf16[1,2,8,128]{3,2,1,0:T(8,128)(2,1)S(1)}, bf16[1,2,8,128]{3,2,1,0:T(8,128)(2,1)S(1)}, u32[]{:S(2)}, u32[]{:S(2)}) collective-permute-start(bf16[1,2,8,128]{3,2,1,0:T(8,128)(2,1)S(1)} %get-tuple-element.51), channel_id=1, source_target_pairs={{0,32},{16,48},{32,0},{48,16},{64,96},{80,112},{96,64},{112,80},{1... | collective-permute-start | bytes 12296 | tf_op jit(solution)/shard_map/ppermute | solution.py:696
  12.4 5.2 %collective-permute-start.3 = (f32[72,128]{1,0:T(8,128)S(1)}, f32[72,128]{1,0:T(8,128)S(1)}, u32[]{:S(2)}, u32[]{:S(2)}) collective-permute-start(f32[72,128]{1,0:T(8,128)S(1)} %get-tuple-element.52), channel_id=1, source_target_pairs={{0,16},{16,0},{32,48},{48,32},{64,80},{80,64},{96,112},{112,96},{1... | collective-permute-start | bytes 110600 | tf_op jit(solution)/shard_map/ppermute | solution.py:696
  13.4 4.2 %collective-permute-start.4 = (f32[72,128]{1,0:T(8,128)S(1)}, f32[72,128]{1,0:T(8,128)S(1)}, u32[]{:S(2)}, u32[]{:S(2)}) collective-permute-start(f32[72,128]{1,0:T(8,128)S(1)} %get-tuple-element.53), channel_id=1, source_target_pairs={{0,4},{1,5},{2,6},{3,7},{4,0},{5,1},{6,2},{7,3},{8,12},{9,13},{10,... | collective-permute-start | bytes 110600 | tf_op jit(solution)/shard_map/ppermute | solution.py:708
